TPU v7x, 512 devices: a whole 4x8x8 slice. The times are simulated.
512 devices in a mesh: seq: 128 (over y, z, core), rep: 4 (over x).
Axes of the slice: x: 4, y: 8, z: 8, core: 2. Of those that a mesh axis runs over, the one named last changes fastest.
Arguments:
- points: bfloat16 [65536, 512], P(('rep', 'seq')), parts along dimension 0, may hold values from -6 to 6
- decay_one: float32 [8, 65536], P(None, ('rep', 'seq')), parts along dimension 1, may hold values from -1 to 0
- decay_two: float32 [8, 131072], P(None, ('rep', 'seq')), parts along dimension 1, may hold values from -1 to 0
- block_target: int32 [8192], P('rep'), parts along dimension 0, may hold values from 0 to 4095, as said below
- w_qkv_one: bfloat16 [512, 1536], replicated, may hold values from -0.25 to 0.25
- w_out_one: bfloat16 [512, 512], replicated, may hold values from -0.25 to 0.25
- w_up: bfloat16 [512, 2048], P(None, 'seq'), may hold values from -0.25 to 0.25
- w_down: bfloat16 [2048, 512], P('seq'), may hold values from -0.125 to 0.125
- w_qkv_two: bfloat16 [512, 1536], replicated, may hold values from -0.25 to 0.25
- w_out_two: bfloat16 [512, 512], replicated, may hold values from -0.25 to 0.25
Outputs:
- mixed: bfloat16 [131072, 512], P(('rep', 'seq')), parts along dimension 0
There are 4 independent parts, one for each index of `rep`. A program takes and returns all parts, laid end to end along the dimension named above; an argument that names none is the same for every part. Nothing has to cross between parts.
Inputs may be any that keep to these rules, and one draw needn't show every extreme that they name: `block_target`: entry b is the slot of block b of points; slot g is position g % 32 on device g // 32 of seq, and slots in increasing order give the second sequence. Entries are distinct, every device uses its first slots only, and some device uses all 32. Taken in slot order the blocks go column by column: for one local index j, the j-th block of every device in increasing device order, the columns in some order. At most 1 block of one device go to one device, and some device sends that many to one device.
All inputs are finite; a program needn't handle non-finite values.
Results may differ from a plain program's by a relative error of at most 0.018.
Values may be sent and summed in bfloat16 or wider, within the bound.
No kernel may reach another device: no remote copies, remote signals or barrier semaphores. Data moves between devices by JAX's collectives and lax.ppermute only.
A program may use at most 128 MiB of HBM per device.

v0:
```python
import jax
import jax.numpy as jnp
from jax import lax
from jax.sharding import Mesh
from jax.sharding import PartitionSpec as P

D = 512
MIXER_STREAMS = 8
HEAD_DIM = 64
BR = 8
CAP = 32
SEQ = ("seq_0", "seq_1", "seq_2")
REP_SEQ = ("rep", "seq_0", "seq_1", "seq_2")


epsilon = 1e-05
highest = lax.Precision.HIGHEST


def nothing_yet(value, identity):
    return jax.tree.map(
        lambda a, e: jnp.broadcast_to(jnp.asarray(e, a.dtype), a.shape), value, identity
    )


def entering_2(value, axes, combine, identity):
    before = start = nothing_yet(value, identity)
    running = value
    for axis in reversed(axes):
        devices, position = (lax.axis_size(axis), lax.axis_index(axis))
        pieces = jax.tree.map(
            lambda part, kind: lax.all_gather(part.astype(kind), axis),
            running,
            jax.tree.map(lambda a: jnp.bfloat16 if a.dtype == jnp.float32 else a.dtype, value),
        )
        inside, running = (start, start)
        for k in range(devices):
            passed = k < position
            running = combine(
                running, jax.tree.map(lambda part, own: part[k].astype(own.dtype), pieces, value)
            )
            inside = jax.tree.map(lambda new, old: jnp.where(passed, new, old), running, inside)
        before = combine(inside, before)
    return before


def rows_first(arrays, axis, dims):
    turned = [jnp.moveaxis(a, dim, 0) for a, dim in zip(arrays, dims)]
    both = jnp.concatenate([t.reshape(len(t), -1) for t in turned], axis=1)
    filled, at, done = (lax.all_gather(both, axis, axis=0, tiled=True), 0, [])
    for t, dim in zip(turned, dims):
        piece = filled[:, at : at + t[0].size].reshape(-1, *t.shape[1:])
        done.append(jnp.moveaxis(piece, 0, dim))
        at += t[0].size
    return tuple(done)


def rms_rows(inputs):
    wide = inputs.astype(jnp.float32)
    return wide * lax.rsqrt(jnp.mean(wide * wide, axis=-1, keepdims=True) + epsilon)


def project(inputs, weight):
    normed = rms_rows(inputs).astype(jnp.bfloat16)
    joined = jnp.dot(normed, weight, preferred_element_type=jnp.float32)
    column = lax.broadcasted_iota(jnp.int32, (1, 3 * D), 1)
    scaled = jnp.where(column < D, joined * HEAD_DIM ** (-0.5), joined)
    return scaled.astype(jnp.bfloat16)


def split_heads(matrix):
    return matrix.reshape(matrix.shape[0], MIXER_STREAMS, HEAD_DIM).transpose(1, 0, 2)


def combine(earlier, later):
    return (earlier[0] + later[0], earlier[1] * jnp.exp(later[0])[:, None, None] + later[1])


def block_summary(key_rows, values, decay):
    cumulative = jnp.cumsum(decay, axis=1)
    decay_total = cumulative[:, -1]
    weighted = key_rows.astype(jnp.float32) * jnp.exp(decay_total[:, None] - cumulative)[:, :, None]
    state_sum = jnp.einsum("hsd,hse->hde", weighted, values.astype(jnp.float32), precision=highest)
    return (cumulative, decay_total, state_sum)


def block_output(queries, key_rows, values, cumulative, entering):
    span = queries.shape[1]
    causal = (
        lax.broadcasted_iota(jnp.int32, (span, span), 0)
        >= lax.broadcasted_iota(jnp.int32, (span, span), 1)
    )[None]
    gap = cumulative[:, :, None] - cumulative[:, None, :]
    weight = jnp.where(causal, jnp.exp(jnp.where(causal, gap, 0.0)), 0.0)
    scores = jnp.einsum("htd,hsd->hts", queries, key_rows, preferred_element_type=jnp.float32)
    weighted = (scores * weight).astype(jnp.bfloat16)
    inner = jnp.einsum("hts,hse->hte", weighted, values, preferred_element_type=jnp.float32)
    carried = jnp.einsum("htd,hde->hte", queries.astype(jnp.float32), entering, precision=highest)
    summed = inner + carried * jnp.exp(cumulative)[:, :, None]
    return summed * lax.rsqrt(jnp.mean(summed * summed, axis=-1, keepdims=True) + epsilon)


def attend_local(joined, decay, chain):
    queries = split_heads(joined[:, :D])
    key_rows = split_heads(joined[:, D : 2 * D])
    values = split_heads(joined[:, 2 * D :])
    total_rows = joined.shape[0]
    device_sum = (
        jnp.zeros((MIXER_STREAMS,), jnp.float32),
        jnp.zeros((MIXER_STREAMS, HEAD_DIM, HEAD_DIM), jnp.float32),
    )
    summary = block_summary(key_rows, values, decay)
    device_sum = combine(device_sum, (summary[1], summary[2]))
    entering = chain(device_sum)[1]
    cumulative, decay_total, state_sum = summary
    result = block_output(queries, key_rows, values, cumulative, entering)
    outputs = result.astype(jnp.bfloat16)
    return outputs.transpose(1, 0, 2).reshape(total_rows, D)


def empty_state():
    return (
        jnp.zeros((MIXER_STREAMS,), jnp.float32),
        jnp.zeros((MIXER_STREAMS, HEAD_DIM, HEAD_DIM), jnp.float32),
    )


def shards(
    points,
    decay_one,
    decay_two,
    block_target,
    w_qkv_one,
    w_out_one,
    w_up,
    w_down,
    w_qkv_two,
    w_out_two,
):

    def chain_first(summary):
        return entering_2(summary, SEQ, combine, empty_state())

    def chain_second(summary):
        return entering_2(summary, SEQ, combine, empty_state())

    joined = project(points, w_qkv_one)
    attended = attend_local(joined, decay_one, chain_first)
    first = (
        points.astype(jnp.float32)
        + jnp.dot(attended, w_out_one, preferred_element_type=jnp.float32)
    ).astype(jnp.bfloat16)
    normed = rms_rows(first).astype(jnp.bfloat16)
    full_up, full_down = rows_first((w_up, w_down), SEQ, (1, 0))
    hidden = jax.nn.gelu(
        jnp.dot(normed, full_up, preferred_element_type=jnp.float32), approximate=True
    ).astype(jnp.bfloat16)
    down_sum = jnp.dot(hidden, full_down, preferred_element_type=jnp.float32)
    layer_out = (first.astype(jnp.float32) + down_sum).astype(jnp.bfloat16)
    seq_count = lax.axis_size(SEQ)
    position = lax.axis_index(SEQ)
    local_blocks = layer_out.shape[0] // BR
    per_pair = max(1, CAP // seq_count)
    destination = (block_target // CAP).reshape(seq_count, local_blocks)
    this_block = lax.broadcasted_iota(jnp.int32, (local_blocks, local_blocks), 0)
    other_block = lax.broadcasted_iota(jnp.int32, (local_blocks, local_blocks), 1)
    before = (other_block < this_block)[None]
    same_target = destination[:, :, None] == destination[:, None, :]
    rank_grid = jnp.sum(jnp.where(same_target & before, 1, 0), axis=2).astype(jnp.int32)
    my_target = lax.dynamic_index_in_dim(destination, position, 0, keepdims=False)
    my_rank = lax.dynamic_index_in_dim(rank_grid, position, 0, keepdims=False)
    send_slot = my_target * per_pair + my_rank
    outgoing_ids = lax.broadcasted_iota(jnp.int32, (seq_count * per_pair, local_blocks), 0)
    block_ids = lax.broadcasted_iota(jnp.int32, (seq_count * per_pair, local_blocks), 1)
    pick = outgoing_ids == send_slot[None, :]
    source_block = jnp.sum(jnp.where(pick, block_ids, 0), axis=1)
    occupied = jnp.any(pick, axis=1)
    slot_ids = position * CAP + lax.broadcasted_iota(jnp.int32, (1, CAP), 1)
    match = block_target[:, None] == slot_ids
    all_blocks = lax.broadcasted_iota(jnp.int32, match.shape, 0)
    arriving = jnp.sum(jnp.where(match, all_blocks, 0), axis=0)
    in_use = jnp.any(match, axis=0)
    arrival_slot = arriving // local_blocks * per_pair + rank_grid.reshape(-1)[arriving]
    width = layer_out.shape[1]
    blocks = layer_out.reshape(local_blocks, BR, width)
    chosen = jnp.where(
        occupied[:, None, None], blocks[source_block], jnp.zeros((), layer_out.dtype)
    )
    arrived = lax.all_to_all(
        chosen.reshape(seq_count * per_pair * BR, width),
        SEQ,
        split_axis=0,
        concat_axis=0,
        tiled=True,
    )
    width = arrived.shape[1]
    blocks = arrived.reshape(seq_count * per_pair, BR, width)
    chosen = jnp.where(in_use[:, None, None], blocks[arrival_slot], jnp.zeros((), arrived.dtype))
    placed = chosen.reshape(CAP * BR, width)
    joined_two = project(placed, w_qkv_two)
    decay_mask = jnp.repeat(in_use.astype(jnp.float32), BR)
    attended_two = attend_local(joined_two, decay_two * decay_mask[None, :], chain_second)
    return (
        placed.astype(jnp.float32)
        + jnp.dot(attended_two, w_out_two, preferred_element_type=jnp.float32)
    ).astype(jnp.bfloat16)


def solution(mesh):
    split = Mesh(
        mesh.devices.reshape(8, 8, 2, mesh.shape["rep"]), ("seq_0", "seq_1", "seq_2", "rep")
    )
    placed = (
        P(REP_SEQ, None),
        P(None, REP_SEQ),
        P(None, REP_SEQ),
        P("rep"),
        P(),
        P(),
        P(None, SEQ),
        P(SEQ, None),
        P(),
        P(),
    )
    return jax.shard_map(
        shards, mesh=split, in_specs=placed, out_specs=P(REP_SEQ, None), check_vma=False
    )
```

profile of v0, /device:TPU:4, one launch (start us, length us, event | category | flops | bytes accessed | tf_op | source)
XLA Modules:
  0.0 265.2 jit_solution(12614986197713168852)
XLA Ops:
  6.5 1.5 pad_maximum_fusion
  10.6 1.0 reduce_window_sum.40
  11.6 1.3 dynamic-slice
  14.4 2.4 all-reduce.2
  16.9 1.0 fusion.136
  17.9 1.9 fusion.40
  21.9 22.3 %all-gather.4 = bf16[8,1,8]{2,1,0:T(2,128)(2,1)S(1)} all-gather(bf16[1,1,8]{2,1,0:T(2,128)(2,1)S(1)} %get-tuple-element.64), channel_id=1, replica_groups=mesh['seq_0'=8,'seq_1'=8,'seq_2'=2,'rep'=4] {'seq_1'}, dimensions={0}, use_global_device_ids=true | all-gather | bytes 144 | tf_op jit(solution)/shard_map/all_gather | solution.py:32
  44.3 16.8 %all-gather.5 = bf16[8,1,8]{2,1,0:T(2,128)(2,1)S(1)} all-gather(bf16[1,1,8]{2,1,0:T(2,128)(2,1)S(1)} %get-tuple-element.13), channel_id=1, replica_groups=mesh['seq_0'=8,'seq_1'=8,'seq_2'=2,'rep'=4] {'seq_0'}, dimensions={0}, use_global_device_ids=true | all-gather | bytes 144 | tf_op jit(solution)/shard_map/all_gather | solution.py:32
  61.1 13.3 %all-gather.6 = bf16[8,1,8]{2,1,0:T(2,128)(2,1)S(1)} all-gather(bf16[1,1,8]{2,1,0:T(2,128)(2,1)S(1)} %get-tuple-element.61), channel_id=1, replica_groups=mesh['seq_0'=8,'seq_1'=8,'seq_2'=2,'rep'=4] {'seq_1'}, dimensions={0}, use_global_device_ids=true | all-gather | bytes 144 | tf_op jit(solution)/shard_map/all_gather | solution.py:32
  75.2 2.0 all-gather.1
  77.7 28.5 %all_gather.60 = bf16[8,8,64,64]{3,2,1,0:T(8,128)(2,1)S(1)} all-gather(bf16[1,8,64,64]{3,2,1,0:T(8,128)(2,1)S(1)} %fusion.130), channel_id=1, replica_groups=mesh['seq_0'=8,'seq_1'=8,'seq_2'=2,'rep'=4] {'seq_1'}, dimensions={0}, use_global_device_ids=true | all-gather | bytes 589824 | tf_op jit(solution)/shard_map/all_gather | solution.py:32
  106.5 27.1 %all_gather.61 = bf16[8,8,64,64]{3,2,1,0:T(8,128)(2,1)S(1)} all-gather(bf16[1,8,64,64]{3,2,1,0:T(8,128)(2,1)S(1)} %fusion.208), channel_id=1, replica_groups=mesh['seq_0'=8,'seq_1'=8,'seq_2'=2,'rep'=4] {'seq_0'}, dimensions={0}, use_global_device_ids=true | all-gather | bytes 589824 | tf_op jit(solution)/shard_map/all_gather | solution.py:32
  133.5 1.5 fusion.67
  136.5 3.4 %fusion.19 = bf16[16,8,512]{2,1,0:T(8,128)(2,1)S(1)} fusion(f32[128,512]{1,0:T(8,128)S(1)} %get-tuple-element.69, bf16[2048,1024]{1,0:T(8,128)(2,1)} %all-gather.10.cloned.1.call-done, f32[128]{0:T(128)S(1)} %add_rsqrt_fusion.1), kind=kOutput, calls=%fused_computation.27 | convolution fusion | flops 539492352 | bytes 4850176 | tf_op jit(solution)/shard_map/dot_general | solution.py:158
  140.5 1.2 broadcast_select_fusion
  141.7 8.0 %all-to-all-start = ((bf16[128,8,512]{2,1,0:T(8,128)(2,1)}), bf16[128,8,512]{2,1,0:T(8,128)(2,1)S(1)}, u32[]{:S(2)}, u32[]{:S(2)}) async-start(bf16[128,8,512]{2,1,0:T(8,128)(2,1)} %broadcast_select_fusion), calls=%async_computation | async-start | bytes 2097152 | tf_op jit(solution)/shard_map/all_to_all | solution.py:189
  149.7 34.5 %all-gather.7 = bf16[8,1,8]{2,1,0:T(2,128)(2,1)S(1)} all-gather(bf16[1,1,8]{2,1,0:T(2,128)(2,1)S(1)} %get-tuple-element.9), channel_id=1, replica_groups=mesh['seq_0'=8,'seq_1'=8,'seq_2'=2,'rep'=4] {'seq_0'}, dimensions={0}, use_global_device_ids=true | all-gather | bytes 144 | tf_op jit(solution)/shard_map/all_gather | solution.py:32
  189.5 2.0 all-gather.3
  191.7 27.9 %all_gather.68 = bf16[8,8,64,64]{3,2,1,0:T(8,128)(2,1)S(1)} all-gather(bf16[1,8,64,64]{3,2,1,0:T(8,128)(2,1)S(1)} %fusion.134), channel_id=1, replica_groups=mesh['seq_0'=8,'seq_1'=8,'seq_2'=2,'rep'=4] {'seq_1'}, dimensions={0}, use_global_device_ids=true | all-gather | bytes 589824 | tf_op jit(solution)/shard_map/all_gather | solution.py:32
  219.9 28.8 %all_gather.69 = bf16[8,8,64,64]{3,2,1,0:T(8,128)(2,1)} all-gather(bf16[1,8,64,64]{3,2,1,0:T(8,128)(2,1)S(1)} %fusion.209), channel_id=1, replica_groups=mesh['seq_0'=8,'seq_1'=8,'seq_2'=2,'rep'=4] {'seq_0'}, dimensions={0}, use_global_device_ids=true | all-gather | bytes 589824 | tf_op jit(solution)/shard_map/all_gather | solution.py:32
  248.7 1.8 copy.68
  250.5 3.4 %fusion.62 = f32[8,256,64]{1,2,0:T(8,128)} fusion(bf16[8,256,64]{1,2,0:T(8,128)(2,1)} %bitcast.666, bf16[8,8,64,64]{3,2,1,0:T(8,128)(2,1)} %all_gather.69, f32[8]{0:T(128)S(1)} %get-tuple-element.60, f32[8]{0:T(128)S(1)} %get-tuple-element.62, f32[8]{0:T(128)} %exponential_bitcast_fusion.4, f32[8]{0:T(128)S(1)} %get-tuple-element.35, ...), kind=kOutput, calls=%fused_computation.111 | convolution fusion | flops 103055360 | bytes 1966738 | tf_op jit(solution)/shard_map/htd,hde->hte/dot_general | solution.py:98
  253.9 2.3 multiply_reduce_fusion
  256.3 2.1 fusion.6
  (101 shorter events, 14.9 us)
Async XLA Ops:
  6.5 180.2 %copy-start = (bf16[512,1536]{1,0:T(8,128)(2,1)S(1)}, bf16[512,1536]{1,0:T(8,128)(2,1)}, u32[]{:S(2)}) copy-start(bf16[512,1536]{1,0:T(8,128)(2,1)} %param.18) | copy-start | bytes 4718596
  6.5 13.7 %copy-start.5 = (s32[2048]{0:T(1024)S(1)}, s32[2048]{0:T(1024)}, u32[]{:S(2)}) copy-start(s32[2048]{0:T(1024)} %param.13) | copy-start | bytes 24580
  6.5 129.9 %all-gather.10.cloned.1.call-start = ((), (), s32[]{:S(2)}) async-start(), calls=%async_computation.1 | async-start | bytes 4227072 | tf_op jit(solution)/shard_map/all_gather | solution.py:50
  135.0 1.0 copy-start.2
  135.0 1.1 copy-start.4
  141.7 44.1 %all-to-all-start = ((bf16[128,8,512]{2,1,0:T(8,128)(2,1)}), bf16[128,8,512]{2,1,0:T(8,128)(2,1)S(1)}, u32[]{:S(2)}, u32[]{:S(2)}) async-start(bf16[128,8,512]{2,1,0:T(8,128)(2,1)} %broadcast_select_fusion), calls=%async_computation | async-start | bytes 2097152 | tf_op jit(solution)/shard_map/all_to_all | solution.py:189
  188.4 0.7 copy-start.1
  253.9 2.3 copy-start.3
Sparse Core Ops, SparseCore 0:
  10.5 90.3 all-gather.9
where the time goes:
time: 266 us; the launch traced here: 265 us
  blocking collectives  206 us (77%)
  matrix products  16.6 us (6%)
  between operations  14.4 us (5%)
  local copies, waits for them, and re-layouts  10.3 us (4%)
  other arithmetic  10.1 us (4%)
  starting transfers between devices  8.03 us (3%)
    all_gather x10, blocking collectives, entering_2(): lax.all_gather(part.astype(kind), axis)  203 us
    all_to_all x1, starting transfers between devices, shards(): lax.all_to_all(chosen.reshape(seq_count * per_pair * BR, width), SEQ, spl...  8.03 us
  transfers between devices with their start and end apart: 2, of which 0 were waited for; matrix products, arithmetic and copies ran while one was open for 6% of the time, Pallas kernels for 0%

commit v1 on v0

v1 whole, which is shorter than its diff:
```python
import jax
import jax.numpy as jnp
from jax import lax
from jax.experimental import pallas as pl
from jax.experimental.pallas import tpu as pltpu
from jax.sharding import Mesh
from jax.sharding import PartitionSpec as P

D = 512
HEADS = 8
HEAD_DIM = 64
PAIRS = HEADS // 2
BR = 8
CAP = 32
SEQ = ("seq_0", "seq_1", "seq_2")
ROW = ("seq_1", "seq_2")
REP_SEQ = ("rep", "seq_0", "seq_1", "seq_2")
EPS = 1e-05
F32 = jnp.float32
BF16 = jnp.bfloat16
DIRECT = False

NN = (((1,), (0,)), ((), ()))
NT = (((1,), (1,)), ((), ()))
TN = (((0,), (0,)), ((), ()))


def dot(a, b, dims=NN):
    return lax.dot_general(a, b, dims, preferred_element_type=F32)


def iota(shape, dim):
    return lax.broadcasted_iota(jnp.int32, shape, dim)


def ones_where(cond):
    return jnp.where(cond, 1.0, 0.0).astype(BF16)


def halves(x):
    high = x.astype(BF16)
    return high, (x - high.astype(F32)).astype(BF16)


def thirds(x):
    high, rest = x.astype(BF16), x - x.astype(BF16).astype(F32)
    middle, low = halves(rest)
    return high, middle, low


def rms_rows(wide):
    return wide * lax.rsqrt(jnp.mean(wide * wide, axis=-1, keepdims=True) + EPS)


def project(wide, weight):
    normed = rms_rows(wide).astype(BF16)
    joined = dot(normed, weight)
    return jnp.concatenate(
        [(joined[:, :D] * HEAD_DIM ** (-0.5)).astype(BF16), joined[:, D:].astype(BF16)], axis=1
    )


def running_sums(decay):
    rows = decay.shape[1]
    parts = thirds(decay)
    upto = ones_where(iota((rows, rows), 0) >= iota((rows, rows), 1))
    by_head = sum(dot(part, upto, NT) for part in parts)
    by_row = sum(dot(upto, part, NT) for part in parts)
    return by_head, by_row


def pair_lanes(columns, pair):
    rows = columns.shape[0]
    first = iota((rows, 2 * HEAD_DIM), 1) < HEAD_DIM
    return jnp.where(
        first, columns[:, 2 * pair : 2 * pair + 1], columns[:, 2 * pair + 1 : 2 * pair + 2]
    )


def pack_state(qkv, by_row):
    rows = qkv.shape[0]
    total = by_row[rows - 1 : rows]
    weight = jnp.exp(total - by_row)
    lane = iota((HEAD_DIM, 128), 1)
    place = iota((128, HEAD_DIM), 0)
    spread = ones_where((place % 4 < 2) & (iota((128, HEAD_DIM), 1) == (place // 4) * 2 + place % 4))
    kind = iota((128, 128), 0) % 4
    packed = []
    for p in range(PAIRS):
        keys = qkv[:, D + 128 * p : D + 128 * (p + 1)].astype(F32) * pair_lanes(weight, p)
        values = qkv[:, 2 * D + 128 * p : 2 * D + 128 * (p + 1)]
        high, low = halves(keys)
        both = dot(high, values, TN) + dot(low, values, TN)
        state = jnp.where(lane < HEAD_DIM, both[:HEAD_DIM], both[HEAD_DIM:]).astype(BF16)
        high, low = halves(pair_lanes(total, p))
        piece = dot(spread, state)
        piece = jnp.where(kind == 2, high.astype(F32), piece)
        piece = jnp.where(kind == 3, low.astype(F32), piece)
        packed.append(piece.astype(BF16))
    return jnp.concatenate(packed, axis=0)


def front(points, weight, decay):
    qkv = project(points[...].astype(F32), weight[...])
    by_head, by_row = running_sums(decay[...])
    return qkv, pack_state(qkv, by_row)


def prefix(received):
    rows = received[...]
    total = rows.shape[0]
    devices = total // 4
    shape = (2 * devices, total)
    target, source = iota(shape, 0) // 2, iota(shape, 1) // 4
    part = iota(shape, 1) % 4
    earlier = source < target
    between = ones_where((part >= 2) & earlier)
    mask = earlier & (part == iota(shape, 0) % 2)
    later = iota((total, total), 0) // 4 > iota((total, total), 1) // 4
    outs = []
    for half in range(2):
        decay = rows[:, half * HEAD_DIM : half * HEAD_DIM + 1].astype(F32)
        gap = dot(between, jnp.where(later, decay, 0.0).astype(BF16))
        weight = jnp.where(mask, jnp.exp(gap), 0.0)
        high, low = halves(weight)
        outs.append(dot(high, rows) + dot(low, rows))
    lane = iota(outs[0].shape, 1)
    return jnp.where(lane < HEAD_DIM, outs[0], outs[1]).astype(BF16)


def attend(qkv, by_head, by_row, entering):
    rows = qkv.shape[0]
    causal = iota((rows, rows), 0) >= iota((rows, rows), 1)
    lanes = iota((1, 128), 1)
    sides = (ones_where(lanes < HEAD_DIM), ones_where(lanes >= HEAD_DIM))
    same = ones_where(iota((128, 128), 0) // HEAD_DIM == iota((128, 128), 1) // HEAD_DIM)
    first = iota((rows, 128), 1) < HEAD_DIM
    grown = jnp.exp(by_row)
    attended = []
    for p in range(PAIRS):
        queries = qkv[:, 128 * p : 128 * (p + 1)]
        keys = qkv[:, D + 128 * p : D + 128 * (p + 1)]
        values = qkv[:, 2 * D + 128 * p : 2 * D + 128 * (p + 1)]
        state = entering[HEAD_DIM * p : HEAD_DIM * (p + 1)]
        state = jnp.concatenate([state * sides[0], state * sides[1]], axis=0)
        carried = dot(queries, state) * pair_lanes(grown, p)
        inner = []
        for side in range(2):
            h = 2 * p + side
            scores = dot(queries * sides[side], keys, NT)
            gap = by_row[:, h : h + 1] - by_head[h : h + 1, :]
            weighted = scores * jnp.exp(jnp.where(causal, gap, -1e30))
            inner.append(dot(weighted.astype(BF16), values))
        summed = jnp.where(first, inner[0], inner[1]) + carried
        high, low = halves(summed * summed)
        mean = (dot(high, same) + dot(low, same)) * (1.0 / HEAD_DIM)
        attended.append((summed * lax.rsqrt(mean + EPS)).astype(BF16))
    return jnp.concatenate(attended, axis=1)


def picked(meta, base, count, group):
    return sum(jnp.where(group == k, meta[base + k], 0) for k in range(count))


def middle(meta, points, qkv, decay, entering, w_out):
    by_head, by_row = running_sums(decay[...])
    attended = attend(qkv[...], by_head, by_row, entering[...])
    first = (points[...].astype(F32) + dot(attended, w_out[...])).astype(BF16)
    shape = (256, 128)
    place, column = iota(shape, 0), iota(shape, 1)
    begin = picked_strided(meta, 0, place // 32)
    end = picked_strided(meta, 16, place // 32)
    where = begin + ((meta[160] - begin) & 127) + 128 * ((place // BR) & 3)
    block = picked(meta, 144, 16, where >> 7)
    chosen = (where < end) & (column == block * BR + (place & 7))
    return dot(ones_where(chosen), first).astype(BF16)


def picked_strided(meta, shift, group):
    return sum(jnp.where(group == k, meta[shift + 16 * k], 0) for k in range(8))


def across(meta, arrived):
    shape = (256, 256)
    place, column = iota(shape, 0), iota(shape, 1)
    base = meta[161]
    begin = sum(jnp.where(place // 16 == k, meta[base + k], 0) for k in range(16))
    end = sum(jnp.where(place // 16 == k, meta[base + k + 1], 0) for k in range(16))
    where = begin + ((meta[162] - begin) & 15) + 16 * ((place // BR) & 1)
    held = ((where & 127) >> 4) * 4 + ((where - meta[base]) >> 7)
    chosen = (where < end) & (column == held * BR + (place & 7))
    return dot(ones_where(chosen), arrived[...]).astype(BF16)


def second(meta, arrived, weights, w_qkv, decay):
    shape = (256, 256)
    place, column = iota(shape, 0), iota(shape, 1)
    begin = meta[meta[160]]
    used = meta[meta[160] + 1] - begin
    slot = place // BR
    held = ((begin + slot) & 15) * 2 + slot // 16
    chosen = (slot < used) & (column == held * BR + (place & 7))
    first = dot(ones_where(chosen), arrived[...])
    normed = rms_rows(first).astype(BF16)
    hidden = jax.nn.gelu(dot(normed, weights[:, :D], NT), approximate=True).astype(BF16)
    placed = (first + dot(hidden, weights[:, D:])).astype(BF16)
    qkv = project(placed.astype(F32), w_qkv[...])
    kept = jnp.where(iota(decay.shape, 1) < BR * used, decay[...], 0.0)
    by_head, by_row = running_sums(kept)
    return placed, qkv, kept, pack_state(qkv, by_row)


def last(placed, qkv, decay, entering, w_out):
    by_head, by_row = running_sums(decay[...])
    attended = attend(qkv[...], by_head, by_row, entering[...])
    return (placed[...].astype(F32) + dot(attended, w_out[...])).astype(BF16)


def kernel_call(function, outs, *args, scalars=0):
    if DIRECT:
        return function(*args)
    count = len(args)

    def body(*refs):
        results = function(*refs[:count])
        if len(outs) == 1:
            results = (results,)
        for ref, value in zip(refs[count:], results):
            ref[...] = value

    smem = pl.BlockSpec(memory_space=pltpu.SMEM)
    vmem = pl.BlockSpec(memory_space=pltpu.VMEM)
    result = pl.pallas_call(
        body,
        out_shape=[jax.ShapeDtypeStruct(shape, kind) for shape, kind in outs],
        in_specs=[smem] * scalars + [vmem] * (count - scalars),
        out_specs=[vmem] * len(outs),
        name=function.__name__,
    )(*args)
    return result[0] if len(outs) == 1 else result


def whole(x, axes, pieces):
    split = x.reshape(pieces, x.shape[0] // pieces, x.shape[1])
    return lax.all_to_all(split, axes, split_axis=0, concat_axis=0, tiled=True).reshape(x.shape)


def shards(
    points,
    decay_one,
    decay_two,
    block_target,
    w_qkv_one,
    w_out_one,
    w_up,
    w_down,
    w_qkv_two,
    w_out_two,
):
    position = lax.axis_index(SEQ)
    joined = jnp.concatenate([w_up.T, w_down], axis=1)
    weights = lax.all_gather(joined, SEQ, axis=0, tiled=True)

    limits = CAP * iota((144, 1), 0)
    starts = jnp.sum((block_target[None, :] < limits).astype(jnp.int32), axis=1)
    own = block_target[:16]
    rank = jnp.sum((own[None, :] < own[:, None]).astype(jnp.int32), axis=1)
    order = jnp.sum(jnp.where(rank[None, :] == iota((16, 16), 0), iota((16, 16), 1), 0), axis=1)
    here = jnp.stack([position, position // 16 * 16, position % 16]).astype(jnp.int32)
    meta = jnp.concatenate([starts, order, here])

    qkv, sent = kernel_call(
        front, [((128, 3 * D), BF16), ((512, 128), BF16)], points, w_qkv_one, decay_one
    )
    received = whole(sent, SEQ, 128)
    summed = kernel_call(prefix, [((256, 128), BF16)], received)
    entering = whole(summed, SEQ, 128)
    outgoing = kernel_call(
        middle,
        [((256, D), BF16)],
        meta,
        points,
        qkv,
        decay_one,
        entering,
        w_out_one,
        scalars=1,
    )
    arrived = whole(outgoing, "seq_0", 8)
    outgoing = kernel_call(across, [((256, D), BF16)], meta, arrived, scalars=1)
    arrived = whole(outgoing, ROW, 16)
    placed, qkv, decay, sent = kernel_call(
        second,
        [((256, D), BF16), ((256, 3 * D), BF16), ((HEADS, 256), F32), ((512, 128), BF16)],
        meta,
        arrived,
        weights,
        w_qkv_two,
        decay_two,
        scalars=1,
    )
    received = whole(sent, SEQ, 128)
    summed = kernel_call(prefix, [((256, 128), BF16)], received)
    entering = whole(summed, SEQ, 128)
    return kernel_call(last, [((256, D), BF16)], placed, qkv, decay, entering, w_out_two)


def solution(mesh):
    split = Mesh(
        mesh.devices.reshape(8, 8, 2, mesh.shape["rep"]), ("seq_0", "seq_1", "seq_2", "rep")
    )
    placed = (
        P(REP_SEQ, None),
        P(None, REP_SEQ),
        P(None, REP_SEQ),
        P("rep"),
        P(),
        P(),
        P(None, SEQ),
        P(SEQ, None),
        P(),
        P(),
    )
    return jax.shard_map(
        shards, mesh=split, in_specs=placed, out_specs=P(REP_SEQ, None), check_vma=False
    )
```

time: 266 us -> 168 us (0.63)
  the two profiles are of different devices: /device:TPU:4 before, /device:TPU:1 now
where the time goes in v1:
time: 168 us; the launch traced here: 167 us
  blocking collectives  75.7 us (45%)
  Pallas kernels  25.5 us (15%)
  starting transfers between devices  24.5 us (15%)
  waiting for transfers between devices  23.9 us (14%)
  between operations  13.5 us (8%)
  other arithmetic  1.93 us (1%)
  local copies, waits for them, and re-layouts  1.92 us (1%)
    all_to_all x4, blocking collectives, whole(): lax.all_to_all(split, axes, split_axis=0, concat_axis=0, tiled=True)  75.7 us
    pallas_call x7, Pallas kernels, kernel_call(): pl.pallas_call(body, out_shape=[jax.ShapeDtypeStruct(shape, kind) for sha...  25.5 us
    all_to_all x2, starting transfers between devices, whole(): lax.all_to_all(split, axes, split_axis=0, concat_axis=0, tiled=True)  24.5 us
    all_to_all x2, waiting for transfers between devices, whole(): lax.all_to_all(split, axes, split_axis=0, concat_axis=0, tiled=True)  22.7 us
  transfers between devices with their start and end apart: 3, of which 3 were waited for; matrix products, arithmetic and copies ran while one was open for 1% of the time, Pallas kernels for 7%

profile of v1, /device:TPU:1, one launch (start us, length us, event | category | flops | bytes accessed | tf_op | source)
XLA Modules:
  0.0 167.0 jit_solution(16042611607579948353)
XLA Ops:
  6.5 1.4 pad_maximum_fusion
  7.9 0.0 all-gather.2.cloned.1.call-update
  7.9 3.5 %front.1 = (bf16[128,1536]{1,0:T(8,128)(2,1)}, bf16[512,128]{1,0:T(8,128)(2,1)}) custom-call(bf16[128,512]{1,0:T(8,128)(2,1)} %refs_1_.3, bf16[512,1536]{1,0:T(8,128)(2,1)} %refs_1_.2, f32[8,128]{1,0:T(8,128)} %refs_3_.2), custom_call_target="tpu_custom_call" | custom-call | tf_op jit(solution)/shard_map/front/pallas_call | solution.py:233
  11.4 18.4 %all-to-all-start = ((bf16[128,4,128]{2,1,0:T(4,128)(2,1)}), bf16[128,4,128]{2,1,0:T(4,128)(2,1)S(1)}, u32[]{:S(2)}, u32[]{:S(2)}) async-start(bf16[128,4,128]{2,1,0:T(4,128)(2,1)} %bitcast.26), calls=%async_computation | async-start | bytes 262144 | tf_op jit(solution)/shard_map/all_to_all | solution.py:245
  29.9 0.2 convert_reduce_fusion.1
  30.0 0.1 select_reduce_fusion
  30.2 12.0 %all-to-all-done = bf16[128,4,128]{2,1,0:T(4,128)(2,1)S(1)} async-done(((bf16[128,4,128]{2,1,0:T(4,128)(2,1)}), bf16[128,4,128]{2,1,0:T(4,128)(2,1)S(1)}, u32[]{:S(2)}, u32[]{:S(2)}) %all-to-all-start) | async-done | bytes 131104 | tf_op jit(solution)/shard_map/all_to_all | solution.py:245
  42.1 0.7 copy-done
  42.8 2.5 %prefix.2 = bf16[256,128]{1,0:T(8,128)(2,1)} custom-call(bf16[512,128]{1,0:T(8,128)(2,1)} %bitcast.20), custom_call_target="tpu_custom_call" | custom-call | tf_op jit(solution)/shard_map/prefix/pallas_call | solution.py:233
  45.3 6.1 %all-to-all-start.1 = ((bf16[128,2,128]{2,1,0:T(2,128)(2,1)}), bf16[128,2,128]{2,1,0:T(2,128)(2,1)S(1)}, u32[]{:S(2)}, u32[]{:S(2)}) async-start(bf16[128,2,128]{2,1,0:T(2,128)(2,1)} %bitcast.23), calls=%async_computation.1 | async-start | bytes 131072 | tf_op jit(solution)/shard_map/all_to_all | solution.py:245
  51.5 0.3 convert_reduce_fusion
  51.7 0.6 concatenate.6.refs_0_
  52.4 10.7 %all-to-all-done.1 = bf16[128,2,128]{2,1,0:T(2,128)(2,1)S(1)} async-done(((bf16[128,2,128]{2,1,0:T(2,128)(2,1)}), bf16[128,2,128]{2,1,0:T(2,128)(2,1)S(1)}, u32[]{:S(2)}, u32[]{:S(2)}) %all-to-all-start.1) | async-done | bytes 65568 | tf_op jit(solution)/shard_map/all_to_all | solution.py:245
  63.1 0.6 copy-done.1
  63.7 4.0 %middle.1 = bf16[256,512]{1,0:T(8,128)(2,1)} custom-call(s32[163]{0:T(256)} %concatenate.6.refs_0_, bf16[128,512]{1,0:T(8,128)(2,1)} %refs_1_.3, bf16[128,1536]{1,0:T(8,128)(2,1)} %get-tuple-element.11.refs_2_, f32[8,128]{1,0:T(8,128)} %refs_3_.2, bf16[256,128]{1,0:T(8,128)(2,1)} %bitcast.22, bf16[512,512]{1,0:T(8,128)(2,1)} %refs_5_.1), custom_call_target="tpu_custom_call" | custom-call | tf_op jit(solution)/shard_map/middle/pallas_call | solution.py:233
  67.7 16.4 %all_to_all.30 = bf16[8,32,512]{2,1,0:T(8,128)(2,1)} all-to-all(bf16[8,32,512]{2,1,0:T(8,128)(2,1)} %bitcast.19), channel_id=1, replica_groups=mesh['seq_0'=8,'seq_1'=8,'seq_2'=2,'rep'=4] {'seq_0'}, dimensions={0} | all-to-all | bytes 524288 | tf_op jit(solution)/shard_map/all_to_all | solution.py:245
  84.0 1.9 %across.1 = bf16[256,512]{1,0:T(8,128)(2,1)} custom-call(s32[163]{0:T(256)} %concatenate.6.refs_0_, bf16[256,512]{1,0:T(8,128)(2,1)} %bitcast.17), custom_call_target="tpu_custom_call" | custom-call | tf_op jit(solution)/shard_map/across/pallas_call | solution.py:233
  86.0 17.4 %all_to_all.31 = bf16[16,16,512]{2,1,0:T(8,128)(2,1)} all-to-all(bf16[16,16,512]{2,1,0:T(8,128)(2,1)} %bitcast.18), channel_id=1, replica_groups=mesh['seq_0'=8,'seq_1'=8,'seq_2'=2,'rep'=4] {'seq_1','seq_2'}, dimensions={0} | all-to-all | bytes 524288 | tf_op jit(solution)/shard_map/all_to_all | solution.py:245
  103.3 1.3 all-gather.2.cloned.1.call-done.refs_2_
  104.6 7.0 %second.1 = (bf16[256,512]{1,0:T(8,128)(2,1)}, bf16[256,1536]{1,0:T(8,128)(2,1)}, f32[8,256]{1,0:T(8,128)}, bf16[512,128]{1,0:T(8,128)(2,1)}) custom-call(s32[163]{0:T(256)} %concatenate.6.refs_0_, bf16[256,512]{1,0:T(8,128)(2,1)} %bitcast.16, bf16[2048,1024]{1,0:T(8,128)(2,1)} %all-gather.2.cloned.1.call-done.refs_2_, bf16[512,1536]{1,0:T(8,128)(2,1)} %refs_3_.3, ...), custom_call_target="tpu_custom_call" | custom-call | tf_op jit(solution)/shard_map/second/pallas_call | solution.py:233
  111.6 23.8 %all_to_all.32 = bf16[128,4,128]{2,1,0:T(4,128)(2,1)} all-to-all(bf16[128,4,128]{2,1,0:T(4,128)(2,1)} %bitcast.27), channel_id=1, replica_groups=mesh['seq_0'=8,'seq_1'=8,'seq_2'=2,'rep'=4] {'seq_0','seq_1','seq_2'}, dimensions={0} | all-to-all | bytes 262144 | tf_op jit(solution)/shard_map/all_to_all | solution.py:245
  135.3 2.5 %prefix.3 = bf16[256,128]{1,0:T(8,128)(2,1)} custom-call(bf16[512,128]{1,0:T(8,128)(2,1)} %bitcast.21), custom_call_target="tpu_custom_call" | custom-call | tf_op jit(solution)/shard_map/prefix/pallas_call | solution.py:233
  137.9 18.3 %all_to_all.33 = bf16[128,2,128]{2,1,0:T(2,128)(2,1)} all-to-all(bf16[128,2,128]{2,1,0:T(2,128)(2,1)} %bitcast.24), channel_id=1, replica_groups=mesh['seq_0'=8,'seq_1'=8,'seq_2'=2,'rep'=4] {'seq_0','seq_1','seq_2'}, dimensions={0} | all-to-all | bytes 131072 | tf_op jit(solution)/shard_map/all_to_all | solution.py:245
  156.1 4.0 %last.1 = bf16[256,512]{1,0:T(8,128)(2,1)} custom-call(bf16[256,512]{1,0:T(8,128)(2,1)} %get-tuple-element.13.refs_0_, bf16[256,1536]{1,0:T(8,128)(2,1)} %get-tuple-element.14.refs_1_, f32[8,256]{1,0:T(8,128)} %get-tuple-element.15.refs_2_, bf16[256,128]{1,0:T(8,128)(2,1)} %bitcast.25, bf16[512,512]{1,0:T(8,128)(2,1)} %refs_4_.3), custom_call_target="tpu_custom_call" | custom-call | tf_op jit(solution)/shard_map/last/pallas_call | solution.py:233
  (8 shorter events, 0.0 us)
Async XLA Ops:
  6.5 23.3 %slice-start = ((s32[2048]{0:T(1024)}), s32[16]{0:T(128)S(1)}, s32[]{:S(2)}) async-start(s32[2048]{0:T(1024)} %param.13), calls=%async_computation.7 | async-start | bytes 1024 | tf_op jit(solution)/shard_map/slice | solution.py:266
  6.5 44.9 %copy-start.2 = (s32[2048]{0:T(1024)S(1)}, s32[2048]{0:T(1024)}, u32[]{:S(2)}) copy-start(s32[2048]{0:T(1024)} %param.13) | copy-start | bytes 24580
  6.5 98.0 %all-gather.2.cloned.1.call-start = ((), (), s32[]{:S(2)}) async-start(), calls=%async_computation.6 | async-start | bytes 4227072 | tf_op jit(solution)/shard_map/all_gather | solution.py:262
  11.4 30.7 %all-to-all-start = ((bf16[128,4,128]{2,1,0:T(4,128)(2,1)}), bf16[128,4,128]{2,1,0:T(4,128)(2,1)S(1)}, u32[]{:S(2)}, u32[]{:S(2)}) async-start(bf16[128,4,128]{2,1,0:T(4,128)(2,1)} %bitcast.26), calls=%async_computation | async-start | bytes 262144 | tf_op jit(solution)/shard_map/all_to_all | solution.py:245
  42.1 0.7 copy-start
  45.3 17.8 %all-to-all-start.1 = ((bf16[128,2,128]{2,1,0:T(2,128)(2,1)}), bf16[128,2,128]{2,1,0:T(2,128)(2,1)S(1)}, u32[]{:S(2)}, u32[]{:S(2)}) async-start(bf16[128,2,128]{2,1,0:T(2,128)(2,1)} %bitcast.23), calls=%async_computation.1 | async-start | bytes 131072 | tf_op jit(solution)/shard_map/all_to_all | solution.py:245
  63.1 0.6 copy-start.1
Sparse Core Ops, SparseCore 0:
  10.5 94.0 all-gather.1

commit v2 on v1

--- a/solution.py
+++ b/solution.py
@@ -13,7 +13,7 @@
 BR = 8
 CAP = 32
 SEQ = ("seq_0", "seq_1", "seq_2")
-ROW = ("seq_1", "seq_2")
+CHIPS = ("seq_0", "seq_1")
 REP_SEQ = ("rep", "seq_0", "seq_1", "seq_2")
 EPS = 1e-05
 F32 = jnp.float32
@@ -158,52 +158,45 @@
     return jnp.concatenate(attended, axis=1)
 
 
-def picked(meta, base, count, group):
-    return sum(jnp.where(group == k, meta[base + k], 0) for k in range(count))
-
-
-def middle(meta, points, qkv, decay, entering, w_out):
+def middle(chips, points, qkv, decay, entering, w_out):
     by_head, by_row = running_sums(decay[...])
     attended = attend(qkv[...], by_head, by_row, entering[...])
     first = (points[...].astype(F32) + dot(attended, w_out[...])).astype(BF16)
-    shape = (256, 128)
+    shape = (512, 128)
     place, column = iota(shape, 0), iota(shape, 1)
-    begin = picked_strided(meta, 0, place // 32)
-    end = picked_strided(meta, 16, place // 32)
-    where = begin + ((meta[160] - begin) & 127) + 128 * ((place // BR) & 3)
-    block = picked(meta, 144, 16, where >> 7)
-    chosen = (where < end) & (column == block * BR + (place & 7))
+    chosen = (place // BR == chips[...]) & ((place & 7) == (column & 7))
     return dot(ones_where(chosen), first).astype(BF16)
 
 
-def picked_strided(meta, shift, group):
-    return sum(jnp.where(group == k, meta[shift + 16 * k], 0) for k in range(8))
-
-
 def across(meta, arrived):
+    shape = (256, 512)
+    place, column = iota(shape, 0), iota(shape, 1)
+    begin = jnp.where(place < 128, meta[0], meta[1])
+    end = jnp.where(place < 128, meta[1], meta[2])
+    where = begin + ((meta[3] - begin) & 1) + 2 * ((place // BR) & 15)
+    held = (where & 127) >> 1
+    chosen = (where < end) & (column == held * BR + (place & 7))
+    return dot(ones_where(chosen), arrived[...]).astype(BF16)
+
+
+def second(meta, arrived, weights, others, w_qkv, decay):
     shape = (256, 256)
     place, column = iota(shape, 0), iota(shape, 1)
-    base = meta[161]
-    begin = sum(jnp.where(place // 16 == k, meta[base + k], 0) for k in range(16))
-    end = sum(jnp.where(place // 16 == k, meta[base + k + 1], 0) for k in range(16))
-    where = begin + ((meta[162] - begin) & 15) + 16 * ((place // BR) & 1)
-    held = ((where & 127) >> 4) * 4 + ((where - meta[base]) >> 7)
-    chosen = (where < end) & (column == held * BR + (place & 7))
-    return dot(ones_where(chosen), arrived[...]).astype(BF16)
-
-
-def second(meta, arrived, weights, w_qkv, decay):
-    shape = (256, 256)
-    place, column = iota(shape, 0), iota(shape, 1)
-    begin = meta[meta[160]]
-    used = meta[meta[160] + 1] - begin
+    begin = jnp.where(meta[3] == 0, meta[0], meta[1])
+    used = jnp.where(meta[3] == 0, meta[1], meta[2]) - begin
     slot = place // BR
-    held = ((begin + slot) & 15) * 2 + slot // 16
+    held = ((begin + slot) & 1) * 16 + slot // 2
     chosen = (slot < used) & (column == held * BR + (place & 7))
     first = dot(ones_where(chosen), arrived[...])
     normed = rms_rows(first).astype(BF16)
-    hidden = jax.nn.gelu(dot(normed, weights[:, :D], NT), approximate=True).astype(BF16)
-    placed = (first + dot(hidden, weights[:, D:])).astype(BF16)
+    rows = weights.shape[0] // 2
+    down_sum = first
+    for part in (weights, others):
+        up = part[pl.ds(pl.multiple_of(meta[4], rows), rows), :]
+        down = part[pl.ds(pl.multiple_of(rows - meta[4], rows), rows), :]
+        hidden = jax.nn.gelu(dot(normed, up, NT), approximate=True).astype(BF16)
+        down_sum = down_sum + dot(hidden, down)
+    placed = down_sum.astype(BF16)
     qkv = project(placed.astype(F32), w_qkv[...])
     kept = jnp.where(iota(decay.shape, 1) < BR * used, decay[...], 0.0)
     by_head, by_row = running_sums(kept)
@@ -257,44 +250,52 @@
     w_qkv_two,
     w_out_two,
 ):
+    plane = lax.axis_index("rep")
+    half = plane // 2 * BR
+    mine = jnp.where(
+        plane % 2 == 0,
+        lax.dynamic_slice_in_dim(w_up, half, BR, 1).T,
+        lax.dynamic_slice_in_dim(w_down, half, BR, 0),
+    )
+    quarter = lax.all_to_all(
+        jnp.broadcast_to(mine[None], (64, BR, D)), CHIPS, split_axis=0, concat_axis=0, tiled=True
+    ).reshape(64 * BR, D)
     position = lax.axis_index(SEQ)
-    joined = jnp.concatenate([w_up.T, w_down], axis=1)
-    weights = lax.all_gather(joined, SEQ, axis=0, tiled=True)
-
-    limits = CAP * iota((144, 1), 0)
+    core = lax.axis_index("seq_2")
+    limits = CAP * (position - core + iota((3, 1), 0))
     starts = jnp.sum((block_target[None, :] < limits).astype(jnp.int32), axis=1)
-    own = block_target[:16]
-    rank = jnp.sum((own[None, :] < own[:, None]).astype(jnp.int32), axis=1)
-    order = jnp.sum(jnp.where(rank[None, :] == iota((16, 16), 0), iota((16, 16), 1), 0), axis=1)
-    here = jnp.stack([position, position // 16 * 16, position % 16]).astype(jnp.int32)
-    meta = jnp.concatenate([starts, order, here])
+    meta = jnp.concatenate([starts, jnp.stack([core, plane % 2 * 1024]).astype(jnp.int32)])
+    own = lax.dynamic_slice_in_dim(block_target, position * 16, 16)
+    chips = jnp.repeat(own // (2 * CAP), BR)[None, :]
 
     qkv, sent = kernel_call(
         front, [((128, 3 * D), BF16), ((512, 128), BF16)], points, w_qkv_one, decay_one
     )
+    quarter, sent = lax.optimization_barrier((quarter, sent))
+    planes = [
+        lax.ppermute(quarter, "rep", [(i, i ^ step) for i in range(4)]) for step in (2, 1, 3)
+    ]
     received = whole(sent, SEQ, 128)
+    planes, received = lax.optimization_barrier((planes, received))
     summed = kernel_call(prefix, [((256, 128), BF16)], received)
+    weights = jnp.concatenate([quarter] + planes, axis=0)
     entering = whole(summed, SEQ, 128)
+    weights, entering = lax.optimization_barrier((weights, entering))
+    others = lax.ppermute(weights, "seq_2", [(0, 1), (1, 0)])
     outgoing = kernel_call(
-        middle,
-        [((256, D), BF16)],
-        meta,
-        points,
-        qkv,
-        decay_one,
-        entering,
-        w_out_one,
-        scalars=1,
-    )
-    arrived = whole(outgoing, "seq_0", 8)
+        middle, [((512, D), BF16)], chips, points, qkv, decay_one, entering, w_out_one
+    )
+    arrived = whole(outgoing, CHIPS, 64)
     outgoing = kernel_call(across, [((256, D), BF16)], meta, arrived, scalars=1)
-    arrived = whole(outgoing, ROW, 16)
+    arrived = whole(outgoing, "seq_2", 2)
+    others, arrived = lax.optimization_barrier((others, arrived))
     placed, qkv, decay, sent = kernel_call(
         second,
         [((256, D), BF16), ((256, 3 * D), BF16), ((HEADS, 256), F32), ((512, 128), BF16)],
         meta,
         arrived,
         weights,
+        others,
         w_qkv_two,
         decay_two,
         scalars=1,

time: 168 us -> 182 us (1.083)
  waiting for transfers between devices: 23.9 us -> 39.9 us
  starting transfers between devices: 24.5 us -> 40.4 us
  between operations: 13.5 us -> 0.13 us
  blocking collectives: 75.7 us -> 68.2 us
  local copies, waits for them, and re-layouts: 1.92 us -> 3.97 us
    all_to_all x0 -> x1, starting transfers between devices: none -> 17.1 us  [shards(): lax.all_to_all(jnp.broadcast_to(mine[None], (64, BR, D)), CHIPS, split_ax...]
    all_to_all x2, starting transfers between devices: 24.5 us -> 11.2 us  [whole(): lax.all_to_all(split, axes, split_axis=0, concat_axis=0, tiled=True)]
    all_to_all x0 -> x1, waiting for transfers between devices: none -> 13 us  [shards(): lax.all_to_all(jnp.broadcast_to(mine[None], (64, BR, D)), CHIPS, split_ax...]
    ppermute x0 -> x4, starting transfers between devices: none -> 12 us  [the longest x3 9.57 us: shards(): lax.ppermute(quarter, 'rep', [(i, i ^ step) for i in range(4)])]
    all_to_all x4, blocking collectives: 75.7 us -> 68.2 us  [whole(): lax.all_to_all(split, axes, split_axis=0, concat_axis=0, tiled=True)]
    all_to_all x2, waiting for transfers between devices: 22.7 us -> 27 us  [whole(): lax.all_to_all(split, axes, split_axis=0, concat_axis=0, tiled=True)]
  transfers between devices with their start and end apart: 3 -> 7, of which waited for: 3 -> 3; matrix products, arithmetic and copies ran while one was open for 1% -> 2% of each run, Pallas kernels for 7% -> 5%
where the time goes in v2:
time: 182 us; the launch traced here: 181 us
  blocking collectives  68.2 us (37%)
  starting transfers between devices  40.4 us (22%)
  waiting for transfers between devices  39.9 us (22%)
  Pallas kernels  25.6 us (14%)
  local copies, waits for them, and re-layouts  3.97 us (2%)
  other arithmetic  2.94 us (2%)
    all_to_all x4, blocking collectives, whole(): lax.all_to_all(split, axes, split_axis=0, concat_axis=0, tiled=True)  68.2 us
    all_to_all x2, waiting for transfers between devices, whole(): lax.all_to_all(split, axes, split_axis=0, concat_axis=0, tiled=True)  27 us
    pallas_call x7, Pallas kernels, kernel_call(): pl.pallas_call(body, out_shape=[jax.ShapeDtypeStruct(shape, kind) for sha...  25.6 us
    all_to_all x1, starting transfers between devices, shards(): lax.all_to_all(jnp.broadcast_to(mine[None], (64, BR, D)), CHIPS, split_ax...  17.1 us
    all_to_all x1, waiting for transfers between devices, shards(): lax.all_to_all(jnp.broadcast_to(mine[None], (64, BR, D)), CHIPS, split_ax...  13 us
    all_to_all x2, starting transfers between devices, whole(): lax.all_to_all(split, axes, split_axis=0, concat_axis=0, tiled=True)  11.2 us
    ppermute x3, starting transfers between devices, shards(): lax.ppermute(quarter, 'rep', [(i, i ^ step) for i in range(4)])  9.57 us
  transfers between devices with their start and end apart: 7, of which 3 were waited for; matrix products, arithmetic and copies ran while one was open for 2% of the time, Pallas kernels for 5%

profile of v2, /device:TPU:1, one launch (start us, length us, event | category | flops | bytes accessed | tf_op | source)
XLA Modules:
  0.0 181.1 jit_solution(2157456669996230340)
XLA Ops:
  0.7 0.8 broadcast_in_dim.4
  1.5 17.1 %all-to-all-start = ((bf16[64,8,512]{2,1,0:T(8,128)(2,1)}), bf16[64,8,512]{2,1,0:T(8,128)(2,1)S(1)}, u32[]{:S(2)}, u32[]{:S(2)}) async-start(bf16[64,8,512]{2,1,0:T(8,128)(2,1)} %broadcast_in_dim.4), calls=%async_computation | async-start | bytes 1048576 | tf_op jit(solution)/shard_map/all_to_all | solution.py:260
  18.7 3.5 %front.1 = (bf16[128,1536]{1,0:T(8,128)(2,1)}, bf16[512,128]{1,0:T(8,128)(2,1)}) custom-call(bf16[128,512]{1,0:T(8,128)(2,1)} %refs_1_.3, bf16[512,1536]{1,0:T(8,128)(2,1)} %refs_1_.2, f32[8,128]{1,0:T(8,128)} %refs_3_.1), custom_call_target="tpu_custom_call" | custom-call | tf_op jit(solution)/shard_map/front/pallas_call | solution.py:226
  22.2 13.0 %all-to-all-done = bf16[64,8,512]{2,1,0:T(8,128)(2,1)S(1)} async-done(((bf16[64,8,512]{2,1,0:T(8,128)(2,1)}), bf16[64,8,512]{2,1,0:T(8,128)(2,1)S(1)}, u32[]{:S(2)}, u32[]{:S(2)}) %all-to-all-start) | async-done | bytes 524320 | tf_op jit(solution)/shard_map/all_to_all | solution.py:260
  35.1 4.4 %collective-permute-start.2 = (bf16[512,512]{1,0:T(8,128)(2,1)S(1)}, bf16[512,512]{1,0:T(8,128)(2,1)S(1)}, u32[]{:S(2)}, u32[]{:S(2)}) collective-permute-start(bf16[512,512]{1,0:T(8,128)(2,1)S(1)} %bitcast.19), channel_id=1, source_target_pairs={{0,3},{1,2},{2,1},{3,0},{4,7},{5,6},{6,5},{7,4},{8,11},{9,10},{10,... | collective-permute-start | bytes 1572872 | tf_op jit(solution)/shard_map/ppermute | solution.py:276
  39.5 1.9 %collective-permute-start.1 = (bf16[512,512]{1,0:T(8,128)(2,1)S(1)}, bf16[512,512]{1,0:T(8,128)(2,1)S(1)}, u32[]{:S(2)}, u32[]{:S(2)}) collective-permute-start(bf16[512,512]{1,0:T(8,128)(2,1)S(1)} %bitcast.20), channel_id=1, source_target_pairs={{0,1},{1,0},{2,3},{3,2},{4,5},{5,4},{6,7},{7,6},{8,9},{9,8},{10,11... | collective-permute-start | bytes 1572872 | tf_op jit(solution)/shard_map/ppermute | solution.py:276
  41.5 3.3 %collective-permute-start = (bf16[512,512]{1,0:T(8,128)(2,1)S(1)}, bf16[512,512]{1,0:T(8,128)(2,1)S(1)}, u32[]{:S(2)}, u32[]{:S(2)}) collective-permute-start(bf16[512,512]{1,0:T(8,128)(2,1)S(1)} %bitcast.21), channel_id=1, source_target_pairs={{0,2},{1,3},{2,0},{3,1},{4,6},{5,7},{6,4},{7,5},{8,10},{9,11},{10,... | collective-permute-start | bytes 1572872 | tf_op jit(solution)/shard_map/ppermute | solution.py:276
  44.7 23.1 %all_to_all.35 = bf16[128,4,128]{2,1,0:T(4,128)(2,1)} all-to-all(bf16[128,4,128]{2,1,0:T(4,128)(2,1)} %bitcast.31), channel_id=1, replica_groups=mesh['seq_0'=8,'seq_1'=8,'seq_2'=2,'rep'=4] {'seq_0','seq_1','seq_2'}, dimensions={0} | all-to-all | bytes 262144 | tf_op jit(solution)/shard_map/all_to_all | solution.py:238
  68.7 0.8 copy-done.3
  69.5 2.5 %prefix.2 = bf16[256,128]{1,0:T(8,128)(2,1)} custom-call(bf16[512,128]{1,0:T(8,128)(2,1)} %bitcast.25), custom_call_target="tpu_custom_call" | custom-call | tf_op jit(solution)/shard_map/prefix/pallas_call | solution.py:226
  72.0 6.6 %all-to-all-start.2 = ((bf16[128,2,128]{2,1,0:T(2,128)(2,1)}), bf16[128,2,128]{2,1,0:T(2,128)(2,1)S(1)}, u32[]{:S(2)}, u32[]{:S(2)}) async-start(bf16[128,2,128]{2,1,0:T(2,128)(2,1)} %bitcast.28), calls=%async_computation.2 | async-start | bytes 131072 | tf_op jit(solution)/shard_map/all_to_all | solution.py:238
  78.6 1.3 pad_maximum_fusion.refs_2_
  80.0 10.1 %all-to-all-done.2 = bf16[128,2,128]{2,1,0:T(2,128)(2,1)S(1)} async-done(((bf16[128,2,128]{2,1,0:T(2,128)(2,1)}), bf16[128,2,128]{2,1,0:T(2,128)(2,1)S(1)}, u32[]{:S(2)}, u32[]{:S(2)}) %all-to-all-start.2) | async-done | bytes 65568 | tf_op jit(solution)/shard_map/all_to_all | solution.py:238
  90.1 2.4 %collective-permute-start.3 = (bf16[2048,512]{1,0:T(8,128)(2,1)S(1)}, bf16[2048,512]{1,0:T(8,128)(2,1)}, u32[]{:S(2)}, u32[]{:S(2)}) collective-permute-start(bf16[2048,512]{1,0:T(8,128)(2,1)S(1)} %pad_maximum_fusion.refs_2_), channel_id=1, source_target_pairs={{0,4},{4,0},{1,5},{5,1},{2,6},{6,2},{3,7},{7,3},{8,12},{12,8},{9,1... | collective-permute-start | bytes 6291464 | tf_op jit(solution)/shard_map/ppermute | solution.py:284
  93.4 4.0 %middle.1 = bf16[512,512]{1,0:T(8,128)(2,1)} custom-call(s32[1,128]{1,0:T(1,128)} %broadcast_in_dim_reshape.3.refs_0_, bf16[128,512]{1,0:T(8,128)(2,1)} %refs_1_.3, bf16[128,1536]{1,0:T(8,128)(2,1)} %get-tuple-element.29.refs_2_, f32[8,128]{1,0:T(8,128)} %refs_3_.1, bf16[256,128]{1,0:T(8,128)(2,1)} %bitcast.27, bf16[512,512]{1,0:T(8,128)(2,1)} %refs_5_.2), custom_call_target="tpu_custom_call" | custom-call | tf_op jit(solution)/shard_map/middle/pallas_call | solution.py:226
  97.4 4.6 %all-to-all-start.3 = ((bf16[64,8,512]{2,1,0:T(8,128)(2,1)}), bf16[64,8,512]{2,1,0:T(8,128)(2,1)S(1)}, u32[]{:S(2)}, u32[]{:S(2)}) async-start(bf16[64,8,512]{2,1,0:T(8,128)(2,1)} %bitcast.18), calls=%async_computation.3 | async-start | bytes 1048576 | tf_op jit(solution)/shard_map/all_to_all | solution.py:238
  102.9 16.8 %all-to-all-done.3 = bf16[64,8,512]{2,1,0:T(8,128)(2,1)S(1)} async-done(((bf16[64,8,512]{2,1,0:T(8,128)(2,1)}), bf16[64,8,512]{2,1,0:T(8,128)(2,1)S(1)}, u32[]{:S(2)}, u32[]{:S(2)}) %all-to-all-start.3) | async-done | bytes 524320 | tf_op jit(solution)/shard_map/all_to_all | solution.py:238
  120.5 2.1 %across.1 = bf16[256,512]{1,0:T(8,128)(2,1)} custom-call(s32[5]{0:T(128)} %pad_add_fusion.refs_0_, bf16[512,512]{1,0:T(8,128)(2,1)} %bitcast.17), custom_call_target="tpu_custom_call" | custom-call | tf_op jit(solution)/shard_map/across/pallas_call | solution.py:226
  122.6 7.1 %all_to_all.36 = bf16[2,128,512]{2,1,0:T(8,128)(2,1)} all-to-all(bf16[2,128,512]{2,1,0:T(8,128)(2,1)} %bitcast.24), channel_id=1, replica_groups=mesh['seq_0'=8,'seq_1'=8,'seq_2'=2,'rep'=4] {'seq_2'}, dimensions={0} | all-to-all | bytes 524288 | tf_op jit(solution)/shard_map/all_to_all | solution.py:238
  129.7 6.9 %second.1 = (bf16[256,512]{1,0:T(8,128)(2,1)}, bf16[256,1536]{1,0:T(8,128)(2,1)}, f32[8,256]{1,0:T(8,128)}, bf16[512,128]{1,0:T(8,128)(2,1)}) custom-call(s32[5]{0:T(128)} %pad_add_fusion.refs_0_, bf16[256,512]{1,0:T(8,128)(2,1)} %bitcast.23, bf16[2048,512]{1,0:T(8,128)(2,1)} %copy-done, bf16[2048,512]{1,0:T(8,128)(2,1)} %collective-permute-done.3.refs_3_, ...), custom_call_target="tpu_custom_call" | custom-call | tf_op jit(solution)/shard_map/second/pallas_call | solution.py:226
  136.6 19.6 %all_to_all.37 = bf16[128,4,128]{2,1,0:T(4,128)(2,1)} all-to-all(bf16[128,4,128]{2,1,0:T(4,128)(2,1)} %bitcast.32), channel_id=1, replica_groups=mesh['seq_0'=8,'seq_1'=8,'seq_2'=2,'rep'=4] {'seq_0','seq_1','seq_2'}, dimensions={0} | all-to-all | bytes 262144 | tf_op jit(solution)/shard_map/all_to_all | solution.py:238
  156.3 2.5 %prefix.3 = bf16[256,128]{1,0:T(8,128)(2,1)} custom-call(bf16[512,128]{1,0:T(8,128)(2,1)} %bitcast.26), custom_call_target="tpu_custom_call" | custom-call | tf_op jit(solution)/shard_map/prefix/pallas_call | solution.py:226
  158.8 18.3 %all_to_all.38 = bf16[128,2,128]{2,1,0:T(2,128)(2,1)} all-to-all(bf16[128,2,128]{2,1,0:T(2,128)(2,1)} %bitcast.29), channel_id=1, replica_groups=mesh['seq_0'=8,'seq_1'=8,'seq_2'=2,'rep'=4] {'seq_0','seq_1','seq_2'}, dimensions={0} | all-to-all | bytes 131072 | tf_op jit(solution)/shard_map/all_to_all | solution.py:238
  177.1 4.0 %last.1 = bf16[256,512]{1,0:T(8,128)(2,1)} custom-call(bf16[256,512]{1,0:T(8,128)(2,1)} %get-tuple-element.33.refs_0_, bf16[256,1536]{1,0:T(8,128)(2,1)} %get-tuple-element.34.refs_1_, f32[8,256]{1,0:T(8,128)} %get-tuple-element.35.refs_2_, bf16[256,128]{1,0:T(8,128)(2,1)} %bitcast.30, bf16[512,512]{1,0:T(8,128)(2,1)} %refs_4_.3), custom_call_target="tpu_custom_call" | custom-call | tf_op jit(solution)/shard_map/last/pallas_call | solution.py:226
  (22 shorter events, 4.0 us)
Async XLA Ops:
  1.5 33.6 %all-to-all-start = ((bf16[64,8,512]{2,1,0:T(8,128)(2,1)}), bf16[64,8,512]{2,1,0:T(8,128)(2,1)S(1)}, u32[]{:S(2)}, u32[]{:S(2)}) async-start(bf16[64,8,512]{2,1,0:T(8,128)(2,1)} %broadcast_in_dim.4), calls=%async_computation | async-start | bytes 1048576 | tf_op jit(solution)/shard_map/all_to_all | solution.py:260
  35.1 32.7 %collective-permute-start.2 = (bf16[512,512]{1,0:T(8,128)(2,1)S(1)}, bf16[512,512]{1,0:T(8,128)(2,1)S(1)}, u32[]{:S(2)}, u32[]{:S(2)}) collective-permute-start(bf16[512,512]{1,0:T(8,128)(2,1)S(1)} %bitcast.19), channel_id=1, source_target_pairs={{0,3},{1,2},{2,1},{3,0},{4,7},{5,6},{6,5},{7,4},{8,11},{9,10},{10,... | collective-permute-start | bytes 1572872 | tf_op jit(solution)/shard_map/ppermute | solution.py:276
  39.5 28.4 %collective-permute-start.1 = (bf16[512,512]{1,0:T(8,128)(2,1)S(1)}, bf16[512,512]{1,0:T(8,128)(2,1)S(1)}, u32[]{:S(2)}, u32[]{:S(2)}) collective-permute-start(bf16[512,512]{1,0:T(8,128)(2,1)S(1)} %bitcast.20), channel_id=1, source_target_pairs={{0,1},{1,0},{2,3},{3,2},{4,5},{5,4},{6,7},{7,6},{8,9},{9,8},{10,11... | collective-permute-start | bytes 1572872 | tf_op jit(solution)/shard_map/ppermute | solution.py:276
  41.5 26.4 %collective-permute-start = (bf16[512,512]{1,0:T(8,128)(2,1)S(1)}, bf16[512,512]{1,0:T(8,128)(2,1)S(1)}, u32[]{:S(2)}, u32[]{:S(2)}) collective-permute-start(bf16[512,512]{1,0:T(8,128)(2,1)S(1)} %bitcast.21), channel_id=1, source_target_pairs={{0,2},{1,3},{2,0},{3,1},{4,6},{5,7},{6,4},{7,5},{8,10},{9,11},{10,... | collective-permute-start | bytes 1572872 | tf_op jit(solution)/shard_map/ppermute | solution.py:276
  67.9 0.8 copy-start.2
  68.7 0.8 copy-start.3
  72.0 18.1 %all-to-all-start.2 = ((bf16[128,2,128]{2,1,0:T(2,128)(2,1)}), bf16[128,2,128]{2,1,0:T(2,128)(2,1)S(1)}, u32[]{:S(2)}, u32[]{:S(2)}) async-start(bf16[128,2,128]{2,1,0:T(2,128)(2,1)} %bitcast.28), calls=%async_computation.2 | async-start | bytes 131072 | tf_op jit(solution)/shard_map/all_to_all | solution.py:238
  78.6 14.0 %copy-start.5 = (s32[2048]{0:T(1024)S(1)}, s32[2048]{0:T(1024)}, u32[]{:S(2)}) copy-start(s32[2048]{0:T(1024)} %param.13) | copy-start | bytes 24580
  80.0 49.7 %copy-start = (bf16[2048,512]{1,0:T(8,128)(2,1)}, bf16[2048,512]{1,0:T(8,128)(2,1)S(1)}, u32[]{:S(2)}) copy-start(bf16[2048,512]{1,0:T(8,128)(2,1)S(1)} %pad_maximum_fusion.refs_2_) | copy-start | bytes 6291460
  90.1 3.3 %copy-start.4 = (bf16[128,2,128]{2,1,0:T(2,128)(2,1)}, bf16[128,2,128]{2,1,0:T(2,128)(2,1)S(1)}, u32[]{:S(2)}) copy-start(bf16[128,2,128]{2,1,0:T(2,128)(2,1)S(1)} %all-to-all-done.2) | copy-start | bytes 196612
  90.1 39.6 %collective-permute-start.3 = (bf16[2048,512]{1,0:T(8,128)(2,1)S(1)}, bf16[2048,512]{1,0:T(8,128)(2,1)}, u32[]{:S(2)}, u32[]{:S(2)}) collective-permute-start(bf16[2048,512]{1,0:T(8,128)(2,1)S(1)} %pad_maximum_fusion.refs_2_), channel_id=1, source_target_pairs={{0,4},{4,0},{1,5},{5,1},{2,6},{6,2},{3,7},{7,3},{8,12},{12,8},{9,1... | collective-permute-start | bytes 6291464 | tf_op jit(solution)/shard_map/ppermute | solution.py:284
  97.4 22.3 %all-to-all-start.3 = ((bf16[64,8,512]{2,1,0:T(8,128)(2,1)}), bf16[64,8,512]{2,1,0:T(8,128)(2,1)S(1)}, u32[]{:S(2)}, u32[]{:S(2)}) async-start(bf16[64,8,512]{2,1,0:T(8,128)(2,1)} %bitcast.18), calls=%async_computation.3 | async-start | bytes 1048576 | tf_op jit(solution)/shard_map/all_to_all | solution.py:238
  119.7 0.8 copy-start.1

commit v3 on v2

v3 whole, which is shorter than its diff:
```python
import jax
import jax.numpy as jnp
from jax import lax
from jax.experimental import pallas as pl
from jax.experimental.pallas import tpu as pltpu
from jax.sharding import Mesh
from jax.sharding import PartitionSpec as P

D = 512
HEADS = 8
HEAD_DIM = 64
PAIRS = HEADS // 2
BR = 8
CAP = 32
SEQ = ("seq_0", "seq_1", "seq_2")
CHIPS = ("seq_0", "seq_1")
ROW = ("seq_1", "seq_2")
REP_SEQ = ("rep", "seq_0", "seq_1", "seq_2")
EPS = 1e-05
F32 = jnp.float32
BF16 = jnp.bfloat16
DIRECT = False

NN = (((1,), (0,)), ((), ()))
NT = (((1,), (1,)), ((), ()))
TN = (((0,), (0,)), ((), ()))


def dot(a, b, dims=NN):
    return lax.dot_general(a, b, dims, preferred_element_type=F32)


def iota(shape, dim):
    return lax.broadcasted_iota(jnp.int32, shape, dim)


def ones_where(cond):
    return jnp.where(cond, 1.0, 0.0).astype(BF16)


def halves(x):
    high = x.astype(BF16)
    return high, (x - high.astype(F32)).astype(BF16)


def thirds(x):
    high, rest = x.astype(BF16), x - x.astype(BF16).astype(F32)
    middle, low = halves(rest)
    return high, middle, low


def rms_rows(wide):
    return wide * lax.rsqrt(jnp.mean(wide * wide, axis=-1, keepdims=True) + EPS)


def running_sums(decay):
    rows = decay.shape[1]
    parts = thirds(decay)
    upto = ones_where(iota((rows, rows), 0) >= iota((rows, rows), 1))
    by_head = sum(dot(part, upto, NT) for part in parts)
    by_row = sum(dot(upto, part, NT) for part in parts)
    return by_head, by_row


def pair_lanes(columns, pair):
    rows = columns.shape[0]
    first = iota((rows, 2 * HEAD_DIM), 1) < HEAD_DIM
    return jnp.where(
        first, columns[:, 2 * pair : 2 * pair + 1], columns[:, 2 * pair + 1 : 2 * pair + 2]
    )


def pack_state(keys_values, by_row):
    rows = keys_values.shape[0]
    total = by_row[rows - 1 : rows]
    weight = jnp.exp(total - by_row)
    lane = iota((HEAD_DIM, 128), 1)
    place = iota((128, HEAD_DIM), 0)
    spread = ones_where((place % 4 < 2) & (iota((128, HEAD_DIM), 1) == (place // 4) * 2 + place % 4))
    kind = iota((128, 128), 0) % 4
    packed = []
    for p in range(PAIRS):
        keys = keys_values[:, 128 * p : 128 * (p + 1)].astype(F32) * pair_lanes(weight, p)
        values = keys_values[:, D + 128 * p : D + 128 * (p + 1)]
        high, low = halves(keys)
        both = dot(high, values, TN) + dot(low, values, TN)
        state = jnp.where(lane < HEAD_DIM, both[:HEAD_DIM], both[HEAD_DIM:]).astype(BF16)
        high, low = halves(pair_lanes(total, p))
        piece = dot(spread, state)
        piece = jnp.where(kind == 2, high.astype(F32), piece)
        piece = jnp.where(kind == 3, low.astype(F32), piece)
        packed.append(piece.astype(BF16))
    return jnp.concatenate(packed, axis=0)


def front(points, weight, decay):
    normed = rms_rows(points[...].astype(F32)).astype(BF16)
    keys_values = dot(normed, weight[:, D:]).astype(BF16)
    by_row = running_sums(decay[...])[1]
    return normed, keys_values, pack_state(keys_values, by_row)


def prefix(received):
    rows = received[...]
    devices = rows.shape[0] // 4
    square = (devices, devices)
    pick = iota((devices, 4 * devices), 1) - 4 * iota((devices, 4 * devices), 0)
    states = [dot(ones_where(pick == j), rows).astype(BF16) for j in range(2)]
    totals = [dot(ones_where(pick == 2 + j), rows) for j in range(2)]
    earlier = iota(square, 1) < iota(square, 0)
    before = ones_where(earlier)
    later = iota(square, 0) > iota(square, 1)
    outs = []
    for half in range(2):
        gap = sum(
            dot(
                before,
                jnp.where(later, part[:, half * HEAD_DIM : half * HEAD_DIM + 1], 0.0).astype(BF16),
            )
            for part in totals
        )
        high, low = halves(jnp.where(earlier, jnp.exp(gap), 0.0))
        outs.append([dot(high, state) + dot(low, state) for state in states])
    lane = iota(square, 1) < HEAD_DIM
    back = iota((2 * devices, devices), 0) - 2 * iota((2 * devices, devices), 1)
    return sum(
        dot(ones_where(back == j), jnp.where(lane, outs[0][j], outs[1][j]).astype(BF16))
        for j in range(2)
    ).astype(BF16)


def inner(normed, weight, keys_values, decay):
    by_head, by_row = running_sums(decay[...])
    queries = (dot(normed[...], weight[:, :D]) * HEAD_DIM ** (-0.5)).astype(BF16)
    rows = queries.shape[0]
    causal = iota((rows, rows), 0) >= iota((rows, rows), 1)
    lanes = iota((1, 128), 1)
    sides = (ones_where(lanes < HEAD_DIM), ones_where(lanes >= HEAD_DIM))
    first = iota((rows, 128), 1) < HEAD_DIM
    summed = []
    for p in range(PAIRS):
        query = queries[:, 128 * p : 128 * (p + 1)]
        keys = keys_values[:, 128 * p : 128 * (p + 1)]
        values = keys_values[:, D + 128 * p : D + 128 * (p + 1)]
        both = []
        for side in range(2):
            h = 2 * p + side
            scores = dot(query * sides[side], keys, NT)
            gap = by_row[:, h : h + 1] - by_head[h : h + 1, :]
            weighted = scores * jnp.exp(jnp.where(causal, gap, -1e30))
            both.append(dot(weighted.astype(BF16), values))
        summed.append(jnp.where(first, both[0], both[1]))
    return queries, jnp.concatenate(summed, axis=1), jnp.exp(by_row)


def attended(queries, summed, grown, entering):
    lanes = iota((1, 128), 1)
    sides = (ones_where(lanes < HEAD_DIM), ones_where(lanes >= HEAD_DIM))
    same = ones_where(iota((128, 128), 0) // HEAD_DIM == iota((128, 128), 1) // HEAD_DIM)
    outs = []
    for p in range(PAIRS):
        state = entering[HEAD_DIM * p : HEAD_DIM * (p + 1), :]
        state = jnp.concatenate([state * sides[0], state * sides[1]], axis=0)
        carried = dot(queries[:, 128 * p : 128 * (p + 1)], state) * pair_lanes(grown[...], p)
        number = summed[:, 128 * p : 128 * (p + 1)] + carried
        high, low = halves(number * number)
        mean = (dot(high, same) + dot(low, same)) * (1.0 / HEAD_DIM)
        outs.append((number * lax.rsqrt(mean + EPS)).astype(BF16))
    return jnp.concatenate(outs, axis=1)


def middle(chips, points, queries, summed, grown, entering, w_out):
    mixed = dot(attended(queries, summed, grown, entering), w_out[...])
    first = (points[...].astype(F32) + mixed).astype(BF16)
    shape = (512, 128)
    place, column = iota(shape, 0), iota(shape, 1)
    chosen = (place // BR == chips[...]) & ((place & 7) == (column & 7))
    return dot(ones_where(chosen), first).astype(BF16)


def across(meta, arrived):
    shape = (256, 512)
    place, column = iota(shape, 0), iota(shape, 1)
    begin = jnp.where(place < 128, meta[0], meta[1])
    end = jnp.where(place < 128, meta[1], meta[2])
    where = begin + ((meta[3] - begin) & 1) + 2 * ((place // BR) & 15)
    held = (where & 127) >> 1
    chosen = (where < end) & (column == held * BR + (place & 7))
    return dot(ones_where(chosen), arrived[...]).astype(BF16)


def second(meta, arrived, w_qkv, decay, weights, up=None, down=None, copies=None):
    pieces = []
    if up is None:
        up, down = weights[:, :D], weights[:, D:]
    else:
        for k, buffer in enumerate((up, down)):
            pieces.append(
                pltpu.make_async_copy(weights.at[:, pl.ds(k * D, D)], buffer, copies.at[k])
            )
            pieces[k].start()
    shape = (256, 256)
    place, column = iota(shape, 0), iota(shape, 1)
    begin = jnp.where(meta[3] == 0, meta[0], meta[1])
    used = jnp.where(meta[3] == 0, meta[1], meta[2]) - begin
    slot = place // BR
    held = ((begin + slot) & 1) * 16 + slot // 2
    chosen = (slot < used) & (column == held * BR + (place & 7))
    kept = jnp.where(iota(decay.shape, 1) < BR * used, decay[...], 0.0)
    by_row = running_sums(kept)[1]
    first = dot(ones_where(chosen), arrived[...])
    normed = rms_rows(first).astype(BF16)
    if pieces:
        pieces[0].wait()
    hidden = jax.nn.gelu(dot(normed, up[...], NT), approximate=True).astype(BF16)
    if pieces:
        pieces[1].wait()
    placed = (first + dot(hidden, down[...])).astype(BF16)
    normed = rms_rows(placed.astype(F32)).astype(BF16)
    keys_values = dot(normed, w_qkv[:, D:]).astype(BF16)
    return placed, normed, keys_values, kept, pack_state(keys_values, by_row)


def last(placed, queries, summed, grown, entering, w_out):
    mixed = dot(attended(queries, summed, grown, entering), w_out[...])
    return (placed[...].astype(F32) + mixed).astype(BF16)


def kernel_call(function, outs, *args, scalars=0, loose=(), outside=(), streamed=(), scratch=()):
    if DIRECT:
        return function(*args)
    count = len(args)

    def body(*refs):
        results = function(*refs[:count], *refs[count + len(outs) :])
        if len(outs) == 1:
            results = (results,)
        for ref, value in zip(refs[count:], results):
            ref[...] = value

    def spec(k):
        if k < scalars:
            return pl.BlockSpec(memory_space=pltpu.SMEM)
        return pl.BlockSpec(memory_space=pltpu.HBM if k in streamed else pltpu.VMEM)

    args = [
        arg
        if k < scalars or k in loose
        else pltpu.with_memory_space_constraint(
            arg, pltpu.HBM if k in streamed + outside else pltpu.VMEM
        )
        for k, arg in enumerate(args)
    ]
    result = pl.pallas_call(
        body,
        compiler_params=pltpu.CompilerParams(vmem_limit_bytes=32 << 20),
        out_shape=[jax.ShapeDtypeStruct(shape, kind) for shape, kind in outs],
        in_specs=[spec(k) for k in range(count)],
        out_specs=[pl.BlockSpec(memory_space=pltpu.VMEM)] * len(outs),
        scratch_shapes=list(scratch),
        name=function.__name__,
    )(*args)
    return result[0] if len(outs) == 1 else result


def whole(x, axes, pieces):
    split = x.reshape(pieces, x.shape[0] // pieces, x.shape[1])
    return lax.all_to_all(split, axes, split_axis=0, concat_axis=0, tiled=True).reshape(x.shape)


def shards(
    points,
    decay_one,
    decay_two,
    block_target,
    w_qkv_one,
    w_out_one,
    w_up,
    w_down,
    w_qkv_two,
    w_out_two,
):
    joined = jnp.concatenate([w_up.T, w_down], axis=1)
    spread = jnp.broadcast_to(joined[None], (8, 16, 2 * D))
    column = lax.all_to_all(spread, "seq_0", split_axis=0, concat_axis=0, tiled=True)
    column = column.reshape(128, 2 * D)
    position = lax.axis_index(SEQ)
    core = lax.axis_index("seq_2")
    limits = CAP * (position - core + iota((3, 1), 0))
    starts = jnp.sum((block_target[None, :] < limits).astype(jnp.int32), axis=1)
    meta = jnp.concatenate([starts, jnp.stack([core]).astype(jnp.int32)])
    own = lax.dynamic_slice_in_dim(block_target, position * 16, 16)
    chips = jnp.repeat(own // (2 * CAP), BR)[None, :]

    normed, keys_values, sent = kernel_call(
        front,
        [((128, D), BF16), ((128, 2 * D), BF16), ((512, 128), BF16)],
        points,
        w_qkv_one,
        decay_one,
        loose=(0, 1, 2),
    )
    column, sent = lax.optimization_barrier((column, sent))
    weights = lax.all_gather(column, ROW, axis=0, tiled=True)
    received = whole(sent, SEQ, 128)
    own_rows = kernel_call(
        inner,
        [((128, D), BF16), ((128, D), F32), ((128, HEADS), F32)],
        normed,
        w_qkv_one,
        keys_values,
        decay_one,
        loose=(0, 2, 3),
        outside=(1,),
    )
    entering = whole(kernel_call(prefix, [((256, 128), BF16)], received), SEQ, 128)
    outgoing = kernel_call(
        middle, [((512, D), BF16)], chips, points, *own_rows, entering, w_out_one
    )
    arrived = whole(outgoing, CHIPS, 64)
    outgoing = kernel_call(across, [((256, D), BF16)], meta, arrived, scalars=1)
    arrived = whole(outgoing, "seq_2", 2)
    placed, normed, keys_values, decay, sent = kernel_call(
        second,
        [
            ((256, D), BF16),
            ((256, D), BF16),
            ((256, 2 * D), BF16),
            ((HEADS, 256), F32),
            ((512, 128), BF16),
        ],
        meta,
        arrived,
        w_qkv_two,
        decay_two,
        weights,
        scalars=1,
        streamed=(4,),
        scratch=(
            pltpu.VMEM((4 * D, D), BF16),
            pltpu.VMEM((4 * D, D), BF16),
            pltpu.SemaphoreType.DMA((2,)),
        ),
    )
    received = whole(sent, SEQ, 128)
    own_rows = kernel_call(
        inner,
        [((256, D), BF16), ((256, D), F32), ((256, HEADS), F32)],
        normed,
        w_qkv_two,
        keys_values,
        decay,
        loose=(0, 2, 3),
        outside=(1,),
    )
    entering = whole(kernel_call(prefix, [((256, 128), BF16)], received), SEQ, 128)
    return kernel_call(last, [((256, D), BF16)], placed, *own_rows, entering, w_out_two)


def solution(mesh):
    split = Mesh(
        mesh.devices.reshape(8, 8, 2, mesh.shape["rep"]), ("seq_0", "seq_1", "seq_2", "rep")
    )
    placed = (
        P(REP_SEQ, None),
        P(None, REP_SEQ),
        P(None, REP_SEQ),
        P("rep"),
        P(),
        P(),
        P(None, SEQ),
        P(SEQ, None),
        P(),
        P(),
    )
    return jax.shard_map(
        shards, mesh=split, in_specs=placed, out_specs=P(REP_SEQ, None), check_vma=False
    )
```

time: 182 us -> 156 us (0.86)
  starting transfers between devices: 40.4 us -> 24.3 us
  blocking collectives: 68.2 us -> 52.8 us
  between operations: 0.13 us -> 13.5 us
  Pallas kernels: 25.6 us -> 19.7 us
  other arithmetic: 2.94 us -> 1.1 us
    all_to_all x4 -> x3, blocking collectives: 68.2 us -> 52.8 us  [whole(): lax.all_to_all(split, axes, split_axis=0, concat_axis=0, tiled=True)]
    ppermute x4 -> x0, starting transfers between devices: 12 us -> none  [the longest x3 9.57 us: shards(): lax.ppermute(quarter, 'rep', [(i, i ^ step) for i in range(4)])]
    all_to_all x1, starting transfers between devices: 17.1 us -> 7.77 us  [shards(): lax.all_to_all(spread, 'seq_0', split_axis=0, concat_axis=0, tiled=True)]
    all_to_all x1, waiting for transfers between devices: 13 us -> 5 us  [shards(): lax.all_to_all(spread, 'seq_0', split_axis=0, concat_axis=0, tiled=True)]
    all_to_all x2 -> x3, waiting for transfers between devices: 27 us -> 34.3 us  [whole(): lax.all_to_all(split, axes, split_axis=0, concat_axis=0, tiled=True)]
    pallas_call x7 -> x9, Pallas kernels: 25.6 us -> 19.7 us  [kernel_call(): pl.pallas_call(body, compiler_params=pltpu.CompilerParams(vmem_limit_byte...]
    all_to_all x2 -> x3, starting transfers between devices: 11.2 us -> 16.5 us  [whole(): lax.all_to_all(split, axes, split_axis=0, concat_axis=0, tiled=True)]
    unnamed x12 -> x22, local copies, waits for them, and re-layouts: 2.38 us -> 3.73 us
  transfers between devices with their start and end apart: 7 -> 5, of which waited for: 3 -> 4; matrix products, arithmetic and copies ran while one was open for 2% -> 0% of each run, Pallas kernels for 5% -> 7%
where the time goes in v3:
time: 156 us; the launch traced here: 155 us
  blocking collectives  52.8 us (34%)
  waiting for transfers between devices  39.3 us (25%)
  starting transfers between devices  24.3 us (16%)
  Pallas kernels  19.7 us (13%)
  between operations  13.5 us (9%)
  local copies, waits for them, and re-layouts  4.62 us (3%)
    all_to_all x3, blocking collectives, whole(): lax.all_to_all(split, axes, split_axis=0, concat_axis=0, tiled=True)  52.8 us
    all_to_all x3, waiting for transfers between devices, whole(): lax.all_to_all(split, axes, split_axis=0, concat_axis=0, tiled=True)  34.3 us
    pallas_call x9, Pallas kernels, kernel_call(): pl.pallas_call(body, compiler_params=pltpu.CompilerParams(vmem_limit_byte...  19.7 us
    all_to_all x3, starting transfers between devices, whole(): lax.all_to_all(split, axes, split_axis=0, concat_axis=0, tiled=True)  16.5 us
    all_to_all x1, starting transfers between devices, shards(): lax.all_to_all(spread, 'seq_0', split_axis=0, concat_axis=0, tiled=True)  7.77 us
    all_to_all x1, waiting for transfers between devices, shards(): lax.all_to_all(spread, 'seq_0', split_axis=0, concat_axis=0, tiled=True)  5 us
    unnamed x22, local copies, waits for them, and re-layouts  3.73 us
  transfers between devices with their start and end apart: 5, of which 4 were waited for; matrix products, arithmetic and copies ran while one was open for 0% of the time, Pallas kernels for 7%

profile of v3, /device:TPU:1, one launch (start us, length us, event | category | flops | bytes accessed | tf_op | source)
XLA Modules:
  0.0 155.3 jit_solution(16314383508371858769)
XLA Ops:
  6.5 0.7 pad_maximum_fusion
  7.3 0.7 broadcast_in_dim.5
  8.0 7.8 %all-to-all-start = ((bf16[8,16,1024]{2,1,0:T(8,128)(2,1)}), bf16[8,16,1024]{2,1,0:T(8,128)(2,1)S(1)}, u32[]{:S(2)}, u32[]{:S(2)}) async-start(bf16[8,16,1024]{2,1,0:T(8,128)(2,1)} %broadcast_in_dim.5), calls=%async_computation | async-start | bytes 524288 | tf_op jit(solution)/shard_map/all_to_all | solution.py:285
  15.8 1.4 copy-done.1
  17.2 0.9 copy-done.4
  18.8 1.4 front.1
  20.2 5.0 %all-to-all-done = bf16[8,16,1024]{2,1,0:T(8,128)(2,1)S(1)} async-done(((bf16[8,16,1024]{2,1,0:T(8,128)(2,1)}), bf16[8,16,1024]{2,1,0:T(8,128)(2,1)S(1)}, u32[]{:S(2)}, u32[]{:S(2)}) %all-to-all-start) | async-done | bytes 262176 | tf_op jit(solution)/shard_map/all_to_all | solution.py:285
  25.9 27.3 %all_to_all.35 = bf16[128,4,128]{2,1,0:T(4,128)(2,1)S(1)} all-to-all(bf16[128,4,128]{2,1,0:T(4,128)(2,1)S(1)} %bitcast.22), channel_id=1, replica_groups=mesh['seq_0'=8,'seq_1'=8,'seq_2'=2,'rep'=4] {'seq_0','seq_1','seq_2'}, dimensions={0} | all-to-all | bytes 262144 | tf_op jit(solution)/shard_map/all_to_all | solution.py:268
  53.3 1.7 %prefix.2 = bf16[256,128]{1,0:T(8,128)(2,1)} custom-call(bf16[512,128]{1,0:T(8,128)(2,1)S(1)} %bitcast.18), custom_call_target="tpu_custom_call" | custom-call | tf_op jit(solution)/shard_map/prefix/pallas_call | solution.py:254
  55.0 5.8 %all-to-all-start.2 = ((bf16[128,2,128]{2,1,0:T(2,128)(2,1)}), bf16[128,2,128]{2,1,0:T(2,128)(2,1)S(1)}, u32[]{:S(2)}, u32[]{:S(2)}) async-start(bf16[128,2,128]{2,1,0:T(2,128)(2,1)} %bitcast.5), calls=%async_computation.2 | async-start | bytes 131072 | tf_op jit(solution)/shard_map/all_to_all | solution.py:268
  61.1 2.9 %inner.2 = (bf16[128,512]{1,0:T(8,128)(2,1)S(1)}, f32[128,512]{1,0:T(8,128)S(1)}, f32[128,8]{1,0:T(8,128)S(1)}) custom-call(bf16[128,512]{1,0:T(8,128)(2,1)S(1)} %get-tuple-element.21.refs_0_, bf16[512,1536]{1,0:T(8,128)(2,1)} %refs_1_.5, bf16[128,1024]{1,0:T(8,128)(2,1)S(1)} %get-tuple-element.22.refs_2_, f32[8,128]{1,0:T(8,128)S(1)} %copy-done.7), custom_call_target="tpu_custom_call" | custom-call | tf_op jit(solution)/shard_map/inner/pallas_call | solution.py:254
  63.9 8.6 %all-to-all-done.2 = bf16[128,2,128]{2,1,0:T(2,128)(2,1)S(1)} async-done(((bf16[128,2,128]{2,1,0:T(2,128)(2,1)}), bf16[128,2,128]{2,1,0:T(2,128)(2,1)S(1)}, u32[]{:S(2)}, u32[]{:S(2)}) %all-to-all-start.2) | async-done | bytes 65568 | tf_op jit(solution)/shard_map/all_to_all | solution.py:268
  72.5 1.8 %middle.1 = bf16[512,512]{1,0:T(8,128)(2,1)} custom-call(s32[1,128]{1,0:T(1,128)S(1)} %broadcast_in_dim_reshape.3.refs_0_, bf16[128,512]{1,0:T(8,128)(2,1)S(1)} %copy-done.5, bf16[128,512]{1,0:T(8,128)(2,1)S(1)} %get-tuple-element.23.refs_2_, f32[128,512]{1,0:T(8,128)S(1)} %get-tuple-element.24.refs_3_, f32[128,8]{1,0:T(8,128)S(1)} %get-tuple-element.25.refs_4_, ...), custom_call_target="tpu_custom_call" | custom-call | tf_op jit(solution)/shard_map/middle/pallas_call | solution.py:254
  74.3 4.8 %all-to-all-start.3 = ((bf16[64,8,512]{2,1,0:T(8,128)(2,1)}), bf16[64,8,512]{2,1,0:T(8,128)(2,1)S(1)}, u32[]{:S(2)}, u32[]{:S(2)}) async-start(bf16[64,8,512]{2,1,0:T(8,128)(2,1)} %bitcast.7), calls=%async_computation.3 | async-start | bytes 1048576 | tf_op jit(solution)/shard_map/all_to_all | solution.py:268
  79.4 16.7 %all-to-all-done.3 = bf16[64,8,512]{2,1,0:T(8,128)(2,1)S(1)} async-done(((bf16[64,8,512]{2,1,0:T(8,128)(2,1)}), bf16[64,8,512]{2,1,0:T(8,128)(2,1)S(1)}, u32[]{:S(2)}, u32[]{:S(2)}) %all-to-all-start.3) | async-done | bytes 524320 | tf_op jit(solution)/shard_map/all_to_all | solution.py:268
  96.0 0.8 across.1
  96.9 6.4 %all_to_all.36 = bf16[2,128,512]{2,1,0:T(8,128)(2,1)S(1)} all-to-all(bf16[2,128,512]{2,1,0:T(8,128)(2,1)S(1)} %bitcast.17), channel_id=1, replica_groups=mesh['seq_0'=8,'seq_1'=8,'seq_2'=2,'rep'=4] {'seq_2'}, dimensions={0} | all-to-all | bytes 524288 | tf_op jit(solution)/shard_map/all_to_all | solution.py:268
  103.3 5.3 %second.1 = (bf16[256,512]{1,0:T(8,128)(2,1)S(1)}, bf16[256,512]{1,0:T(8,128)(2,1)S(1)}, bf16[256,1024]{1,0:T(8,128)(2,1)S(1)}, f32[8,256]{1,0:T(8,128)S(1)}, bf16[512,128]{1,0:T(8,128)(2,1)S(1)}) custom-call(s32[4]{0:T(128)S(1)} %pad_add_fusion.refs_0_, bf16[256,512]{1,0:T(8,128)(2,1)S(1)} %bitcast.16, bf16[512,1536]{1,0:T(8,128)(2,1)S(1)} %copy-done, ...), custom_call_target="tpu_custom_call" | custom-call | tf_op jit(solution)/shard_map/second/pallas_call | solution.py:254
  108.6 19.0 %all_to_all.37 = bf16[128,4,128]{2,1,0:T(4,128)(2,1)S(1)} all-to-all(bf16[128,4,128]{2,1,0:T(4,128)(2,1)S(1)} %bitcast.23), channel_id=1, replica_groups=mesh['seq_0'=8,'seq_1'=8,'seq_2'=2,'rep'=4] {'seq_0','seq_1','seq_2'}, dimensions={0} | all-to-all | bytes 262144 | tf_op jit(solution)/shard_map/all_to_all | solution.py:268
  127.6 1.7 %prefix.3 = bf16[256,128]{1,0:T(8,128)(2,1)} custom-call(bf16[512,128]{1,0:T(8,128)(2,1)S(1)} %bitcast.19), custom_call_target="tpu_custom_call" | custom-call | tf_op jit(solution)/shard_map/prefix/pallas_call | solution.py:254
  129.3 5.9 %all-to-all-start.6 = ((bf16[128,2,128]{2,1,0:T(2,128)(2,1)}), bf16[128,2,128]{2,1,0:T(2,128)(2,1)S(1)}, u32[]{:S(2)}, u32[]{:S(2)}) async-start(bf16[128,2,128]{2,1,0:T(2,128)(2,1)} %bitcast.13), calls=%async_computation.6 | async-start | bytes 131072 | tf_op jit(solution)/shard_map/all_to_all | solution.py:268
  135.2 2.6 %inner.3 = (bf16[256,512]{1,0:T(8,128)(2,1)S(1)}, f32[256,512]{1,0:T(8,128)S(1)}, f32[256,8]{1,0:T(8,128)S(1)}) custom-call(bf16[256,512]{1,0:T(8,128)(2,1)S(1)} %get-tuple-element.30.refs_0_, bf16[512,1536]{1,0:T(8,128)(2,1)} %refs_1_.7, bf16[256,1024]{1,0:T(8,128)(2,1)S(1)} %get-tuple-element.31.refs_2_, f32[8,256]{1,0:T(8,128)S(1)} %get-tuple-element.32.refs_3_), custom_call_target="tpu_custom_call" | custom-call | tf_op jit(solution)/shard_map/inner/pallas_call | solution.py:254
  137.8 9.0 %all-to-all-done.6 = bf16[128,2,128]{2,1,0:T(2,128)(2,1)S(1)} async-done(((bf16[128,2,128]{2,1,0:T(2,128)(2,1)}), bf16[128,2,128]{2,1,0:T(2,128)(2,1)S(1)}, u32[]{:S(2)}, u32[]{:S(2)}) %all-to-all-start.6) | async-done | bytes 65568 | tf_op jit(solution)/shard_map/all_to_all | solution.py:268
  146.8 1.6 %last.1 = bf16[256,512]{1,0:T(8,128)(2,1)} custom-call(bf16[256,512]{1,0:T(8,128)(2,1)S(1)} %get-tuple-element.29.refs_0_, bf16[256,512]{1,0:T(8,128)(2,1)S(1)} %get-tuple-element.33.refs_1_, f32[256,512]{1,0:T(8,128)S(1)} %get-tuple-element.34.refs_2_, f32[256,8]{1,0:T(8,128)S(1)} %get-tuple-element.35.refs_3_, bf16[256,128]{1,0:T(8,128)(2,1)S(1)} %bitcast.21, ...), custom_call_target="tpu_custom_call" | custom-call | tf_op jit(solution)/shard_map/last/pallas_call | solution.py:254
  (29 shorter events, 2.0 us)
Async XLA Ops:
  8.0 52.8 %copy-start.10 = (s32[2048]{0:T(1024)S(1)}, s32[2048]{0:T(1024)}, u32[]{:S(2)}) copy-start(s32[2048]{0:T(1024)} %param.13) | copy-start | bytes 24580
  8.0 53.1 %copy-start.7 = (f32[8,128]{1,0:T(8,128)S(1)}, f32[8,128]{1,0:T(8,128)}, u32[]{:S(2)}) copy-start(f32[8,128]{1,0:T(8,128)} %refs_3_.2) | copy-start | bytes 12292
  8.0 17.2 %all-to-all-start = ((bf16[8,16,1024]{2,1,0:T(8,128)(2,1)}), bf16[8,16,1024]{2,1,0:T(8,128)(2,1)S(1)}, u32[]{:S(2)}, u32[]{:S(2)}) async-start(bf16[8,16,1024]{2,1,0:T(8,128)(2,1)} %broadcast_in_dim.5), calls=%async_computation | async-start | bytes 524288 | tf_op jit(solution)/shard_map/all_to_all | solution.py:285
  15.8 87.5 %all-gather.2.cloned.1.call-start = ((), (), s32[]{:S(2)}) async-start(), calls=%async_computation.7 | async-start | bytes 4456448 | tf_op jit(solution)/shard_map/all_gather | solution.py:304
  15.8 1.4 copy-start.1
  17.2 0.9 copy-start.4
  18.1 0.7 copy-start.6
  20.2 52.3 %copy-start.2 = (bf16[512,512]{1,0:T(8,128)(2,1)S(1)}, bf16[512,512]{1,0:T(8,128)(2,1)}, u32[]{:S(2)}) copy-start(bf16[512,512]{1,0:T(8,128)(2,1)} %refs_6_.1) | copy-start | bytes 1572868
  20.2 52.3 %copy-start.5 = (bf16[128,512]{1,0:T(8,128)(2,1)S(1)}, bf16[128,512]{1,0:T(8,128)(2,1)}, u32[]{:S(2)}) copy-start(bf16[128,512]{1,0:T(8,128)(2,1)} %refs_1_.6) | copy-start | bytes 393220
  25.2 0.7 copy-start.9
  55.0 17.5 %all-to-all-start.2 = ((bf16[128,2,128]{2,1,0:T(2,128)(2,1)}), bf16[128,2,128]{2,1,0:T(2,128)(2,1)S(1)}, u32[]{:S(2)}, u32[]{:S(2)}) async-start(bf16[128,2,128]{2,1,0:T(2,128)(2,1)} %bitcast.5), calls=%async_computation.2 | async-start | bytes 131072 | tf_op jit(solution)/shard_map/all_to_all | solution.py:268
  74.3 29.0 %copy-start = (bf16[512,1536]{1,0:T(8,128)(2,1)S(1)}, bf16[512,1536]{1,0:T(8,128)(2,1)}, u32[]{:S(2)}) copy-start(bf16[512,1536]{1,0:T(8,128)(2,1)} %refs_1_.7) | copy-start | bytes 4718596
  74.3 29.0 %copy-start.8 = (f32[8,256]{1,0:T(8,128)S(1)}, f32[8,256]{1,0:T(8,128)}, u32[]{:S(2)}) copy-start(f32[8,256]{1,0:T(8,128)} %refs_3_.3) | copy-start | bytes 24580
  74.3 21.7 %all-to-all-start.3 = ((bf16[64,8,512]{2,1,0:T(8,128)(2,1)}), bf16[64,8,512]{2,1,0:T(8,128)(2,1)S(1)}, u32[]{:S(2)}, u32[]{:S(2)}) async-start(bf16[64,8,512]{2,1,0:T(8,128)(2,1)} %bitcast.7), calls=%async_computation.3 | async-start | bytes 1048576 | tf_op jit(solution)/shard_map/all_to_all | solution.py:268
  108.6 38.3 %copy-start.3 = (bf16[512,512]{1,0:T(8,128)(2,1)S(1)}, bf16[512,512]{1,0:T(8,128)(2,1)}, u32[]{:S(2)}) copy-start(bf16[512,512]{1,0:T(8,128)(2,1)} %refs_5_.1) | copy-start | bytes 1572868
  129.3 17.5 %all-to-all-start.6 = ((bf16[128,2,128]{2,1,0:T(2,128)(2,1)}), bf16[128,2,128]{2,1,0:T(2,128)(2,1)S(1)}, u32[]{:S(2)}, u32[]{:S(2)}) async-start(bf16[128,2,128]{2,1,0:T(2,128)(2,1)} %bitcast.13), calls=%async_computation.6 | async-start | bytes 131072 | tf_op jit(solution)/shard_map/all_to_all | solution.py:268
Sparse Core Ops, SparseCore 0:
  26.1 49.7 all-gather.1

commit v4 on v3

--- a/solution.py
+++ b/solution.py
@@ -12,10 +12,11 @@
 PAIRS = HEADS // 2
 BR = 8
 CAP = 32
-SEQ = ("seq_0", "seq_1", "seq_2")
-CHIPS = ("seq_0", "seq_1")
-ROW = ("seq_1", "seq_2")
-REP_SEQ = ("rep", "seq_0", "seq_1", "seq_2")
+SEQ = ("seq_0", "seq_1", "seq_2", "seq_3")
+GROUPS = ("seq_0", "seq_1")
+INSIDE = ("seq_2", "seq_3")
+ROW = ("seq_1", "seq_2", "seq_3")
+REP_SEQ = ("rep",) + SEQ
 EPS = 1e-05
 F32 = jnp.float32
 BF16 = jnp.bfloat16
@@ -70,14 +71,19 @@
     )
 
 
-def pack_state(keys_values, by_row):
+def pack_state(keys_values, by_row, more=None):
     rows = keys_values.shape[0]
     total = by_row[rows - 1 : rows]
     weight = jnp.exp(total - by_row)
     lane = iota((HEAD_DIM, 128), 1)
-    place = iota((128, HEAD_DIM), 0)
-    spread = ones_where((place % 4 < 2) & (iota((128, HEAD_DIM), 1) == (place // 4) * 2 + place % 4))
-    kind = iota((128, 128), 0) % 4
+    each = 4 if more is None else 12
+    place, column = iota((32 * each, 128), 0), iota((32 * each, 128), 1)
+    device = place >> 2 if more is None else (place * 43691) >> 19
+    kind = place - each * device
+    spread = ones_where((kind < 2) & (column == 2 * device + kind))[:, :HEAD_DIM]
+    if more is not None:
+        chosen = (kind >= 4) & (column == (kind - 4) * 16 + (device & 15))
+        more = dot(ones_where(chosen), more)
     packed = []
     for p in range(PAIRS):
         keys = keys_values[:, 128 * p : 128 * (p + 1)].astype(F32) * pair_lanes(weight, p)
@@ -89,24 +95,36 @@
         piece = dot(spread, state)
         piece = jnp.where(kind == 2, high.astype(F32), piece)
         piece = jnp.where(kind == 3, low.astype(F32), piece)
+        if more is not None:
+            piece = jnp.where(kind >= 4, more, piece)
         packed.append(piece.astype(BF16))
     return jnp.concatenate(packed, axis=0)
 
 
-def front(points, weight, decay):
+def front(points, weight, decay, up, down):
     normed = rms_rows(points[...].astype(F32)).astype(BF16)
     keys_values = dot(normed, weight[:, D:]).astype(BF16)
     by_row = running_sums(decay[...])[1]
-    return normed, keys_values, pack_state(keys_values, by_row)
+    more = [part[:, 128 * k : 128 * (k + 1)] for part in (up, down) for k in range(4)]
+    more = jnp.concatenate(more, axis=0)
+    return normed, keys_values, pack_state(keys_values, by_row, more)
 
 
 def prefix(received):
-    rows = received[...]
-    devices = rows.shape[0] // 4
-    square = (devices, devices)
-    pick = iota((devices, 4 * devices), 1) - 4 * iota((devices, 4 * devices), 0)
-    states = [dot(ones_where(pick == j), rows).astype(BF16) for j in range(2)]
-    totals = [dot(ones_where(pick == 2 + j), rows) for j in range(2)]
+    each = received.shape[0] // 128
+    block = (16 * each, 16 * each)
+    kind, device = iota(block, 0) >> 4, iota(block, 0) & 15
+    sort = ones_where(iota(block, 1) == each * device + kind)
+    blocks = [
+        dot(sort, received[16 * each * g : 16 * each * (g + 1), :]).astype(BF16) for g in range(8)
+    ]
+
+    def rows_of(kind):
+        return jnp.concatenate([block[16 * kind : 16 * (kind + 1)] for block in blocks], axis=0)
+
+    states = [rows_of(j) for j in range(2)]
+    totals = [rows_of(2 + j).astype(F32) for j in range(2)]
+    square = (128, 128)
     earlier = iota(square, 1) < iota(square, 0)
     before = ones_where(earlier)
     later = iota(square, 0) > iota(square, 1)
@@ -122,11 +140,14 @@
         high, low = halves(jnp.where(earlier, jnp.exp(gap), 0.0))
         outs.append([dot(high, state) + dot(low, state) for state in states])
     lane = iota(square, 1) < HEAD_DIM
-    back = iota((2 * devices, devices), 0) - 2 * iota((2 * devices, devices), 1)
-    return sum(
+    back = iota((256, 128), 0) - 2 * iota((256, 128), 1)
+    summed = sum(
         dot(ones_where(back == j), jnp.where(lane, outs[0][j], outs[1][j]).astype(BF16))
         for j in range(2)
     ).astype(BF16)
+    if each == 4:
+        return summed
+    return summed, jnp.concatenate([rows_of(kind) for kind in range(4, each)], axis=1)
 
 
 def inner(normed, weight, keys_values, decay):
@@ -169,22 +190,22 @@
     return jnp.concatenate(outs, axis=1)
 
 
-def middle(chips, points, queries, summed, grown, entering, w_out):
+def middle(fours, points, queries, summed, grown, entering, w_out):
     mixed = dot(attended(queries, summed, grown, entering), w_out[...])
     first = (points[...].astype(F32) + mixed).astype(BF16)
-    shape = (512, 128)
+    shape = (256, 128)
     place, column = iota(shape, 0), iota(shape, 1)
-    chosen = (place // BR == chips[...]) & ((place & 7) == (column & 7))
+    chosen = (place // BR == fours[...]) & ((place & 7) == (column & 7))
     return dot(ones_where(chosen), first).astype(BF16)
 
 
 def across(meta, arrived):
-    shape = (256, 512)
+    shape = (256, 256)
     place, column = iota(shape, 0), iota(shape, 1)
-    begin = jnp.where(place < 128, meta[0], meta[1])
-    end = jnp.where(place < 128, meta[1], meta[2])
-    where = begin + ((meta[3] - begin) & 1) + 2 * ((place // BR) & 15)
-    held = (where & 127) >> 1
+    begin = sum(jnp.where(place // 64 == k, meta[k], 0) for k in range(4))
+    end = sum(jnp.where(place // 64 == k, meta[k + 1], 0) for k in range(4))
+    where = begin + ((meta[5] - begin) & 3) + 4 * ((place // BR) & 7)
+    held = (where & 127) >> 2
     chosen = (where < end) & (column == held * BR + (place & 7))
     return dot(ones_where(chosen), arrived[...]).astype(BF16)
 
@@ -201,10 +222,10 @@
             pieces[k].start()
     shape = (256, 256)
     place, column = iota(shape, 0), iota(shape, 1)
-    begin = jnp.where(meta[3] == 0, meta[0], meta[1])
-    used = jnp.where(meta[3] == 0, meta[1], meta[2]) - begin
+    begin = meta[meta[5]]
+    used = meta[meta[5] + 1] - begin
     slot = place // BR
-    held = ((begin + slot) & 1) * 16 + slot // 2
+    held = ((begin + slot) & 3) * 8 + slot // 4
     chosen = (slot < used) & (column == held * BR + (place & 7))
     kept = jnp.where(iota(decay.shape, 1) < BR * used, decay[...], 0.0)
     by_row = running_sums(kept)[1]
@@ -280,29 +301,31 @@
     w_qkv_two,
     w_out_two,
 ):
-    joined = jnp.concatenate([w_up.T, w_down], axis=1)
-    spread = jnp.broadcast_to(joined[None], (8, 16, 2 * D))
-    column = lax.all_to_all(spread, "seq_0", split_axis=0, concat_axis=0, tiled=True)
-    column = column.reshape(128, 2 * D)
     position = lax.axis_index(SEQ)
-    core = lax.axis_index("seq_2")
-    limits = CAP * (position - core + iota((3, 1), 0))
+    member = position & 3
+    limits = CAP * (position - member + iota((5, 1), 0))
     starts = jnp.sum((block_target[None, :] < limits).astype(jnp.int32), axis=1)
-    meta = jnp.concatenate([starts, jnp.stack([core]).astype(jnp.int32)])
+    meta = jnp.concatenate([starts, member[None].astype(jnp.int32)])
     own = lax.dynamic_slice_in_dim(block_target, position * 16, 16)
-    chips = jnp.repeat(own // (2 * CAP), BR)[None, :]
+    fours = jnp.repeat(own // (4 * CAP), BR)[None, :]
 
     normed, keys_values, sent = kernel_call(
         front,
-        [((128, D), BF16), ((128, 2 * D), BF16), ((512, 128), BF16)],
+        [((128, D), BF16), ((128, 2 * D), BF16), ((1536, 128), BF16)],
         points,
         w_qkv_one,
         decay_one,
-        loose=(0, 1, 2),
-    )
-    column, sent = lax.optimization_barrier((column, sent))
+        w_up.T,
+        w_down,
+        outside=(0, 1, 2, 3, 4),
+    )
+    received = lax.all_to_all(
+        sent.reshape(384, 4, 128), SEQ, split_axis=0, concat_axis=0, tiled=True
+    ).reshape(1536, 128)
+    summed, column = kernel_call(
+        prefix, [((256, 128), BF16), ((128, 2 * D), BF16)], received
+    )
     weights = lax.all_gather(column, ROW, axis=0, tiled=True)
-    received = whole(sent, SEQ, 128)
     own_rows = kernel_call(
         inner,
         [((128, D), BF16), ((128, D), F32), ((128, HEADS), F32)],
@@ -313,13 +336,13 @@
         loose=(0, 2, 3),
         outside=(1,),
     )
-    entering = whole(kernel_call(prefix, [((256, 128), BF16)], received), SEQ, 128)
+    entering = whole(summed, SEQ, 128)
     outgoing = kernel_call(
-        middle, [((512, D), BF16)], chips, points, *own_rows, entering, w_out_one
-    )
-    arrived = whole(outgoing, CHIPS, 64)
+        middle, [((256, D), BF16)], fours, points, *own_rows, entering, w_out_one
+    )
+    arrived = whole(outgoing, GROUPS, 32)
     outgoing = kernel_call(across, [((256, D), BF16)], meta, arrived, scalars=1)
-    arrived = whole(outgoing, "seq_2", 2)
+    arrived = whole(outgoing, INSIDE, 4)
     placed, normed, keys_values, decay, sent = kernel_call(
         second,
         [
@@ -359,7 +382,7 @@
 
 def solution(mesh):
     split = Mesh(
-        mesh.devices.reshape(8, 8, 2, mesh.shape["rep"]), ("seq_0", "seq_1", "seq_2", "rep")
+        mesh.devices.reshape(8, 4, 2, 2, mesh.shape["rep"]), SEQ + ("rep",)
     )
     placed = (
         P(REP_SEQ, None),

time: 156 us -> 148 us (0.949)
  blocking collectives: 52.8 us -> 66 us
  waiting for transfers between devices: 39.3 us -> 30.1 us
  starting transfers between devices: 24.3 us -> 16.8 us
  local copies, waits for them, and re-layouts: 4.62 us -> 0.2 us
    all_to_all x0 -> x1, blocking collectives: none -> 35 us  [shards(): lax.all_to_all(sent.reshape(384, 4, 128), SEQ, split_axis=0, concat_axis=...]
    all_to_all x3 -> x2, blocking collectives: 52.8 us -> 31.1 us  [whole(): lax.all_to_all(split, axes, split_axis=0, concat_axis=0, tiled=True)]
    all_to_all x1 -> x0, starting transfers between devices: 7.77 us -> none  [shards(): lax.all_to_all(spread, 'seq_0', split_axis=0, concat_axis=0, tiled=True)]
    all_to_all x1 -> x0, waiting for transfers between devices: 5 us -> none  [shards(): lax.all_to_all(spread, 'seq_0', split_axis=0, concat_axis=0, tiled=True)]
    all_to_all x3, waiting for transfers between devices: 34.3 us -> 30 us  [whole(): lax.all_to_all(split, axes, split_axis=0, concat_axis=0, tiled=True)]
    unnamed x22 -> x14, local copies, waits for them, and re-layouts: 3.73 us -> 0.03 us
  transfers between devices with their start and end apart: 5 -> 4, of which waited for: 4 -> 3; matrix products, arithmetic and copies ran while one was open for 0% -> 0% of each run, Pallas kernels for 7% -> 5%
where the time goes in v4:
time: 148 us
  blocking collectives  66 us (45%)
  waiting for transfers between devices  30.1 us (20%)
  Pallas kernels  20.6 us (14%)
  starting transfers between devices  16.8 us (11%)
  between operations  13.5 us (9%)
    all_to_all x1, blocking collectives, shards(): lax.all_to_all(sent.reshape(384, 4, 128), SEQ, split_axis=0, concat_axis=...  35 us
    all_to_all x2, blocking collectives, whole(): lax.all_to_all(split, axes, split_axis=0, concat_axis=0, tiled=True)  31.1 us
    all_to_all x3, waiting for transfers between devices, whole(): lax.all_to_all(split, axes, split_axis=0, concat_axis=0, tiled=True)  30 us
    pallas_call x9, Pallas kernels, kernel_call(): pl.pallas_call(body, compiler_params=pltpu.CompilerParams(vmem_limit_byte...  20.6 us
    all_to_all x3, starting transfers between devices, whole(): lax.all_to_all(split, axes, split_axis=0, concat_axis=0, tiled=True)  16.8 us
  transfers between devices with their start and end apart: 4, of which 3 were waited for; matrix products, arithmetic and copies ran while one was open for 0% of the time, Pallas kernels for 5%

profile of v4, /device:TPU:1, one launch (start us, length us, event | category | flops | bytes accessed | tf_op | source)
XLA Modules:
  0.0 147.6 jit_solution(11315516762636137094)
XLA Ops:
  6.5 2.7 %front.1 = (bf16[128,512]{1,0:T(8,128)(2,1)S(1)}, bf16[128,1024]{1,0:T(8,128)(2,1)S(1)}, bf16[1536,128]{1,0:T(8,128)(2,1)S(1)}) custom-call(bf16[128,512]{1,0:T(8,128)(2,1)} %refs_1_.6, bf16[512,1536]{1,0:T(8,128)(2,1)} %refs_1_.5, f32[8,128]{1,0:T(8,128)} %refs_3_.2, bf16[16,512]{1,0:T(8,128)(2,1)} %bitcast.23, bf16[16,512]{1,0:T(8,128)(2,1)} %refs_4_.1), custom_call_target="tpu_custom_call" | custom-call | tf_op jit(solution)/shard_map/front/pallas_call | solution.py:275
  9.2 35.0 %all_to_all.30 = bf16[384,4,128]{2,1,0:T(4,128)(2,1)S(1)} all-to-all(bf16[384,4,128]{2,1,0:T(4,128)(2,1)S(1)} %bitcast.19), channel_id=1, replica_groups=mesh['seq_0'=8,'seq_1'=4,'seq_2'=2,'seq_3'=2,'rep'=4] {'seq_0','seq_1','..., dimensions={0} | all-to-all | bytes 786432 | tf_op jit(solution)/shard_map/all_to_all | solution.py:322
  44.2 1.8 %prefix.2 = (bf16[256,128]{1,0:T(8,128)(2,1)}, bf16[128,1024]{1,0:T(8,128)(2,1)}) custom-call(bf16[1536,128]{1,0:T(8,128)(2,1)S(1)} %bitcast.14), custom_call_target="tpu_custom_call" | custom-call | tf_op jit(solution)/shard_map/prefix/pallas_call | solution.py:275
  46.0 0.0 all-gather.2.cloned.1.call-update
  46.0 7.1 %all-to-all-start.1 = ((bf16[128,2,128]{2,1,0:T(2,128)(2,1)}), bf16[128,2,128]{2,1,0:T(2,128)(2,1)S(1)}, u32[]{:S(2)}, u32[]{:S(2)}) async-start(bf16[128,2,128]{2,1,0:T(2,128)(2,1)} %bitcast.4), calls=%async_computation.1 | async-start | bytes 131072 | tf_op jit(solution)/shard_map/all_to_all | solution.py:289
  53.1 0.1 and_select_fusion
  53.2 0.1 broadcast_in_dim.8
  53.3 0.1 broadcast_in_dim_reshape.3.refs_0_
  53.4 2.9 %inner.2 = (bf16[128,512]{1,0:T(8,128)(2,1)S(1)}, f32[128,512]{1,0:T(8,128)S(1)}, f32[128,8]{1,0:T(8,128)S(1)}) custom-call(bf16[128,512]{1,0:T(8,128)(2,1)S(1)} %get-tuple-element.21.refs_0_, bf16[512,1536]{1,0:T(8,128)(2,1)} %refs_1_.5, bf16[128,1024]{1,0:T(8,128)(2,1)S(1)} %get-tuple-element.22.refs_2_, f32[8,128]{1,0:T(8,128)S(1)} %copy-done.4), custom_call_target="tpu_custom_call" | custom-call | tf_op jit(solution)/shard_map/inner/pallas_call | solution.py:275
  56.2 8.5 %all-to-all-done.1 = bf16[128,2,128]{2,1,0:T(2,128)(2,1)S(1)} async-done(((bf16[128,2,128]{2,1,0:T(2,128)(2,1)}), bf16[128,2,128]{2,1,0:T(2,128)(2,1)S(1)}, u32[]{:S(2)}, u32[]{:S(2)}) %all-to-all-start.1) | async-done | bytes 65568 | tf_op jit(solution)/shard_map/all_to_all | solution.py:289
  64.8 1.6 %middle.1 = bf16[256,512]{1,0:T(8,128)(2,1)} custom-call(s32[1,128]{1,0:T(1,128)S(1)} %broadcast_in_dim_reshape.3.refs_0_, bf16[128,512]{1,0:T(8,128)(2,1)S(1)} %copy-done.3, bf16[128,512]{1,0:T(8,128)(2,1)S(1)} %get-tuple-element.23.refs_2_, f32[128,512]{1,0:T(8,128)S(1)} %get-tuple-element.24.refs_3_, f32[128,8]{1,0:T(8,128)S(1)} %get-tuple-element.25.refs_4_, ...), custom_call_target="tpu_custom_call" | custom-call | tf_op jit(solution)/shard_map/middle/pallas_call | solution.py:275
  66.4 3.9 %all-to-all-start.2 = ((bf16[32,8,512]{2,1,0:T(8,128)(2,1)}), bf16[32,8,512]{2,1,0:T(8,128)(2,1)S(1)}, u32[]{:S(2)}, u32[]{:S(2)}) async-start(bf16[32,8,512]{2,1,0:T(8,128)(2,1)} %bitcast.6), calls=%async_computation.2 | async-start | bytes 524288 | tf_op jit(solution)/shard_map/all_to_all | solution.py:289
  70.3 0.2 convert_reduce_fusion
  70.5 0.1 pad_add_fusion.refs_0_
  70.5 12.5 %all-to-all-done.2 = bf16[32,8,512]{2,1,0:T(8,128)(2,1)S(1)} async-done(((bf16[32,8,512]{2,1,0:T(8,128)(2,1)}), bf16[32,8,512]{2,1,0:T(8,128)(2,1)S(1)}, u32[]{:S(2)}, u32[]{:S(2)}) %all-to-all-start.2) | async-done | bytes 262176 | tf_op jit(solution)/shard_map/all_to_all | solution.py:289
  83.0 0.8 across.1
  83.8 9.4 %all_to_all.31 = bf16[4,64,512]{2,1,0:T(8,128)(2,1)S(1)} all-to-all(bf16[4,64,512]{2,1,0:T(8,128)(2,1)S(1)} %bitcast.17), channel_id=1, replica_groups=mesh['seq_0'=8,'seq_1'=4,'seq_2'=2,'seq_3'=2,'rep'=4] {'seq_2','seq_3'}, dimensions={0} | all-to-all | bytes 524288 | tf_op jit(solution)/shard_map/all_to_all | solution.py:289
  93.2 5.3 %second.1 = (bf16[256,512]{1,0:T(8,128)(2,1)S(1)}, bf16[256,512]{1,0:T(8,128)(2,1)S(1)}, bf16[256,1024]{1,0:T(8,128)(2,1)S(1)}, f32[8,256]{1,0:T(8,128)S(1)}, bf16[512,128]{1,0:T(8,128)(2,1)S(1)}) custom-call(s32[6]{0:T(128)S(1)} %pad_add_fusion.refs_0_, bf16[256,512]{1,0:T(8,128)(2,1)S(1)} %bitcast.15, bf16[512,1536]{1,0:T(8,128)(2,1)S(1)} %copy-done, ...), custom_call_target="tpu_custom_call" | custom-call | tf_op jit(solution)/shard_map/second/pallas_call | solution.py:275
  98.5 21.7 %all_to_all.32 = bf16[128,4,128]{2,1,0:T(4,128)(2,1)S(1)} all-to-all(bf16[128,4,128]{2,1,0:T(4,128)(2,1)S(1)} %bitcast.22), channel_id=1, replica_groups=mesh['seq_0'=8,'seq_1'=4,'seq_2'=2,'seq_3'=2,'rep'=4] {'seq_0','seq_1','..., dimensions={0} | all-to-all | bytes 262144 | tf_op jit(solution)/shard_map/all_to_all | solution.py:289
  120.1 1.5 %prefix.3 = bf16[256,128]{1,0:T(8,128)(2,1)} custom-call(bf16[512,128]{1,0:T(8,128)(2,1)S(1)} %bitcast.18), custom_call_target="tpu_custom_call" | custom-call | tf_op jit(solution)/shard_map/prefix/pallas_call | solution.py:275
  121.7 5.9 %all-to-all-start.5 = ((bf16[128,2,128]{2,1,0:T(2,128)(2,1)}), bf16[128,2,128]{2,1,0:T(2,128)(2,1)S(1)}, u32[]{:S(2)}, u32[]{:S(2)}) async-start(bf16[128,2,128]{2,1,0:T(2,128)(2,1)} %bitcast.12), calls=%async_computation.5 | async-start | bytes 131072 | tf_op jit(solution)/shard_map/all_to_all | solution.py:289
  127.6 2.6 %inner.3 = (bf16[256,512]{1,0:T(8,128)(2,1)S(1)}, f32[256,512]{1,0:T(8,128)S(1)}, f32[256,8]{1,0:T(8,128)S(1)}) custom-call(bf16[256,512]{1,0:T(8,128)(2,1)S(1)} %get-tuple-element.30.refs_0_, bf16[512,1536]{1,0:T(8,128)(2,1)} %refs_1_.7, bf16[256,1024]{1,0:T(8,128)(2,1)S(1)} %get-tuple-element.31.refs_2_, f32[8,256]{1,0:T(8,128)S(1)} %get-tuple-element.32.refs_3_), custom_call_target="tpu_custom_call" | custom-call | tf_op jit(solution)/shard_map/inner/pallas_call | solution.py:275
  130.2 9.0 %all-to-all-done.5 = bf16[128,2,128]{2,1,0:T(2,128)(2,1)S(1)} async-done(((bf16[128,2,128]{2,1,0:T(2,128)(2,1)}), bf16[128,2,128]{2,1,0:T(2,128)(2,1)S(1)}, u32[]{:S(2)}, u32[]{:S(2)}) %all-to-all-start.5) | async-done | bytes 65568 | tf_op jit(solution)/shard_map/all_to_all | solution.py:289
  139.2 1.6 %last.1 = bf16[256,512]{1,0:T(8,128)(2,1)} custom-call(bf16[256,512]{1,0:T(8,128)(2,1)S(1)} %get-tuple-element.29.refs_0_, bf16[256,512]{1,0:T(8,128)(2,1)S(1)} %get-tuple-element.33.refs_1_, f32[256,512]{1,0:T(8,128)S(1)} %get-tuple-element.34.refs_2_, f32[256,8]{1,0:T(8,128)S(1)} %get-tuple-element.35.refs_3_, bf16[256,128]{1,0:T(8,128)(2,1)S(1)} %bitcast.20, ...), custom_call_target="tpu_custom_call" | custom-call | tf_op jit(solution)/shard_map/last/pallas_call | solution.py:275
  (17 shorter events, 0.0 us)
Async XLA Ops:
  6.5 86.6 %all-gather.2.cloned.1.call-start = ((), (), s32[]{:S(2)}) async-start(), calls=%async_computation.6 | async-start | bytes 4456448 | tf_op jit(solution)/shard_map/all_gather | solution.py:328
  6.5 46.6 %copy-start.6 = (s32[2048]{0:T(1024)S(1)}, s32[2048]{0:T(1024)}, u32[]{:S(2)}) copy-start(s32[2048]{0:T(1024)} %param.13) | copy-start | bytes 24580
  6.5 46.8 %copy-start.4 = (f32[8,128]{1,0:T(8,128)S(1)}, f32[8,128]{1,0:T(8,128)}, u32[]{:S(2)}) copy-start(f32[8,128]{1,0:T(8,128)} %refs_3_.2) | copy-start | bytes 12292
  44.2 20.6 %copy-start.1 = (bf16[512,512]{1,0:T(8,128)(2,1)S(1)}, bf16[512,512]{1,0:T(8,128)(2,1)}, u32[]{:S(2)}) copy-start(bf16[512,512]{1,0:T(8,128)(2,1)} %refs_6_.1) | copy-start | bytes 1572868
  44.2 20.6 %copy-start.3 = (bf16[128,512]{1,0:T(8,128)(2,1)S(1)}, bf16[128,512]{1,0:T(8,128)(2,1)}, u32[]{:S(2)}) copy-start(bf16[128,512]{1,0:T(8,128)(2,1)} %refs_1_.6) | copy-start | bytes 393220
  46.0 18.8 %all-to-all-start.1 = ((bf16[128,2,128]{2,1,0:T(2,128)(2,1)}), bf16[128,2,128]{2,1,0:T(2,128)(2,1)S(1)}, u32[]{:S(2)}, u32[]{:S(2)}) async-start(bf16[128,2,128]{2,1,0:T(2,128)(2,1)} %bitcast.4), calls=%async_computation.1 | async-start | bytes 131072 | tf_op jit(solution)/shard_map/all_to_all | solution.py:289
  56.2 37.0 %copy-start = (bf16[512,1536]{1,0:T(8,128)(2,1)S(1)}, bf16[512,1536]{1,0:T(8,128)(2,1)}, u32[]{:S(2)}) copy-start(bf16[512,1536]{1,0:T(8,128)(2,1)} %refs_1_.7) | copy-start | bytes 4718596
  56.2 37.0 %copy-start.5 = (f32[8,256]{1,0:T(8,128)S(1)}, f32[8,256]{1,0:T(8,128)}, u32[]{:S(2)}) copy-start(f32[8,256]{1,0:T(8,128)} %refs_3_.3) | copy-start | bytes 24580
  66.4 16.6 %all-to-all-start.2 = ((bf16[32,8,512]{2,1,0:T(8,128)(2,1)}), bf16[32,8,512]{2,1,0:T(8,128)(2,1)S(1)}, u32[]{:S(2)}, u32[]{:S(2)}) async-start(bf16[32,8,512]{2,1,0:T(8,128)(2,1)} %bitcast.6), calls=%async_computation.2 | async-start | bytes 524288 | tf_op jit(solution)/shard_map/all_to_all | solution.py:289
  98.5 40.7 %copy-start.2 = (bf16[512,512]{1,0:T(8,128)(2,1)S(1)}, bf16[512,512]{1,0:T(8,128)(2,1)}, u32[]{:S(2)}) copy-start(bf16[512,512]{1,0:T(8,128)(2,1)} %refs_5_.1) | copy-start | bytes 1572868
  121.7 17.5 %all-to-all-start.5 = ((bf16[128,2,128]{2,1,0:T(2,128)(2,1)}), bf16[128,2,128]{2,1,0:T(2,128)(2,1)S(1)}, u32[]{:S(2)}, u32[]{:S(2)}) async-start(bf16[128,2,128]{2,1,0:T(2,128)(2,1)} %bitcast.12), calls=%async_computation.5 | async-start | bytes 131072 | tf_op jit(solution)/shard_map/all_to_all | solution.py:289
Sparse Core Ops, SparseCore 0:
  46.1 43.9 all-gather.1

commit v5 on v4

--- a/solution.py
+++ b/solution.py
@@ -71,83 +71,113 @@
     )
 
 
-def pack_state(keys_values, by_row, more=None):
+def own_state(keys_values, by_row):
     rows = keys_values.shape[0]
-    total = by_row[rows - 1 : rows]
-    weight = jnp.exp(total - by_row)
+    weight = jnp.exp(by_row[rows - 1 : rows] - by_row)
     lane = iota((HEAD_DIM, 128), 1)
-    each = 4 if more is None else 12
-    place, column = iota((32 * each, 128), 0), iota((32 * each, 128), 1)
-    device = place >> 2 if more is None else (place * 43691) >> 19
-    kind = place - each * device
-    spread = ones_where((kind < 2) & (column == 2 * device + kind))[:, :HEAD_DIM]
-    if more is not None:
-        chosen = (kind >= 4) & (column == (kind - 4) * 16 + (device & 15))
-        more = dot(ones_where(chosen), more)
-    packed = []
+    states = []
     for p in range(PAIRS):
         keys = keys_values[:, 128 * p : 128 * (p + 1)].astype(F32) * pair_lanes(weight, p)
         values = keys_values[:, D + 128 * p : D + 128 * (p + 1)]
-        high, low = halves(keys)
-        both = dot(high, values, TN) + dot(low, values, TN)
-        state = jnp.where(lane < HEAD_DIM, both[:HEAD_DIM], both[HEAD_DIM:]).astype(BF16)
-        high, low = halves(pair_lanes(total, p))
-        piece = dot(spread, state)
+        both = dot(keys.astype(BF16), values, TN)
+        states.append(jnp.where(lane < HEAD_DIM, both[:HEAD_DIM], both[HEAD_DIM:]).astype(BF16))
+    return states
+
+
+def pack(states, totals, more):
+    place, column = iota((384, 128), 0), iota((384, 128), 1)
+    device = (place * 43691) >> 19
+    kind = place - 12 * device
+    spread = ones_where((kind < 2) & (column == 2 * device + kind))[:, :HEAD_DIM]
+    chosen = (kind >= 4) & (column == (kind - 4) * 16 + (device & 15))
+    more = dot(ones_where(chosen), more)
+    even = (iota((1, 128), 1) & 1) == 0
+    packed = []
+    for p in range(PAIRS):
+        total = jnp.where(even, pair_lanes(totals[0], p), pair_lanes(totals[1], p))
+        high, low = halves(total)
+        piece = dot(spread, states[p]) + more
         piece = jnp.where(kind == 2, high.astype(F32), piece)
         piece = jnp.where(kind == 3, low.astype(F32), piece)
-        if more is not None:
-            piece = jnp.where(kind >= 4, more, piece)
         packed.append(piece.astype(BF16))
     return jnp.concatenate(packed, axis=0)
 
 
-def front(points, weight, decay, up, down):
+def front(here, points, weight, decay, up, down, later, target):
     normed = rms_rows(points[...].astype(F32)).astype(BF16)
     keys_values = dot(normed, weight[:, D:]).astype(BF16)
     by_row = running_sums(decay[...])[1]
+    used = jnp.where((target[...] >> 5) == here[0], 1.0, 0.0)
+    used = jnp.sum(jnp.sum(used, axis=0, keepdims=True), axis=1, keepdims=True)
+    kept = jnp.where(iota(later.shape, 1).astype(F32) < BR * used, later[...], 0.0)
+    ones = ones_where(iota(later.shape, 0) >= 0)
+    second_total = sum(dot(ones, part, NT) for part in thirds(kept))[:1]
+    totals = (by_row[by_row.shape[0] - 1 :], second_total)
     more = [part[:, 128 * k : 128 * (k + 1)] for part in (up, down) for k in range(4)]
     more = jnp.concatenate(more, axis=0)
-    return normed, keys_values, pack_state(keys_values, by_row, more)
-
-
-def prefix(received):
-    each = received.shape[0] // 128
-    block = (16 * each, 16 * each)
+    return normed, keys_values, pack(own_state(keys_values, by_row), totals, more)
+
+
+def sort(received):
+    block = (192, 192)
     kind, device = iota(block, 0) >> 4, iota(block, 0) & 15
-    sort = ones_where(iota(block, 1) == each * device + kind)
-    blocks = [
-        dot(sort, received[16 * each * g : 16 * each * (g + 1), :]).astype(BF16) for g in range(8)
-    ]
+    order = ones_where(iota(block, 1) == 12 * device + kind)
+    blocks = [dot(order, received[192 * g : 192 * (g + 1), :]).astype(BF16) for g in range(8)]
 
     def rows_of(kind):
         return jnp.concatenate([block[16 * kind : 16 * (kind + 1)] for block in blocks], axis=0)
 
-    states = [rows_of(j) for j in range(2)]
-    totals = [rows_of(2 + j).astype(F32) for j in range(2)]
+    return (
+        jnp.concatenate([rows_of(kind) for kind in range(4)], axis=0),
+        jnp.concatenate([rows_of(kind) for kind in range(4, 12)], axis=1),
+    )
+
+
+def device_weights(heads, layer):
     square = (128, 128)
     earlier = iota(square, 1) < iota(square, 0)
+    later = iota(square, 0) > iota(square, 1)
     before = ones_where(earlier)
-    later = iota(square, 0) > iota(square, 1)
-    outs = []
+    before = jnp.concatenate([before, before], axis=1)
+    weights = []
     for half in range(2):
-        gap = sum(
-            dot(
-                before,
-                jnp.where(later, part[:, half * HEAD_DIM : half * HEAD_DIM + 1], 0.0).astype(BF16),
-            )
-            for part in totals
-        )
+        at = half * HEAD_DIM + layer
+        parts = [
+            jnp.where(later, heads[128 * k : 128 * (k + 1), at : at + 1].astype(F32), 0.0)
+            for k in (2, 3)
+        ]
+        gap = dot(before, jnp.concatenate(parts, axis=0).astype(BF16))
         high, low = halves(jnp.where(earlier, jnp.exp(gap), 0.0))
-        outs.append([dot(high, state) + dot(low, state) for state in states])
-    lane = iota(square, 1) < HEAD_DIM
-    back = iota((256, 128), 0) - 2 * iota((256, 128), 1)
-    summed = sum(
-        dot(ones_where(back == j), jnp.where(lane, outs[0][j], outs[1][j]).astype(BF16))
-        for j in range(2)
-    ).astype(BF16)
-    if each == 4:
-        return summed
-    return summed, jnp.concatenate([rows_of(kind) for kind in range(4, each)], axis=1)
+        weights.append(jnp.concatenate([high, low], axis=1))
+    return weights
+
+
+def gather_earlier(weights, states):
+    both = jnp.concatenate([states, states], axis=0)
+    outs = [dot(weight, both) for weight in weights]
+    lane = iota(outs[0].shape, 1) & 127
+    out = jnp.where(lane < HEAD_DIM, outs[0], outs[1]).astype(BF16)
+    out = jnp.concatenate([out[:, :128], out[:, 128:]], axis=0)
+    place, column = iota((256, 256), 0), iota((256, 256), 1)
+    back = ones_where(column == (place & 1) * 128 + (place >> 1))
+    return dot(back, out).astype(BF16)
+
+
+def prefix(heads):
+    states = jnp.concatenate([heads[:128, :], heads[128:256, :]], axis=1)
+    return gather_earlier(device_weights(heads, 0), states)
+
+
+def later_weights(heads):
+    return jnp.concatenate(device_weights(heads, 1), axis=0)
+
+
+def later_prefix(received, weights):
+    place, column = iota((256, 256), 0), iota((256, 256), 1)
+    order = ones_where(column == 2 * (place & 127) + (place >> 7))
+    rows = dot(order, received[...]).astype(BF16)
+    states = jnp.concatenate([rows[:128], rows[128:]], axis=1)
+    return gather_earlier([weights[:128, :], weights[128:, :]], states)
 
 
 def inner(normed, weight, keys_values, decay):
@@ -239,7 +269,8 @@
     placed = (first + dot(hidden, down[...])).astype(BF16)
     normed = rms_rows(placed.astype(F32)).astype(BF16)
     keys_values = dot(normed, w_qkv[:, D:]).astype(BF16)
-    return placed, normed, keys_values, kept, pack_state(keys_values, by_row)
+    state = jnp.concatenate(own_state(keys_values, by_row), axis=0)
+    return placed, normed, keys_values, kept, state
 
 
 def last(placed, queries, summed, grown, entering, w_out):
@@ -312,20 +343,24 @@
     normed, keys_values, sent = kernel_call(
         front,
         [((128, D), BF16), ((128, 2 * D), BF16), ((1536, 128), BF16)],
+        position[None].astype(jnp.int32),
         points,
         w_qkv_one,
         decay_one,
         w_up.T,
         w_down,
-        outside=(0, 1, 2, 3, 4),
+        decay_two,
+        block_target.reshape(16, 128),
+        scalars=1,
+        outside=(1, 2, 3, 4, 5, 6, 7),
     )
     received = lax.all_to_all(
         sent.reshape(384, 4, 128), SEQ, split_axis=0, concat_axis=0, tiled=True
     ).reshape(1536, 128)
-    summed, column = kernel_call(
-        prefix, [((256, 128), BF16), ((128, 2 * D), BF16)], received
-    )
+    heads, column = kernel_call(sort, [((512, 128), BF16), ((128, 2 * D), BF16)], received)
     weights = lax.all_gather(column, ROW, axis=0, tiled=True)
+    summed = kernel_call(prefix, [((256, 128), BF16)], heads)
+    device_weight = kernel_call(later_weights, [((256, 256), BF16)], heads)
     own_rows = kernel_call(
         inner,
         [((128, D), BF16), ((128, D), F32), ((128, HEADS), F32)],
@@ -350,7 +385,7 @@
             ((256, D), BF16),
             ((256, 2 * D), BF16),
             ((HEADS, 256), F32),
-            ((512, 128), BF16),
+            ((256, 128), BF16),
         ],
         meta,
         arrived,
@@ -376,7 +411,8 @@
         loose=(0, 2, 3),
         outside=(1,),
     )
-    entering = whole(kernel_call(prefix, [((256, 128), BF16)], received), SEQ, 128)
+    summed = kernel_call(later_prefix, [((256, 128), BF16)], received, device_weight)
+    entering = whole(summed, SEQ, 128)
     return kernel_call(last, [((256, D), BF16)], placed, *own_rows, entering, w_out_two)
 
 

time: 148 us -> 147 us (level)
  blocking collectives: 66 us -> 44.6 us
  waiting for transfers between devices: 30.1 us -> 41.1 us
  starting transfers between devices: 16.8 us -> 25.9 us
    all_to_all x2 -> x1, blocking collectives: 31.1 us -> 9.61 us  [whole(): lax.all_to_all(split, axes, split_axis=0, concat_axis=0, tiled=True)]
    all_to_all x3 -> x4, waiting for transfers between devices: 30 us -> 41 us  [whole(): lax.all_to_all(split, axes, split_axis=0, concat_axis=0, tiled=True)]
    all_to_all x3 -> x4, starting transfers between devices: 16.8 us -> 25.9 us  [whole(): lax.all_to_all(split, axes, split_axis=0, concat_axis=0, tiled=True)]
    pallas_call x9 -> x11, Pallas kernels: 20.6 us -> 21 us  [kernel_call(): pl.pallas_call(body, compiler_params=pltpu.CompilerParams(vmem_limit_byte...]
  transfers between devices with their start and end apart: 4 -> 5, of which waited for: 3 -> 4; matrix products, arithmetic and copies ran while one was open for 0% -> 0% of each run, Pallas kernels for 5% -> 6%
where the time goes in v5:
time: 147 us
  blocking collectives  44.6 us (30%)
  waiting for transfers between devices  41.1 us (28%)
  starting transfers between devices  25.9 us (18%)
  Pallas kernels  21 us (14%)
  between operations  13.5 us (9%)
    all_to_all x4, waiting for transfers between devices, whole(): lax.all_to_all(split, axes, split_axis=0, concat_axis=0, tiled=True)  41 us
    all_to_all x1, blocking collectives, shards(): lax.all_to_all(sent.reshape(384, 4, 128), SEQ, split_axis=0, concat_axis=...  35 us
    all_to_all x4, starting transfers between devices, whole(): lax.all_to_all(split, axes, split_axis=0, concat_axis=0, tiled=True)  25.9 us
    pallas_call x11, Pallas kernels, kernel_call(): pl.pallas_call(body, compiler_params=pltpu.CompilerParams(vmem_limit_byte...  21 us
    all_to_all x1, blocking collectives, whole(): lax.all_to_all(split, axes, split_axis=0, concat_axis=0, tiled=True)  9.61 us
  transfers between devices with their start and end apart: 5, of which 4 were waited for; matrix products, arithmetic and copies ran while one was open for 0% of the time, Pallas kernels for 6%

profile of v5, /device:TPU:1, one launch (start us, length us, event | category | flops | bytes accessed | tf_op | source)
XLA Modules:
  0.0 146.7 jit_solution(17979705253848338919)
XLA Ops:
  6.5 2.6 %front.1 = (bf16[128,512]{1,0:T(8,128)(2,1)S(1)}, bf16[128,1024]{1,0:T(8,128)(2,1)S(1)}, bf16[1536,128]{1,0:T(8,128)(2,1)S(1)}) custom-call(s32[1]{0:T(128)} %bitcast.1.refs_0_, bf16[128,512]{1,0:T(8,128)(2,1)} %refs_1_.6, bf16[512,1536]{1,0:T(8,128)(2,1)} %refs_1_.5, f32[8,128]{1,0:T(8,128)} %refs_3_.4, bf16[16,512]{1,0:T(8,128)(2,1)} %bitcast.25, ...), custom_call_target="tpu_custom_call" | custom-call | tf_op jit(solution)/shard_map/front/pallas_call | solution.py:306
  9.1 35.0 %all_to_all.30 = bf16[384,4,128]{2,1,0:T(4,128)(2,1)S(1)} all-to-all(bf16[384,4,128]{2,1,0:T(4,128)(2,1)S(1)} %bitcast.20), channel_id=1, replica_groups=mesh['seq_0'=8,'seq_1'=4,'seq_2'=2,'seq_3'=2,'rep'=4] {'seq_0','seq_1','..., dimensions={0} | all-to-all | bytes 786432 | tf_op jit(solution)/shard_map/all_to_all | solution.py:357
  44.1 1.1 sort.1
  45.2 1.2 prefix.1
  46.4 7.1 %all-to-all-start.1 = ((bf16[128,2,128]{2,1,0:T(2,128)(2,1)}), bf16[128,2,128]{2,1,0:T(2,128)(2,1)S(1)}, u32[]{:S(2)}, u32[]{:S(2)}) async-start(bf16[128,2,128]{2,1,0:T(2,128)(2,1)} %bitcast.6), calls=%async_computation.1 | async-start | bytes 131072 | tf_op jit(solution)/shard_map/all_to_all | solution.py:320
  53.6 0.1 and_select_fusion
  53.7 0.1 broadcast_in_dim_reshape.3.refs_0_
  53.8 2.8 %inner.2 = (bf16[128,512]{1,0:T(8,128)(2,1)S(1)}, f32[128,512]{1,0:T(8,128)S(1)}, f32[128,8]{1,0:T(8,128)S(1)}) custom-call(bf16[128,512]{1,0:T(8,128)(2,1)S(1)} %get-tuple-element.21.refs_0_, bf16[512,1536]{1,0:T(8,128)(2,1)} %refs_1_.5, bf16[128,1024]{1,0:T(8,128)(2,1)S(1)} %get-tuple-element.22.refs_2_, f32[8,128]{1,0:T(8,128)S(1)} %copy-done.5), custom_call_target="tpu_custom_call" | custom-call | tf_op jit(solution)/shard_map/inner/pallas_call | solution.py:306
  56.7 8.5 %all-to-all-done.1 = bf16[128,2,128]{2,1,0:T(2,128)(2,1)S(1)} async-done(((bf16[128,2,128]{2,1,0:T(2,128)(2,1)}), bf16[128,2,128]{2,1,0:T(2,128)(2,1)S(1)}, u32[]{:S(2)}, u32[]{:S(2)}) %all-to-all-start.1) | async-done | bytes 65568 | tf_op jit(solution)/shard_map/all_to_all | solution.py:320
  65.2 1.6 %middle.1 = bf16[256,512]{1,0:T(8,128)(2,1)} custom-call(s32[1,128]{1,0:T(1,128)S(1)} %broadcast_in_dim_reshape.3.refs_0_, bf16[128,512]{1,0:T(8,128)(2,1)S(1)} %copy-done.3, bf16[128,512]{1,0:T(8,128)(2,1)S(1)} %get-tuple-element.23.refs_2_, f32[128,512]{1,0:T(8,128)S(1)} %get-tuple-element.24.refs_3_, f32[128,8]{1,0:T(8,128)S(1)} %get-tuple-element.25.refs_4_, ...), custom_call_target="tpu_custom_call" | custom-call | tf_op jit(solution)/shard_map/middle/pallas_call | solution.py:306
  66.8 3.9 %all-to-all-start.2 = ((bf16[32,8,512]{2,1,0:T(8,128)(2,1)}), bf16[32,8,512]{2,1,0:T(8,128)(2,1)S(1)}, u32[]{:S(2)}, u32[]{:S(2)}) async-start(bf16[32,8,512]{2,1,0:T(8,128)(2,1)} %bitcast.8), calls=%async_computation.2 | async-start | bytes 524288 | tf_op jit(solution)/shard_map/all_to_all | solution.py:320
  70.7 0.2 convert_reduce_fusion
  71.0 12.3 %all-to-all-done.2 = bf16[32,8,512]{2,1,0:T(8,128)(2,1)S(1)} async-done(((bf16[32,8,512]{2,1,0:T(8,128)(2,1)}), bf16[32,8,512]{2,1,0:T(8,128)(2,1)S(1)}, u32[]{:S(2)}, u32[]{:S(2)}) %all-to-all-start.2) | async-done | bytes 262176 | tf_op jit(solution)/shard_map/all_to_all | solution.py:320
  83.3 0.8 across.1
  84.1 9.6 %all_to_all.31 = bf16[4,64,512]{2,1,0:T(8,128)(2,1)S(1)} all-to-all(bf16[4,64,512]{2,1,0:T(8,128)(2,1)S(1)} %bitcast.19), channel_id=1, replica_groups=mesh['seq_0'=8,'seq_1'=4,'seq_2'=2,'seq_3'=2,'rep'=4] {'seq_2','seq_3'}, dimensions={0} | all-to-all | bytes 524288 | tf_op jit(solution)/shard_map/all_to_all | solution.py:320
  93.7 5.3 %second.1 = (bf16[256,512]{1,0:T(8,128)(2,1)S(1)}, bf16[256,512]{1,0:T(8,128)(2,1)S(1)}, bf16[256,1024]{1,0:T(8,128)(2,1)S(1)}, f32[8,256]{1,0:T(8,128)S(1)}, bf16[256,128]{1,0:T(8,128)(2,1)}) custom-call(s32[6]{0:T(128)S(1)} %pad_add_fusion.refs_0_, bf16[256,512]{1,0:T(8,128)(2,1)S(1)} %bitcast.17, bf16[512,1536]{1,0:T(8,128)(2,1)S(1)} %copy-done, ...), custom_call_target="tpu_custom_call" | custom-call | tf_op jit(solution)/shard_map/second/pallas_call | solution.py:306
  99.0 9.2 %all-to-all-start.4 = ((bf16[128,2,128]{2,1,0:T(2,128)(2,1)}), bf16[128,2,128]{2,1,0:T(2,128)(2,1)S(1)}, u32[]{:S(2)}, u32[]{:S(2)}) async-start(bf16[128,2,128]{2,1,0:T(2,128)(2,1)} %bitcast.12), calls=%async_computation.4 | async-start | bytes 131072 | tf_op jit(solution)/shard_map/all_to_all | solution.py:320
  108.2 0.3 later_weights.1.refs_1_
  108.5 11.2 %all-to-all-done.4 = bf16[128,2,128]{2,1,0:T(2,128)(2,1)S(1)} async-done(((bf16[128,2,128]{2,1,0:T(2,128)(2,1)}), bf16[128,2,128]{2,1,0:T(2,128)(2,1)S(1)}, u32[]{:S(2)}, u32[]{:S(2)}) %all-to-all-start.4) | async-done | bytes 65568 | tf_op jit(solution)/shard_map/all_to_all | solution.py:320
  119.7 1.2 later_prefix.1
  120.9 5.7 %all-to-all-start.5 = ((bf16[128,2,128]{2,1,0:T(2,128)(2,1)}), bf16[128,2,128]{2,1,0:T(2,128)(2,1)S(1)}, u32[]{:S(2)}, u32[]{:S(2)}) async-start(bf16[128,2,128]{2,1,0:T(2,128)(2,1)} %bitcast.14), calls=%async_computation.5 | async-start | bytes 131072 | tf_op jit(solution)/shard_map/all_to_all | solution.py:320
  126.6 2.6 %inner.3 = (bf16[256,512]{1,0:T(8,128)(2,1)S(1)}, f32[256,512]{1,0:T(8,128)S(1)}, f32[256,8]{1,0:T(8,128)S(1)}) custom-call(bf16[256,512]{1,0:T(8,128)(2,1)S(1)} %get-tuple-element.30.refs_0_, bf16[512,1536]{1,0:T(8,128)(2,1)} %refs_1_.7, bf16[256,1024]{1,0:T(8,128)(2,1)S(1)} %get-tuple-element.31.refs_2_, f32[8,256]{1,0:T(8,128)S(1)} %get-tuple-element.32.refs_3_), custom_call_target="tpu_custom_call" | custom-call | tf_op jit(solution)/shard_map/inner/pallas_call | solution.py:306
  129.2 9.0 %all-to-all-done.5 = bf16[128,2,128]{2,1,0:T(2,128)(2,1)S(1)} async-done(((bf16[128,2,128]{2,1,0:T(2,128)(2,1)}), bf16[128,2,128]{2,1,0:T(2,128)(2,1)S(1)}, u32[]{:S(2)}, u32[]{:S(2)}) %all-to-all-start.5) | async-done | bytes 65568 | tf_op jit(solution)/shard_map/all_to_all | solution.py:320
  138.2 1.6 %last.1 = bf16[256,512]{1,0:T(8,128)(2,1)} custom-call(bf16[256,512]{1,0:T(8,128)(2,1)S(1)} %get-tuple-element.29.refs_0_, bf16[256,512]{1,0:T(8,128)(2,1)S(1)} %get-tuple-element.33.refs_1_, f32[256,512]{1,0:T(8,128)S(1)} %get-tuple-element.34.refs_2_, f32[256,8]{1,0:T(8,128)S(1)} %get-tuple-element.35.refs_3_, bf16[256,128]{1,0:T(8,128)(2,1)S(1)} %bitcast.21, ...), custom_call_target="tpu_custom_call" | custom-call | tf_op jit(solution)/shard_map/last/pallas_call | solution.py:306
  (20 shorter events, 0.2 us)
Async XLA Ops:
  6.5 87.2 %all-gather.2.cloned.1.call-start = ((), (), s32[]{:S(2)}) async-start(), calls=%async_computation.6 | async-start | bytes 4456448 | tf_op jit(solution)/shard_map/all_gather | solution.py:361
  6.5 47.0 %copy-start.6 = (s32[2048]{0:T(1024)S(1)}, s32[2048]{0:T(1024)}, u32[]{:S(2)}) copy-start(s32[2048]{0:T(1024)} %param.13) | copy-start | bytes 24580
  6.5 47.3 %copy-start.5 = (f32[8,128]{1,0:T(8,128)S(1)}, f32[8,128]{1,0:T(8,128)}, u32[]{:S(2)}) copy-start(f32[8,128]{1,0:T(8,128)} %refs_3_.4) | copy-start | bytes 12292
  44.1 21.1 %copy-start.1 = (bf16[512,512]{1,0:T(8,128)(2,1)S(1)}, bf16[512,512]{1,0:T(8,128)(2,1)}, u32[]{:S(2)}) copy-start(bf16[512,512]{1,0:T(8,128)(2,1)} %refs_6_.3) | copy-start | bytes 1572868
  44.1 21.1 %copy-start.3 = (bf16[128,512]{1,0:T(8,128)(2,1)S(1)}, bf16[128,512]{1,0:T(8,128)(2,1)}, u32[]{:S(2)}) copy-start(bf16[128,512]{1,0:T(8,128)(2,1)} %refs_1_.6) | copy-start | bytes 393220
  46.4 18.7 %all-to-all-start.1 = ((bf16[128,2,128]{2,1,0:T(2,128)(2,1)}), bf16[128,2,128]{2,1,0:T(2,128)(2,1)S(1)}, u32[]{:S(2)}, u32[]{:S(2)}) async-start(bf16[128,2,128]{2,1,0:T(2,128)(2,1)} %bitcast.6), calls=%async_computation.1 | async-start | bytes 131072 | tf_op jit(solution)/shard_map/all_to_all | solution.py:320
  56.7 37.0 %copy-start = (bf16[512,1536]{1,0:T(8,128)(2,1)S(1)}, bf16[512,1536]{1,0:T(8,128)(2,1)}, u32[]{:S(2)}) copy-start(bf16[512,1536]{1,0:T(8,128)(2,1)} %refs_1_.7) | copy-start | bytes 4718596
  56.7 37.0 %copy-start.4 = (f32[8,256]{1,0:T(8,128)S(1)}, f32[8,256]{1,0:T(8,128)}, u32[]{:S(2)}) copy-start(f32[8,256]{1,0:T(8,128)} %refs_3_.5) | copy-start | bytes 24580
  66.8 16.5 %all-to-all-start.2 = ((bf16[32,8,512]{2,1,0:T(8,128)(2,1)}), bf16[32,8,512]{2,1,0:T(8,128)(2,1)S(1)}, u32[]{:S(2)}, u32[]{:S(2)}) async-start(bf16[32,8,512]{2,1,0:T(8,128)(2,1)} %bitcast.8), calls=%async_computation.2 | async-start | bytes 524288 | tf_op jit(solution)/shard_map/all_to_all | solution.py:320
  99.0 39.2 %copy-start.2 = (bf16[512,512]{1,0:T(8,128)(2,1)S(1)}, bf16[512,512]{1,0:T(8,128)(2,1)}, u32[]{:S(2)}) copy-start(bf16[512,512]{1,0:T(8,128)(2,1)} %refs_5_.3) | copy-start | bytes 1572868
  99.0 20.7 %all-to-all-start.4 = ((bf16[128,2,128]{2,1,0:T(2,128)(2,1)}), bf16[128,2,128]{2,1,0:T(2,128)(2,1)S(1)}, u32[]{:S(2)}, u32[]{:S(2)}) async-start(bf16[128,2,128]{2,1,0:T(2,128)(2,1)} %bitcast.12), calls=%async_computation.4 | async-start | bytes 131072 | tf_op jit(solution)/shard_map/all_to_all | solution.py:320
  120.9 17.3 %all-to-all-start.5 = ((bf16[128,2,128]{2,1,0:T(2,128)(2,1)}), bf16[128,2,128]{2,1,0:T(2,128)(2,1)S(1)}, u32[]{:S(2)}, u32[]{:S(2)}) async-start(bf16[128,2,128]{2,1,0:T(2,128)(2,1)} %bitcast.14), calls=%async_computation.5 | async-start | bytes 131072 | tf_op jit(solution)/shard_map/all_to_all | solution.py:320
Sparse Core Ops, SparseCore 0:
  45.3 43.8 all-gather.1

commit v6 on v5

--- a/solution.py
+++ b/solution.py
@@ -1,3 +1,5 @@
+import math
+
 import jax
 import jax.numpy as jnp
 from jax import lax
@@ -18,6 +20,7 @@
 ROW = ("seq_1", "seq_2", "seq_3")
 REP_SEQ = ("rep",) + SEQ
 EPS = 1e-05
+GELU = (2.0 / math.pi) ** 0.5
 F32 = jnp.float32
 BF16 = jnp.bfloat16
 DIRECT = False
@@ -103,9 +106,11 @@
     return jnp.concatenate(packed, axis=0)
 
 
-def front(here, points, weight, decay, up, down, later, target):
+def front(here, points, weight, decay, up, down, later, target, buffer=None, copies=None):
+    if buffer is not None:
+        piece = pltpu.make_async_copy(weight.at[:, pl.ds(D, 2 * D)], buffer, copies.at[0])
+        piece.start()
     normed = rms_rows(points[...].astype(F32)).astype(BF16)
-    keys_values = dot(normed, weight[:, D:]).astype(BF16)
     by_row = running_sums(decay[...])[1]
     used = jnp.where((target[...] >> 5) == here[0], 1.0, 0.0)
     used = jnp.sum(jnp.sum(used, axis=0, keepdims=True), axis=1, keepdims=True)
@@ -115,6 +120,11 @@
     totals = (by_row[by_row.shape[0] - 1 :], second_total)
     more = [part[:, 128 * k : 128 * (k + 1)] for part in (up, down) for k in range(4)]
     more = jnp.concatenate(more, axis=0)
+    if buffer is None:
+        buffer = weight[:, D:]
+    else:
+        piece.wait()
+    keys_values = dot(normed, buffer[...]).astype(BF16)
     return normed, keys_values, pack(own_state(keys_values, by_row), totals, more)
 
 
@@ -201,10 +211,15 @@
             weighted = scores * jnp.exp(jnp.where(causal, gap, -1e30))
             both.append(dot(weighted.astype(BF16), values))
         summed.append(jnp.where(first, both[0], both[1]))
-    return queries, jnp.concatenate(summed, axis=1), jnp.exp(by_row)
-
-
-def attended(queries, summed, grown, entering):
+    grown = jnp.exp(by_row)
+    carrying = [
+        queries[:, 128 * p : 128 * (p + 1)].astype(F32) * pair_lanes(grown, p)
+        for p in range(PAIRS)
+    ]
+    return jnp.concatenate(carrying, axis=1).astype(BF16), jnp.concatenate(summed, axis=1)
+
+
+def attended(carrying, summed, entering):
     lanes = iota((1, 128), 1)
     sides = (ones_where(lanes < HEAD_DIM), ones_where(lanes >= HEAD_DIM))
     same = ones_where(iota((128, 128), 0) // HEAD_DIM == iota((128, 128), 1) // HEAD_DIM)
@@ -212,16 +227,15 @@
     for p in range(PAIRS):
         state = entering[HEAD_DIM * p : HEAD_DIM * (p + 1), :]
         state = jnp.concatenate([state * sides[0], state * sides[1]], axis=0)
-        carried = dot(queries[:, 128 * p : 128 * (p + 1)], state) * pair_lanes(grown[...], p)
-        number = summed[:, 128 * p : 128 * (p + 1)] + carried
-        high, low = halves(number * number)
-        mean = (dot(high, same) + dot(low, same)) * (1.0 / HEAD_DIM)
+        number = summed[:, 128 * p : 128 * (p + 1)]
+        number = number + dot(carrying[:, 128 * p : 128 * (p + 1)], state)
+        mean = dot((number * number).astype(BF16), same) * (1.0 / HEAD_DIM)
         outs.append((number * lax.rsqrt(mean + EPS)).astype(BF16))
     return jnp.concatenate(outs, axis=1)
 
 
-def middle(fours, points, queries, summed, grown, entering, w_out):
-    mixed = dot(attended(queries, summed, grown, entering), w_out[...])
+def middle(fours, points, carrying, summed, entering, w_out):
+    mixed = dot(attended(carrying, summed, entering), w_out[...])
     first = (points[...].astype(F32) + mixed).astype(BF16)
     shape = (256, 128)
     place, column = iota(shape, 0), iota(shape, 1)
@@ -263,18 +277,20 @@
     normed = rms_rows(first).astype(BF16)
     if pieces:
         pieces[0].wait()
-    hidden = jax.nn.gelu(dot(normed, up[...], NT), approximate=True).astype(BF16)
+    raw = dot(normed, up[...], NT)
+    bent = jnp.tanh(raw * (GELU + (GELU * 0.044715) * (raw * raw)))
+    hidden = (raw + raw * bent).astype(BF16)
     if pieces:
         pieces[1].wait()
-    placed = (first + dot(hidden, down[...])).astype(BF16)
+    placed = (first + 0.5 * dot(hidden, down[...])).astype(BF16)
     normed = rms_rows(placed.astype(F32)).astype(BF16)
     keys_values = dot(normed, w_qkv[:, D:]).astype(BF16)
     state = jnp.concatenate(own_state(keys_values, by_row), axis=0)
     return placed, normed, keys_values, kept, state
 
 
-def last(placed, queries, summed, grown, entering, w_out):
-    mixed = dot(attended(queries, summed, grown, entering), w_out[...])
+def last(placed, carrying, summed, entering, w_out):
+    mixed = dot(attended(carrying, summed, entering), w_out[...])
     return (placed[...].astype(F32) + mixed).astype(BF16)
 
 
@@ -352,7 +368,9 @@
         decay_two,
         block_target.reshape(16, 128),
         scalars=1,
-        outside=(1, 2, 3, 4, 5, 6, 7),
+        outside=(1, 3, 4, 5, 6, 7),
+        streamed=(2,),
+        scratch=(pltpu.VMEM((D, 2 * D), BF16), pltpu.SemaphoreType.DMA((1,))),
     )
     received = lax.all_to_all(
         sent.reshape(384, 4, 128), SEQ, split_axis=0, concat_axis=0, tiled=True
@@ -363,7 +381,7 @@
     device_weight = kernel_call(later_weights, [((256, 256), BF16)], heads)
     own_rows = kernel_call(
         inner,
-        [((128, D), BF16), ((128, D), F32), ((128, HEADS), F32)],
+        [((128, D), BF16), ((128, D), F32)],
         normed,
         w_qkv_one,
         keys_values,
@@ -403,7 +421,7 @@
     received = whole(sent, SEQ, 128)
     own_rows = kernel_call(
         inner,
-        [((256, D), BF16), ((256, D), F32), ((256, HEADS), F32)],
+        [((256, D), BF16), ((256, D), F32)],
         normed,
         w_qkv_two,
         keys_values,

time: 147 us -> 147 us (level)
  no operation moved by 1% of the time
where the time goes in v6:
time: 147 us; the launch traced here: 146 us
  blocking collectives  44.6 us (30%)
  waiting for transfers between devices  41 us (28%)
  starting transfers between devices  25.7 us (17%)
  Pallas kernels  20.8 us (14%)
  between operations  13.5 us (9%)
    all_to_all x4, waiting for transfers between devices, whole(): lax.all_to_all(split, axes, split_axis=0, concat_axis=0, tiled=True)  41 us
    all_to_all x1, blocking collectives, shards(): lax.all_to_all(sent.reshape(384, 4, 128), SEQ, split_axis=0, concat_axis=...  35 us
    all_to_all x4, starting transfers between devices, whole(): lax.all_to_all(split, axes, split_axis=0, concat_axis=0, tiled=True)  25.7 us
    pallas_call x11, Pallas kernels, kernel_call(): pl.pallas_call(body, compiler_params=pltpu.CompilerParams(vmem_limit_byte...  20.8 us
    all_to_all x1, blocking collectives, whole(): lax.all_to_all(split, axes, split_axis=0, concat_axis=0, tiled=True)  9.62 us
  transfers between devices with their start and end apart: 5, of which 4 were waited for; matrix products, arithmetic and copies ran while one was open for 0% of the time, Pallas kernels for 6%

profile of v6, /device:TPU:1, one launch (start us, length us, event | category | flops | bytes accessed | tf_op | source)
XLA Modules:
  0.0 146.2 jit_solution(5878207029733830918)
XLA Ops:
  6.5 3.0 %front.1 = (bf16[128,512]{1,0:T(8,128)(2,1)S(1)}, bf16[128,1024]{1,0:T(8,128)(2,1)S(1)}, bf16[1536,128]{1,0:T(8,128)(2,1)S(1)}) custom-call(s32[1]{0:T(128)} %bitcast.1.refs_0_, bf16[128,512]{1,0:T(8,128)(2,1)} %refs_1_.6, bf16[512,1536]{1,0:T(8,128)(2,1)} %refs_1_.5, f32[8,128]{1,0:T(8,128)} %refs_3_.4, bf16[16,512]{1,0:T(8,128)(2,1)} %bitcast.25, ...), custom_call_target="tpu_custom_call" | custom-call | tf_op jit(solution)/shard_map/front/pallas_call | solution.py:322
  9.5 35.0 %all_to_all.30 = bf16[384,4,128]{2,1,0:T(4,128)(2,1)S(1)} all-to-all(bf16[384,4,128]{2,1,0:T(4,128)(2,1)S(1)} %bitcast.20), channel_id=1, replica_groups=mesh['seq_0'=8,'seq_1'=4,'seq_2'=2,'seq_3'=2,'rep'=4] {'seq_0','seq_1','..., dimensions={0} | all-to-all | bytes 786432 | tf_op jit(solution)/shard_map/all_to_all | solution.py:375
  44.5 1.1 sort.1
  45.6 1.2 prefix.1
  46.8 7.1 %all-to-all-start.1 = ((bf16[128,2,128]{2,1,0:T(2,128)(2,1)}), bf16[128,2,128]{2,1,0:T(2,128)(2,1)S(1)}, u32[]{:S(2)}, u32[]{:S(2)}) async-start(bf16[128,2,128]{2,1,0:T(2,128)(2,1)} %bitcast.6), calls=%async_computation.1 | async-start | bytes 131072 | tf_op jit(solution)/shard_map/all_to_all | solution.py:336
  54.0 0.1 and_select_fusion
  54.1 0.1 broadcast_in_dim_reshape.3.refs_0_
  54.2 2.8 %inner.2 = (bf16[128,512]{1,0:T(8,128)(2,1)S(1)}, f32[128,512]{1,0:T(8,128)S(1)}) custom-call(bf16[128,512]{1,0:T(8,128)(2,1)S(1)} %get-tuple-element.19.refs_0_, bf16[512,1536]{1,0:T(8,128)(2,1)} %refs_1_.5, bf16[128,1024]{1,0:T(8,128)(2,1)S(1)} %get-tuple-element.20.refs_2_, f32[8,128]{1,0:T(8,128)S(1)} %copy-done.5), custom_call_target="tpu_custom_call" | custom-call | tf_op jit(solution)/shard_map/inner/pallas_call | solution.py:322
  57.1 8.5 %all-to-all-done.1 = bf16[128,2,128]{2,1,0:T(2,128)(2,1)S(1)} async-done(((bf16[128,2,128]{2,1,0:T(2,128)(2,1)}), bf16[128,2,128]{2,1,0:T(2,128)(2,1)S(1)}, u32[]{:S(2)}, u32[]{:S(2)}) %all-to-all-start.1) | async-done | bytes 65568 | tf_op jit(solution)/shard_map/all_to_all | solution.py:336
  65.6 1.4 middle.1
  67.0 3.9 %all-to-all-start.2 = ((bf16[32,8,512]{2,1,0:T(8,128)(2,1)}), bf16[32,8,512]{2,1,0:T(8,128)(2,1)S(1)}, u32[]{:S(2)}, u32[]{:S(2)}) async-start(bf16[32,8,512]{2,1,0:T(8,128)(2,1)} %bitcast.8), calls=%async_computation.2 | async-start | bytes 524288 | tf_op jit(solution)/shard_map/all_to_all | solution.py:336
  70.9 0.2 convert_reduce_fusion
  71.2 12.3 %all-to-all-done.2 = bf16[32,8,512]{2,1,0:T(8,128)(2,1)S(1)} async-done(((bf16[32,8,512]{2,1,0:T(8,128)(2,1)}), bf16[32,8,512]{2,1,0:T(8,128)(2,1)S(1)}, u32[]{:S(2)}, u32[]{:S(2)}) %all-to-all-start.2) | async-done | bytes 262176 | tf_op jit(solution)/shard_map/all_to_all | solution.py:336
  83.5 0.8 across.1
  84.3 9.6 %all_to_all.31 = bf16[4,64,512]{2,1,0:T(8,128)(2,1)S(1)} all-to-all(bf16[4,64,512]{2,1,0:T(8,128)(2,1)S(1)} %bitcast.19), channel_id=1, replica_groups=mesh['seq_0'=8,'seq_1'=4,'seq_2'=2,'seq_3'=2,'rep'=4] {'seq_2','seq_3'}, dimensions={0} | all-to-all | bytes 524288 | tf_op jit(solution)/shard_map/all_to_all | solution.py:336
  93.9 5.1 %second.1 = (bf16[256,512]{1,0:T(8,128)(2,1)S(1)}, bf16[256,512]{1,0:T(8,128)(2,1)S(1)}, bf16[256,1024]{1,0:T(8,128)(2,1)S(1)}, f32[8,256]{1,0:T(8,128)S(1)}, bf16[256,128]{1,0:T(8,128)(2,1)}) custom-call(s32[6]{0:T(128)S(1)} %pad_add_fusion.refs_0_, bf16[256,512]{1,0:T(8,128)(2,1)S(1)} %bitcast.17, bf16[512,1536]{1,0:T(8,128)(2,1)S(1)} %copy-done, ...), custom_call_target="tpu_custom_call" | custom-call | tf_op jit(solution)/shard_map/second/pallas_call | solution.py:322
  99.0 9.0 %all-to-all-start.4 = ((bf16[128,2,128]{2,1,0:T(2,128)(2,1)}), bf16[128,2,128]{2,1,0:T(2,128)(2,1)S(1)}, u32[]{:S(2)}, u32[]{:S(2)}) async-start(bf16[128,2,128]{2,1,0:T(2,128)(2,1)} %bitcast.12), calls=%async_computation.4 | async-start | bytes 131072 | tf_op jit(solution)/shard_map/all_to_all | solution.py:336
  108.1 0.3 later_weights.1.refs_1_
  108.3 11.2 %all-to-all-done.4 = bf16[128,2,128]{2,1,0:T(2,128)(2,1)S(1)} async-done(((bf16[128,2,128]{2,1,0:T(2,128)(2,1)}), bf16[128,2,128]{2,1,0:T(2,128)(2,1)S(1)}, u32[]{:S(2)}, u32[]{:S(2)}) %all-to-all-start.4) | async-done | bytes 65568 | tf_op jit(solution)/shard_map/all_to_all | solution.py:336
  119.5 1.2 later_prefix.1
  120.7 5.7 %all-to-all-start.5 = ((bf16[128,2,128]{2,1,0:T(2,128)(2,1)}), bf16[128,2,128]{2,1,0:T(2,128)(2,1)S(1)}, u32[]{:S(2)}, u32[]{:S(2)}) async-start(bf16[128,2,128]{2,1,0:T(2,128)(2,1)} %bitcast.14), calls=%async_computation.5 | async-start | bytes 131072 | tf_op jit(solution)/shard_map/all_to_all | solution.py:336
  126.4 2.6 %inner.3 = (bf16[256,512]{1,0:T(8,128)(2,1)S(1)}, f32[256,512]{1,0:T(8,128)S(1)}) custom-call(bf16[256,512]{1,0:T(8,128)(2,1)S(1)} %get-tuple-element.27.refs_0_, bf16[512,1536]{1,0:T(8,128)(2,1)} %refs_1_.7, bf16[256,1024]{1,0:T(8,128)(2,1)S(1)} %get-tuple-element.28.refs_2_, f32[8,256]{1,0:T(8,128)S(1)} %get-tuple-element.29.refs_3_), custom_call_target="tpu_custom_call" | custom-call | tf_op jit(solution)/shard_map/inner/pallas_call | solution.py:322
  129.0 9.0 %all-to-all-done.5 = bf16[128,2,128]{2,1,0:T(2,128)(2,1)S(1)} async-done(((bf16[128,2,128]{2,1,0:T(2,128)(2,1)}), bf16[128,2,128]{2,1,0:T(2,128)(2,1)S(1)}, u32[]{:S(2)}, u32[]{:S(2)}) %all-to-all-start.5) | async-done | bytes 65568 | tf_op jit(solution)/shard_map/all_to_all | solution.py:336
  138.1 1.3 last.1
  (20 shorter events, 0.2 us)
Async XLA Ops:
  6.5 87.4 %all-gather.2.cloned.1.call-start = ((), (), s32[]{:S(2)}) async-start(), calls=%async_computation.6 | async-start | bytes 4456448 | tf_op jit(solution)/shard_map/all_gather | solution.py:379
  6.5 47.4 %copy-start.6 = (s32[2048]{0:T(1024)S(1)}, s32[2048]{0:T(1024)}, u32[]{:S(2)}) copy-start(s32[2048]{0:T(1024)} %param.13) | copy-start | bytes 24580
  6.5 47.7 %copy-start.5 = (f32[8,128]{1,0:T(8,128)S(1)}, f32[8,128]{1,0:T(8,128)}, u32[]{:S(2)}) copy-start(f32[8,128]{1,0:T(8,128)} %refs_3_.4) | copy-start | bytes 12292
  44.5 21.1 %copy-start.1 = (bf16[512,512]{1,0:T(8,128)(2,1)S(1)}, bf16[512,512]{1,0:T(8,128)(2,1)}, u32[]{:S(2)}) copy-start(bf16[512,512]{1,0:T(8,128)(2,1)} %refs_5_.3) | copy-start | bytes 1572868
  44.5 21.1 %copy-start.3 = (bf16[128,512]{1,0:T(8,128)(2,1)S(1)}, bf16[128,512]{1,0:T(8,128)(2,1)}, u32[]{:S(2)}) copy-start(bf16[128,512]{1,0:T(8,128)(2,1)} %refs_1_.6) | copy-start | bytes 393220
  46.8 18.7 %all-to-all-start.1 = ((bf16[128,2,128]{2,1,0:T(2,128)(2,1)}), bf16[128,2,128]{2,1,0:T(2,128)(2,1)S(1)}, u32[]{:S(2)}, u32[]{:S(2)}) async-start(bf16[128,2,128]{2,1,0:T(2,128)(2,1)} %bitcast.6), calls=%async_computation.1 | async-start | bytes 131072 | tf_op jit(solution)/shard_map/all_to_all | solution.py:336
  57.1 36.8 %copy-start = (bf16[512,1536]{1,0:T(8,128)(2,1)S(1)}, bf16[512,1536]{1,0:T(8,128)(2,1)}, u32[]{:S(2)}) copy-start(bf16[512,1536]{1,0:T(8,128)(2,1)} %refs_1_.7) | copy-start | bytes 4718596
  57.1 36.8 %copy-start.4 = (f32[8,256]{1,0:T(8,128)S(1)}, f32[8,256]{1,0:T(8,128)}, u32[]{:S(2)}) copy-start(f32[8,256]{1,0:T(8,128)} %refs_3_.5) | copy-start | bytes 24580
  67.0 16.5 %all-to-all-start.2 = ((bf16[32,8,512]{2,1,0:T(8,128)(2,1)}), bf16[32,8,512]{2,1,0:T(8,128)(2,1)S(1)}, u32[]{:S(2)}, u32[]{:S(2)}) async-start(bf16[32,8,512]{2,1,0:T(8,128)(2,1)} %bitcast.8), calls=%async_computation.2 | async-start | bytes 524288 | tf_op jit(solution)/shard_map/all_to_all | solution.py:336
  99.0 39.0 %copy-start.2 = (bf16[512,512]{1,0:T(8,128)(2,1)S(1)}, bf16[512,512]{1,0:T(8,128)(2,1)}, u32[]{:S(2)}) copy-start(bf16[512,512]{1,0:T(8,128)(2,1)} %refs_4_.1) | copy-start | bytes 1572868
  99.0 20.5 %all-to-all-start.4 = ((bf16[128,2,128]{2,1,0:T(2,128)(2,1)}), bf16[128,2,128]{2,1,0:T(2,128)(2,1)S(1)}, u32[]{:S(2)}, u32[]{:S(2)}) async-start(bf16[128,2,128]{2,1,0:T(2,128)(2,1)} %bitcast.12), calls=%async_computation.4 | async-start | bytes 131072 | tf_op jit(solution)/shard_map/all_to_all | solution.py:336
  120.7 17.3 %all-to-all-start.5 = ((bf16[128,2,128]{2,1,0:T(2,128)(2,1)}), bf16[128,2,128]{2,1,0:T(2,128)(2,1)S(1)}, u32[]{:S(2)}, u32[]{:S(2)}) async-start(bf16[128,2,128]{2,1,0:T(2,128)(2,1)} %bitcast.14), calls=%async_computation.5 | async-start | bytes 131072 | tf_op jit(solution)/shard_map/all_to_all | solution.py:336
Sparse Core Ops, SparseCore 0:
  45.7 43.7 all-gather.1

commit v7 on v6

--- a/solution.py
+++ b/solution.py
@@ -106,11 +106,9 @@
     return jnp.concatenate(packed, axis=0)
 
 
-def front(here, points, weight, decay, up, down, later, target, buffer=None, copies=None):
-    if buffer is not None:
-        piece = pltpu.make_async_copy(weight.at[:, pl.ds(D, 2 * D)], buffer, copies.at[0])
-        piece.start()
+def front(here, points, weight, decay, up, down, later, target):
     normed = rms_rows(points[...].astype(F32)).astype(BF16)
+    keys_values = dot(normed, weight[:, D:]).astype(BF16)
     by_row = running_sums(decay[...])[1]
     used = jnp.where((target[...] >> 5) == here[0], 1.0, 0.0)
     used = jnp.sum(jnp.sum(used, axis=0, keepdims=True), axis=1, keepdims=True)
@@ -120,11 +118,6 @@
     totals = (by_row[by_row.shape[0] - 1 :], second_total)
     more = [part[:, 128 * k : 128 * (k + 1)] for part in (up, down) for k in range(4)]
     more = jnp.concatenate(more, axis=0)
-    if buffer is None:
-        buffer = weight[:, D:]
-    else:
-        piece.wait()
-    keys_values = dot(normed, buffer[...]).astype(BF16)
     return normed, keys_values, pack(own_state(keys_values, by_row), totals, more)
 
 
@@ -254,7 +247,20 @@
     return dot(ones_where(chosen), arrived[...]).astype(BF16)
 
 
-def second(meta, arrived, w_qkv, decay, weights, up=None, down=None, copies=None):
+def arrive(meta, arrived, decay):
+    shape = (256, 256)
+    place, column = iota(shape, 0), iota(shape, 1)
+    begin = meta[meta[5]]
+    used = meta[meta[5] + 1] - begin
+    slot = place // BR
+    held = ((begin + slot) & 3) * 8 + slot // 4
+    chosen = (slot < used) & (column == held * BR + (place & 7))
+    first = dot(ones_where(chosen), arrived[...])
+    kept = jnp.where(iota(decay.shape, 1) < BR * used, decay[...], 0.0)
+    return first.astype(BF16), rms_rows(first).astype(BF16), kept, running_sums(kept)[1]
+
+
+def second(first, normed, by_row, w_qkv, weights, up=None, down=None, copies=None):
     pieces = []
     if up is None:
         up, down = weights[:, :D], weights[:, D:]
@@ -264,29 +270,18 @@
                 pltpu.make_async_copy(weights.at[:, pl.ds(k * D, D)], buffer, copies.at[k])
             )
             pieces[k].start()
-    shape = (256, 256)
-    place, column = iota(shape, 0), iota(shape, 1)
-    begin = meta[meta[5]]
-    used = meta[meta[5] + 1] - begin
-    slot = place // BR
-    held = ((begin + slot) & 3) * 8 + slot // 4
-    chosen = (slot < used) & (column == held * BR + (place & 7))
-    kept = jnp.where(iota(decay.shape, 1) < BR * used, decay[...], 0.0)
-    by_row = running_sums(kept)[1]
-    first = dot(ones_where(chosen), arrived[...])
-    normed = rms_rows(first).astype(BF16)
     if pieces:
         pieces[0].wait()
-    raw = dot(normed, up[...], NT)
+    raw = dot(normed[...], up[...], NT)
     bent = jnp.tanh(raw * (GELU + (GELU * 0.044715) * (raw * raw)))
     hidden = (raw + raw * bent).astype(BF16)
     if pieces:
         pieces[1].wait()
-    placed = (first + 0.5 * dot(hidden, down[...])).astype(BF16)
+    placed = (first[...].astype(F32) + 0.5 * dot(hidden, down[...])).astype(BF16)
     normed = rms_rows(placed.astype(F32)).astype(BF16)
     keys_values = dot(normed, w_qkv[:, D:]).astype(BF16)
-    state = jnp.concatenate(own_state(keys_values, by_row), axis=0)
-    return placed, normed, keys_values, kept, state
+    state = jnp.concatenate(own_state(keys_values, by_row[...]), axis=0)
+    return placed, normed, keys_values, state
 
 
 def last(placed, carrying, summed, entering, w_out):
@@ -368,9 +363,7 @@
         decay_two,
         block_target.reshape(16, 128),
         scalars=1,
-        outside=(1, 3, 4, 5, 6, 7),
-        streamed=(2,),
-        scratch=(pltpu.VMEM((D, 2 * D), BF16), pltpu.SemaphoreType.DMA((1,))),
+        outside=(1, 2, 3, 4, 5, 6, 7),
     )
     received = lax.all_to_all(
         sent.reshape(384, 4, 128), SEQ, split_axis=0, concat_axis=0, tiled=True
@@ -396,21 +389,23 @@
     arrived = whole(outgoing, GROUPS, 32)
     outgoing = kernel_call(across, [((256, D), BF16)], meta, arrived, scalars=1)
     arrived = whole(outgoing, INSIDE, 4)
-    placed, normed, keys_values, decay, sent = kernel_call(
-        second,
-        [
-            ((256, D), BF16),
-            ((256, D), BF16),
-            ((256, 2 * D), BF16),
-            ((HEADS, 256), F32),
-            ((256, 128), BF16),
-        ],
+    first, normed, decay, by_row = kernel_call(
+        arrive,
+        [((256, D), BF16), ((256, D), BF16), ((HEADS, 256), F32), ((256, HEADS), F32)],
         meta,
         arrived,
+        decay_two,
+        scalars=1,
+    )
+    first, weights = lax.optimization_barrier((first, weights))
+    placed, normed, keys_values, sent = kernel_call(
+        second,
+        [((256, D), BF16), ((256, D), BF16), ((256, 2 * D), BF16), ((256, 128), BF16)],
+        first,
+        normed,
+        by_row,
         w_qkv_two,
-        decay_two,
         weights,
-        scalars=1,
         streamed=(4,),
         scratch=(
             pltpu.VMEM((4 * D, D), BF16),

time: 147 us -> 146 us (level)
    pallas_call x11 -> x12, Pallas kernels: 20.8 us -> 20.7 us  [kernel_call(): pl.pallas_call(body, compiler_params=pltpu.CompilerParams(vmem_limit_byte...]
  transfers between devices with their start and end apart: 5 -> 5, of which waited for: 4 -> 4; matrix products, arithmetic and copies ran while one was open for 0% -> 0% of each run, Pallas kernels for 6% -> 7%
where the time goes in v7:
time: 146 us; the launch traced here: 145 us
  blocking collectives  44.5 us (30%)
  waiting for transfers between devices  41.3 us (28%)
  starting transfers between devices  24.7 us (17%)
  Pallas kernels  20.7 us (14%)
  between operations  13.6 us (9%)
    all_to_all x4, waiting for transfers between devices, whole(): lax.all_to_all(split, axes, split_axis=0, concat_axis=0, tiled=True)  41.3 us
    all_to_all x1, blocking collectives, shards(): lax.all_to_all(sent.reshape(384, 4, 128), SEQ, split_axis=0, concat_axis=...  35 us
    all_to_all x4, starting transfers between devices, whole(): lax.all_to_all(split, axes, split_axis=0, concat_axis=0, tiled=True)  24.7 us
    pallas_call x12, Pallas kernels, kernel_call(): pl.pallas_call(body, compiler_params=pltpu.CompilerParams(vmem_limit_byte...  20.7 us
    all_to_all x1, blocking collectives, whole(): lax.all_to_all(split, axes, split_axis=0, concat_axis=0, tiled=True)  9.47 us
  transfers between devices with their start and end apart: 5, of which 4 were waited for; matrix products, arithmetic and copies ran while one was open for 0% of the time, Pallas kernels for 7%

profile of v7, /device:TPU:1, one launch (start us, length us, event | category | flops | bytes accessed | tf_op | source)
XLA Modules:
  0.0 145.3 jit_solution(3958373127573877631)
XLA Ops:
  6.5 2.6 %front.1 = (bf16[128,512]{1,0:T(8,128)(2,1)S(1)}, bf16[128,1024]{1,0:T(8,128)(2,1)S(1)}, bf16[1536,128]{1,0:T(8,128)(2,1)S(1)}) custom-call(s32[1]{0:T(128)} %bitcast.1.refs_0_, bf16[128,512]{1,0:T(8,128)(2,1)} %refs_1_.6, bf16[512,1536]{1,0:T(8,128)(2,1)} %refs_1_.5, f32[8,128]{1,0:T(8,128)} %refs_3_.4, bf16[16,512]{1,0:T(8,128)(2,1)} %bitcast.25, ...), custom_call_target="tpu_custom_call" | custom-call | tf_op jit(solution)/shard_map/front/pallas_call | solution.py:317
  9.1 35.0 %all_to_all.30 = bf16[384,4,128]{2,1,0:T(4,128)(2,1)S(1)} all-to-all(bf16[384,4,128]{2,1,0:T(4,128)(2,1)S(1)} %bitcast.20), channel_id=1, replica_groups=mesh['seq_0'=8,'seq_1'=4,'seq_2'=2,'seq_3'=2,'rep'=4] {'seq_0','seq_1','..., dimensions={0} | all-to-all | bytes 786432 | tf_op jit(solution)/shard_map/all_to_all | solution.py:368
  44.1 1.1 sort.1
  45.2 1.2 prefix.1
  46.4 7.1 %all-to-all-start.1 = ((bf16[128,2,128]{2,1,0:T(2,128)(2,1)}), bf16[128,2,128]{2,1,0:T(2,128)(2,1)S(1)}, u32[]{:S(2)}, u32[]{:S(2)}) async-start(bf16[128,2,128]{2,1,0:T(2,128)(2,1)} %bitcast.6), calls=%async_computation.1 | async-start | bytes 131072 | tf_op jit(solution)/shard_map/all_to_all | solution.py:331
  53.7 0.1 broadcast_in_dim_reshape.3.refs_0_
  53.8 2.8 %inner.2 = (bf16[128,512]{1,0:T(8,128)(2,1)S(1)}, f32[128,512]{1,0:T(8,128)S(1)}) custom-call(bf16[128,512]{1,0:T(8,128)(2,1)S(1)} %get-tuple-element.24.refs_0_, bf16[512,1536]{1,0:T(8,128)(2,1)} %refs_1_.5, bf16[128,1024]{1,0:T(8,128)(2,1)S(1)} %get-tuple-element.25.refs_2_, f32[8,128]{1,0:T(8,128)S(1)} %copy-done.5), custom_call_target="tpu_custom_call" | custom-call | tf_op jit(solution)/shard_map/inner/pallas_call | solution.py:317
  56.7 8.6 %all-to-all-done.1 = bf16[128,2,128]{2,1,0:T(2,128)(2,1)S(1)} async-done(((bf16[128,2,128]{2,1,0:T(2,128)(2,1)}), bf16[128,2,128]{2,1,0:T(2,128)(2,1)S(1)}, u32[]{:S(2)}, u32[]{:S(2)}) %all-to-all-start.1) | async-done | bytes 65568 | tf_op jit(solution)/shard_map/all_to_all | solution.py:331
  65.2 1.4 middle.1
  66.7 3.9 %all-to-all-start.2 = ((bf16[32,8,512]{2,1,0:T(8,128)(2,1)}), bf16[32,8,512]{2,1,0:T(8,128)(2,1)S(1)}, u32[]{:S(2)}, u32[]{:S(2)}) async-start(bf16[32,8,512]{2,1,0:T(8,128)(2,1)} %bitcast.8), calls=%async_computation.2 | async-start | bytes 524288 | tf_op jit(solution)/shard_map/all_to_all | solution.py:331
  70.6 0.2 convert_reduce_fusion
  70.8 12.5 %all-to-all-done.2 = bf16[32,8,512]{2,1,0:T(8,128)(2,1)S(1)} async-done(((bf16[32,8,512]{2,1,0:T(8,128)(2,1)}), bf16[32,8,512]{2,1,0:T(8,128)(2,1)S(1)}, u32[]{:S(2)}, u32[]{:S(2)}) %all-to-all-start.2) | async-done | bytes 262176 | tf_op jit(solution)/shard_map/all_to_all | solution.py:331
  83.3 0.8 across.1
  84.1 9.5 %all_to_all.31 = bf16[4,64,512]{2,1,0:T(8,128)(2,1)S(1)} all-to-all(bf16[4,64,512]{2,1,0:T(8,128)(2,1)S(1)} %bitcast.18), channel_id=1, replica_groups=mesh['seq_0'=8,'seq_1'=4,'seq_2'=2,'seq_3'=2,'rep'=4] {'seq_2','seq_3'}, dimensions={0} | all-to-all | bytes 524288 | tf_op jit(solution)/shard_map/all_to_all | solution.py:331
  93.6 0.9 arrive.1
  94.5 4.5 %second.1 = (bf16[256,512]{1,0:T(8,128)(2,1)S(1)}, bf16[256,512]{1,0:T(8,128)(2,1)S(1)}, bf16[256,1024]{1,0:T(8,128)(2,1)S(1)}, bf16[256,128]{1,0:T(8,128)(2,1)}) custom-call(bf16[256,512]{1,0:T(8,128)(2,1)S(1)} %get-tuple-element.32.refs_0_, bf16[256,512]{1,0:T(8,128)(2,1)S(1)} %get-tuple-element.33.refs_1_, f32[256,8]{1,0:T(8,128)S(1)} %get-tuple-element.34.refs_2_, ...), custom_call_target="tpu_custom_call" | custom-call | tf_op jit(solution)/shard_map/second/pallas_call | solution.py:317
  99.1 8.1 %all-to-all-start.4 = ((bf16[128,2,128]{2,1,0:T(2,128)(2,1)}), bf16[128,2,128]{2,1,0:T(2,128)(2,1)S(1)}, u32[]{:S(2)}, u32[]{:S(2)}) async-start(bf16[128,2,128]{2,1,0:T(2,128)(2,1)} %bitcast.12), calls=%async_computation.4 | async-start | bytes 131072 | tf_op jit(solution)/shard_map/all_to_all | solution.py:331
  107.2 0.3 later_weights.1.refs_1_
  107.5 11.2 %all-to-all-done.4 = bf16[128,2,128]{2,1,0:T(2,128)(2,1)S(1)} async-done(((bf16[128,2,128]{2,1,0:T(2,128)(2,1)}), bf16[128,2,128]{2,1,0:T(2,128)(2,1)S(1)}, u32[]{:S(2)}, u32[]{:S(2)}) %all-to-all-start.4) | async-done | bytes 65568 | tf_op jit(solution)/shard_map/all_to_all | solution.py:331
  118.6 1.2 later_prefix.1
  119.8 5.7 %all-to-all-start.5 = ((bf16[128,2,128]{2,1,0:T(2,128)(2,1)}), bf16[128,2,128]{2,1,0:T(2,128)(2,1)S(1)}, u32[]{:S(2)}, u32[]{:S(2)}) async-start(bf16[128,2,128]{2,1,0:T(2,128)(2,1)} %bitcast.14), calls=%async_computation.5 | async-start | bytes 131072 | tf_op jit(solution)/shard_map/all_to_all | solution.py:331
  125.5 2.6 %inner.3 = (bf16[256,512]{1,0:T(8,128)(2,1)S(1)}, f32[256,512]{1,0:T(8,128)S(1)}) custom-call(bf16[256,512]{1,0:T(8,128)(2,1)S(1)} %get-tuple-element.37.refs_0_, bf16[512,1536]{1,0:T(8,128)(2,1)} %refs_1_.7, bf16[256,1024]{1,0:T(8,128)(2,1)S(1)} %get-tuple-element.38.refs_2_, f32[8,256]{1,0:T(8,128)S(1)} %get-tuple-element.39.refs_3_), custom_call_target="tpu_custom_call" | custom-call | tf_op jit(solution)/shard_map/inner/pallas_call | solution.py:317
  128.2 9.0 %all-to-all-done.5 = bf16[128,2,128]{2,1,0:T(2,128)(2,1)S(1)} async-done(((bf16[128,2,128]{2,1,0:T(2,128)(2,1)}), bf16[128,2,128]{2,1,0:T(2,128)(2,1)S(1)}, u32[]{:S(2)}, u32[]{:S(2)}) %all-to-all-start.5) | async-done | bytes 65568 | tf_op jit(solution)/shard_map/all_to_all | solution.py:331
  137.2 1.3 last.1
  (21 shorter events, 0.3 us)
Async XLA Ops:
  6.5 88.0 %all-gather.2.cloned.1.call-start = ((), (), s32[]{:S(2)}) async-start(), calls=%async_computation.6 | async-start | bytes 4456448 | tf_op jit(solution)/shard_map/all_gather | solution.py:372
  6.5 47.0 %copy-start.6 = (s32[2048]{0:T(1024)S(1)}, s32[2048]{0:T(1024)}, u32[]{:S(2)}) copy-start(s32[2048]{0:T(1024)} %param.13) | copy-start | bytes 24580
  6.5 47.3 %copy-start.5 = (f32[8,128]{1,0:T(8,128)S(1)}, f32[8,128]{1,0:T(8,128)}, u32[]{:S(2)}) copy-start(f32[8,128]{1,0:T(8,128)} %refs_3_.4) | copy-start | bytes 12292
  44.1 21.1 %copy-start.1 = (bf16[512,512]{1,0:T(8,128)(2,1)S(1)}, bf16[512,512]{1,0:T(8,128)(2,1)}, u32[]{:S(2)}) copy-start(bf16[512,512]{1,0:T(8,128)(2,1)} %refs_5_.3) | copy-start | bytes 1572868
  44.1 21.1 %copy-start.3 = (bf16[128,512]{1,0:T(8,128)(2,1)S(1)}, bf16[128,512]{1,0:T(8,128)(2,1)}, u32[]{:S(2)}) copy-start(bf16[128,512]{1,0:T(8,128)(2,1)} %refs_1_.6) | copy-start | bytes 393220
  46.4 18.8 %all-to-all-start.1 = ((bf16[128,2,128]{2,1,0:T(2,128)(2,1)}), bf16[128,2,128]{2,1,0:T(2,128)(2,1)S(1)}, u32[]{:S(2)}, u32[]{:S(2)}) async-start(bf16[128,2,128]{2,1,0:T(2,128)(2,1)} %bitcast.6), calls=%async_computation.1 | async-start | bytes 131072 | tf_op jit(solution)/shard_map/all_to_all | solution.py:331
  56.7 36.9 %copy-start.4 = (f32[8,256]{1,0:T(8,128)S(1)}, f32[8,256]{1,0:T(8,128)}, u32[]{:S(2)}) copy-start(f32[8,256]{1,0:T(8,128)} %refs_2_.3) | copy-start | bytes 24580
  65.2 29.3 %copy-start = (bf16[512,1536]{1,0:T(8,128)(2,1)S(1)}, bf16[512,1536]{1,0:T(8,128)(2,1)}, u32[]{:S(2)}) copy-start(bf16[512,1536]{1,0:T(8,128)(2,1)} %refs_1_.7) | copy-start | bytes 4718596
  66.7 16.6 %all-to-all-start.2 = ((bf16[32,8,512]{2,1,0:T(8,128)(2,1)}), bf16[32,8,512]{2,1,0:T(8,128)(2,1)S(1)}, u32[]{:S(2)}, u32[]{:S(2)}) async-start(bf16[32,8,512]{2,1,0:T(8,128)(2,1)} %bitcast.8), calls=%async_computation.2 | async-start | bytes 524288 | tf_op jit(solution)/shard_map/all_to_all | solution.py:331
  99.1 38.1 %copy-start.2 = (bf16[512,512]{1,0:T(8,128)(2,1)S(1)}, bf16[512,512]{1,0:T(8,128)(2,1)}, u32[]{:S(2)}) copy-start(bf16[512,512]{1,0:T(8,128)(2,1)} %refs_4_.1) | copy-start | bytes 1572868
  99.1 19.5 %all-to-all-start.4 = ((bf16[128,2,128]{2,1,0:T(2,128)(2,1)}), bf16[128,2,128]{2,1,0:T(2,128)(2,1)S(1)}, u32[]{:S(2)}, u32[]{:S(2)}) async-start(bf16[128,2,128]{2,1,0:T(2,128)(2,1)} %bitcast.12), calls=%async_computation.4 | async-start | bytes 131072 | tf_op jit(solution)/shard_map/all_to_all | solution.py:331
  119.8 17.3 %all-to-all-start.5 = ((bf16[128,2,128]{2,1,0:T(2,128)(2,1)}), bf16[128,2,128]{2,1,0:T(2,128)(2,1)S(1)}, u32[]{:S(2)}, u32[]{:S(2)}) async-start(bf16[128,2,128]{2,1,0:T(2,128)(2,1)} %bitcast.14), calls=%async_computation.5 | async-start | bytes 131072 | tf_op jit(solution)/shard_map/all_to_all | solution.py:331
Sparse Core Ops, SparseCore 0:
  45.3 43.8 all-gather.1

commit v8 on v7

--- a/solution.py
+++ b/solution.py
@@ -272,9 +272,9 @@
             pieces[k].start()
     if pieces:
         pieces[0].wait()
-    raw = dot(normed[...], up[...], NT)
+    raw = dot(normed[...], up[...], NT).astype(BF16)
     bent = jnp.tanh(raw * (GELU + (GELU * 0.044715) * (raw * raw)))
-    hidden = (raw + raw * bent).astype(BF16)
+    hidden = raw + raw * bent
     if pieces:
         pieces[1].wait()
     placed = (first[...].astype(F32) + 0.5 * dot(hidden, down[...])).astype(BF16)

time: 146 us -> 146 us (level)
  no operation moved by 1% of the time
where the time goes in v8:
time: 146 us; the launch traced here: 145 us
  blocking collectives  44.5 us (30%)
  waiting for transfers between devices  41.3 us (28%)
  starting transfers between devices  24.7 us (17%)
  Pallas kernels  20.7 us (14%)
  between operations  13.6 us (9%)
    all_to_all x4, waiting for transfers between devices, whole(): lax.all_to_all(split, axes, split_axis=0, concat_axis=0, tiled=True)  41.3 us
    all_to_all x1, blocking collectives, shards(): lax.all_to_all(sent.reshape(384, 4, 128), SEQ, split_axis=0, concat_axis=...  35 us
    all_to_all x4, starting transfers between devices, whole(): lax.all_to_all(split, axes, split_axis=0, concat_axis=0, tiled=True)  24.7 us
    pallas_call x12, Pallas kernels, kernel_call(): pl.pallas_call(body, compiler_params=pltpu.CompilerParams(vmem_limit_byte...  20.7 us
    all_to_all x1, blocking collectives, whole(): lax.all_to_all(split, axes, split_axis=0, concat_axis=0, tiled=True)  9.47 us
  transfers between devices with their start and end apart: 5, of which 4 were waited for; matrix products, arithmetic and copies ran while one was open for 0% of the time, Pallas kernels for 7%

profile of v8, /device:TPU:1, one launch (start us, length us, event | category | flops | bytes accessed | tf_op | source)
XLA Modules:
  0.0 145.3 jit_solution(17401366361423344398)
XLA Ops:
  6.5 2.6 %front.1 = (bf16[128,512]{1,0:T(8,128)(2,1)S(1)}, bf16[128,1024]{1,0:T(8,128)(2,1)S(1)}, bf16[1536,128]{1,0:T(8,128)(2,1)S(1)}) custom-call(s32[1]{0:T(128)} %bitcast.1.refs_0_, bf16[128,512]{1,0:T(8,128)(2,1)} %refs_1_.6, bf16[512,1536]{1,0:T(8,128)(2,1)} %refs_1_.5, f32[8,128]{1,0:T(8,128)} %refs_3_.4, bf16[16,512]{1,0:T(8,128)(2,1)} %bitcast.25, ...), custom_call_target="tpu_custom_call" | custom-call | tf_op jit(solution)/shard_map/front/pallas_call | solution.py:317
  9.1 35.0 %all_to_all.30 = bf16[384,4,128]{2,1,0:T(4,128)(2,1)S(1)} all-to-all(bf16[384,4,128]{2,1,0:T(4,128)(2,1)S(1)} %bitcast.20), channel_id=1, replica_groups=mesh['seq_0'=8,'seq_1'=4,'seq_2'=2,'seq_3'=2,'rep'=4] {'seq_0','seq_1','..., dimensions={0} | all-to-all | bytes 786432 | tf_op jit(solution)/shard_map/all_to_all | solution.py:368
  44.1 1.1 sort.1
  45.2 1.2 prefix.1
  46.4 7.1 %all-to-all-start.1 = ((bf16[128,2,128]{2,1,0:T(2,128)(2,1)}), bf16[128,2,128]{2,1,0:T(2,128)(2,1)S(1)}, u32[]{:S(2)}, u32[]{:S(2)}) async-start(bf16[128,2,128]{2,1,0:T(2,128)(2,1)} %bitcast.6), calls=%async_computation.1 | async-start | bytes 131072 | tf_op jit(solution)/shard_map/all_to_all | solution.py:331
  53.7 0.1 broadcast_in_dim_reshape.3.refs_0_
  53.8 2.8 %inner.2 = (bf16[128,512]{1,0:T(8,128)(2,1)S(1)}, f32[128,512]{1,0:T(8,128)S(1)}) custom-call(bf16[128,512]{1,0:T(8,128)(2,1)S(1)} %get-tuple-element.24.refs_0_, bf16[512,1536]{1,0:T(8,128)(2,1)} %refs_1_.5, bf16[128,1024]{1,0:T(8,128)(2,1)S(1)} %get-tuple-element.25.refs_2_, f32[8,128]{1,0:T(8,128)S(1)} %copy-done.5), custom_call_target="tpu_custom_call" | custom-call | tf_op jit(solution)/shard_map/inner/pallas_call | solution.py:317
  56.7 8.6 %all-to-all-done.1 = bf16[128,2,128]{2,1,0:T(2,128)(2,1)S(1)} async-done(((bf16[128,2,128]{2,1,0:T(2,128)(2,1)}), bf16[128,2,128]{2,1,0:T(2,128)(2,1)S(1)}, u32[]{:S(2)}, u32[]{:S(2)}) %all-to-all-start.1) | async-done | bytes 65568 | tf_op jit(solution)/shard_map/all_to_all | solution.py:331
  65.2 1.4 middle.1
  66.7 3.9 %all-to-all-start.2 = ((bf16[32,8,512]{2,1,0:T(8,128)(2,1)}), bf16[32,8,512]{2,1,0:T(8,128)(2,1)S(1)}, u32[]{:S(2)}, u32[]{:S(2)}) async-start(bf16[32,8,512]{2,1,0:T(8,128)(2,1)} %bitcast.8), calls=%async_computation.2 | async-start | bytes 524288 | tf_op jit(solution)/shard_map/all_to_all | solution.py:331
  70.6 0.2 convert_reduce_fusion
  70.8 12.5 %all-to-all-done.2 = bf16[32,8,512]{2,1,0:T(8,128)(2,1)S(1)} async-done(((bf16[32,8,512]{2,1,0:T(8,128)(2,1)}), bf16[32,8,512]{2,1,0:T(8,128)(2,1)S(1)}, u32[]{:S(2)}, u32[]{:S(2)}) %all-to-all-start.2) | async-done | bytes 262176 | tf_op jit(solution)/shard_map/all_to_all | solution.py:331
  83.3 0.8 across.1
  84.1 9.5 %all_to_all.31 = bf16[4,64,512]{2,1,0:T(8,128)(2,1)S(1)} all-to-all(bf16[4,64,512]{2,1,0:T(8,128)(2,1)S(1)} %bitcast.18), channel_id=1, replica_groups=mesh['seq_0'=8,'seq_1'=4,'seq_2'=2,'seq_3'=2,'rep'=4] {'seq_2','seq_3'}, dimensions={0} | all-to-all | bytes 524288 | tf_op jit(solution)/shard_map/all_to_all | solution.py:331
  93.6 0.9 arrive.1
  94.5 4.5 %second.1 = (bf16[256,512]{1,0:T(8,128)(2,1)S(1)}, bf16[256,512]{1,0:T(8,128)(2,1)S(1)}, bf16[256,1024]{1,0:T(8,128)(2,1)S(1)}, bf16[256,128]{1,0:T(8,128)(2,1)}) custom-call(bf16[256,512]{1,0:T(8,128)(2,1)S(1)} %get-tuple-element.32.refs_0_, bf16[256,512]{1,0:T(8,128)(2,1)S(1)} %get-tuple-element.33.refs_1_, f32[256,8]{1,0:T(8,128)S(1)} %get-tuple-element.34.refs_2_, ...), custom_call_target="tpu_custom_call" | custom-call | tf_op jit(solution)/shard_map/second/pallas_call | solution.py:317
  99.1 8.1 %all-to-all-start.4 = ((bf16[128,2,128]{2,1,0:T(2,128)(2,1)}), bf16[128,2,128]{2,1,0:T(2,128)(2,1)S(1)}, u32[]{:S(2)}, u32[]{:S(2)}) async-start(bf16[128,2,128]{2,1,0:T(2,128)(2,1)} %bitcast.12), calls=%async_computation.4 | async-start | bytes 131072 | tf_op jit(solution)/shard_map/all_to_all | solution.py:331
  107.1 0.3 later_weights.1.refs_1_
  107.4 11.2 %all-to-all-done.4 = bf16[128,2,128]{2,1,0:T(2,128)(2,1)S(1)} async-done(((bf16[128,2,128]{2,1,0:T(2,128)(2,1)}), bf16[128,2,128]{2,1,0:T(2,128)(2,1)S(1)}, u32[]{:S(2)}, u32[]{:S(2)}) %all-to-all-start.4) | async-done | bytes 65568 | tf_op jit(solution)/shard_map/all_to_all | solution.py:331
  118.6 1.2 later_prefix.1
  119.8 5.7 %all-to-all-start.5 = ((bf16[128,2,128]{2,1,0:T(2,128)(2,1)}), bf16[128,2,128]{2,1,0:T(2,128)(2,1)S(1)}, u32[]{:S(2)}, u32[]{:S(2)}) async-start(bf16[128,2,128]{2,1,0:T(2,128)(2,1)} %bitcast.14), calls=%async_computation.5 | async-start | bytes 131072 | tf_op jit(solution)/shard_map/all_to_all | solution.py:331
  125.5 2.6 %inner.3 = (bf16[256,512]{1,0:T(8,128)(2,1)S(1)}, f32[256,512]{1,0:T(8,128)S(1)}) custom-call(bf16[256,512]{1,0:T(8,128)(2,1)S(1)} %get-tuple-element.37.refs_0_, bf16[512,1536]{1,0:T(8,128)(2,1)} %refs_1_.7, bf16[256,1024]{1,0:T(8,128)(2,1)S(1)} %get-tuple-element.38.refs_2_, f32[8,256]{1,0:T(8,128)S(1)} %get-tuple-element.39.refs_3_), custom_call_target="tpu_custom_call" | custom-call | tf_op jit(solution)/shard_map/inner/pallas_call | solution.py:317
  128.1 9.0 %all-to-all-done.5 = bf16[128,2,128]{2,1,0:T(2,128)(2,1)S(1)} async-done(((bf16[128,2,128]{2,1,0:T(2,128)(2,1)}), bf16[128,2,128]{2,1,0:T(2,128)(2,1)S(1)}, u32[]{:S(2)}, u32[]{:S(2)}) %all-to-all-start.5) | async-done | bytes 65568 | tf_op jit(solution)/shard_map/all_to_all | solution.py:331
  137.1 1.3 last.1
  (21 shorter events, 0.3 us)
Async XLA Ops:
  6.5 88.0 %all-gather.2.cloned.1.call-start = ((), (), s32[]{:S(2)}) async-start(), calls=%async_computation.6 | async-start | bytes 4456448 | tf_op jit(solution)/shard_map/all_gather | solution.py:372
  6.5 47.0 %copy-start.6 = (s32[2048]{0:T(1024)S(1)}, s32[2048]{0:T(1024)}, u32[]{:S(2)}) copy-start(s32[2048]{0:T(1024)} %param.13) | copy-start | bytes 24580
  6.5 47.3 %copy-start.5 = (f32[8,128]{1,0:T(8,128)S(1)}, f32[8,128]{1,0:T(8,128)}, u32[]{:S(2)}) copy-start(f32[8,128]{1,0:T(8,128)} %refs_3_.4) | copy-start | bytes 12292
  44.1 21.1 %copy-start.1 = (bf16[512,512]{1,0:T(8,128)(2,1)S(1)}, bf16[512,512]{1,0:T(8,128)(2,1)}, u32[]{:S(2)}) copy-start(bf16[512,512]{1,0:T(8,128)(2,1)} %refs_5_.3) | copy-start | bytes 1572868
  44.1 21.1 %copy-start.3 = (bf16[128,512]{1,0:T(8,128)(2,1)S(1)}, bf16[128,512]{1,0:T(8,128)(2,1)}, u32[]{:S(2)}) copy-start(bf16[128,512]{1,0:T(8,128)(2,1)} %refs_1_.6) | copy-start | bytes 393220
  46.4 18.8 %all-to-all-start.1 = ((bf16[128,2,128]{2,1,0:T(2,128)(2,1)}), bf16[128,2,128]{2,1,0:T(2,128)(2,1)S(1)}, u32[]{:S(2)}, u32[]{:S(2)}) async-start(bf16[128,2,128]{2,1,0:T(2,128)(2,1)} %bitcast.6), calls=%async_computation.1 | async-start | bytes 131072 | tf_op jit(solution)/shard_map/all_to_all | solution.py:331
  56.7 36.9 %copy-start.4 = (f32[8,256]{1,0:T(8,128)S(1)}, f32[8,256]{1,0:T(8,128)}, u32[]{:S(2)}) copy-start(f32[8,256]{1,0:T(8,128)} %refs_2_.3) | copy-start | bytes 24580
  65.2 29.3 %copy-start = (bf16[512,1536]{1,0:T(8,128)(2,1)S(1)}, bf16[512,1536]{1,0:T(8,128)(2,1)}, u32[]{:S(2)}) copy-start(bf16[512,1536]{1,0:T(8,128)(2,1)} %refs_1_.7) | copy-start | bytes 4718596
  66.7 16.6 %all-to-all-start.2 = ((bf16[32,8,512]{2,1,0:T(8,128)(2,1)}), bf16[32,8,512]{2,1,0:T(8,128)(2,1)S(1)}, u32[]{:S(2)}, u32[]{:S(2)}) async-start(bf16[32,8,512]{2,1,0:T(8,128)(2,1)} %bitcast.8), calls=%async_computation.2 | async-start | bytes 524288 | tf_op jit(solution)/shard_map/all_to_all | solution.py:331
  99.1 38.1 %copy-start.2 = (bf16[512,512]{1,0:T(8,128)(2,1)S(1)}, bf16[512,512]{1,0:T(8,128)(2,1)}, u32[]{:S(2)}) copy-start(bf16[512,512]{1,0:T(8,128)(2,1)} %refs_4_.1) | copy-start | bytes 1572868
  99.1 19.5 %all-to-all-start.4 = ((bf16[128,2,128]{2,1,0:T(2,128)(2,1)}), bf16[128,2,128]{2,1,0:T(2,128)(2,1)S(1)}, u32[]{:S(2)}, u32[]{:S(2)}) async-start(bf16[128,2,128]{2,1,0:T(2,128)(2,1)} %bitcast.12), calls=%async_computation.4 | async-start | bytes 131072 | tf_op jit(solution)/shard_map/all_to_all | solution.py:331
  119.8 17.3 %all-to-all-start.5 = ((bf16[128,2,128]{2,1,0:T(2,128)(2,1)}), bf16[128,2,128]{2,1,0:T(2,128)(2,1)S(1)}, u32[]{:S(2)}, u32[]{:S(2)}) async-start(bf16[128,2,128]{2,1,0:T(2,128)(2,1)} %bitcast.14), calls=%async_computation.5 | async-start | bytes 131072 | tf_op jit(solution)/shard_map/all_to_all | solution.py:331
Sparse Core Ops, SparseCore 0:
  45.3 43.8 all-gather.1
